TPU v7x, 32 devices: a whole 2x2x4 slice. The times are simulated.
32 devices in a mesh: seq: 4 (over y, x), shard: 8 (over z, core).
Axes of the slice: x: 2, y: 2, z: 4, core: 2. Of those that a mesh axis runs over, the one named last changes fastest.
Arguments:
- tokens: bfloat16 [8, 1024, 2048], P('shard', 'seq'), may hold values from -6 to 6
- w_query: bfloat16 [2048, 2048], P('shard'), may hold values from -0.125 to 0.125
- w_key: bfloat16 [2048, 256], P('shard'), may hold values from -0.125 to 0.125
- w_value: bfloat16 [2048, 256], P('shard'), may hold values from -0.125 to 0.125
- w_out: bfloat16 [2048, 2048], P('shard'), may hold values from -1 to 1
- w_gate: bfloat16 [2048, 5632], P('shard'), may hold values from -0.125 to 0.125
- w_up: bfloat16 [2048, 5632], P('shard'), may hold values from -0.125 to 0.125
- w_down: bfloat16 [5632, 2048], P('shard'), may hold values from -0.078125 to 0.078125
- gain_attn: bfloat16 [2048], P('shard'), may hold values from 0.5 to 1.5
- gain_mlp: bfloat16 [2048], P('shard'), may hold values from 0.5 to 1.5
- cotangent: bfloat16 [8, 1024, 2048], P('shard', 'seq'), may hold values from -6 to 6
Outputs:
- output: bfloat16 [8, 1024, 2048], P('shard', 'seq')
- grad_tokens: float32 [8, 1024, 2048], P('shard', 'seq')
- grad_query: float32 [2048, 2048], P('shard')
- grad_key: float32 [2048, 256], P('shard')
- grad_value: float32 [2048, 256], P('shard')
- grad_out: float32 [2048, 2048], P('shard')
- grad_gate: float32 [2048, 5632], P('shard')
- grad_up: float32 [2048, 5632], P('shard')
- grad_down: float32 [5632, 2048], P('shard')
- grad_gain_attn: float32 [2048], P('shard')
- grad_gain_mlp: float32 [2048], P('shard')
All inputs are finite; a program needn't handle non-finite values.
Results may differ from a plain program's by a relative error of at most 0.022.
Values may be sent and summed in bfloat16 or wider, within the bound.
No kernel may reach another device: no remote copies, remote signals or barrier semaphores. Data moves between devices by JAX's collectives and lax.ppermute only.
A program may use at most 384 MiB of HBM per device.

v0:
```python
import math

import jax
import jax.numpy as jnp
from jax import lax
from jax.sharding import PartitionSpec as P

HEADS = 32
KV_HEADS = 4
HEAD_DIM = 64


EPSILON = 1e-05
THETA = 10000.0


def rms_norm(values):
    return values * lax.rsqrt(jnp.mean(values * values, axis=-1, keepdims=True) + EPSILON)


def scaled_norm(values, gain_vec):
    return rms_norm(values) * gain_vec


def norm_back(values, gain_vec, cotangent):
    outcome, pullback = jax.vjp(scaled_norm, values, gain_vec)
    return pullback(cotangent)


def rope_angles(positions):
    half_dim = HEAD_DIM // 2
    frequency = jnp.exp(
        -math.log(THETA) * jnp.arange(half_dim).astype(jnp.float32) * 2.0 / HEAD_DIM
    )
    angles = positions[:, None] * frequency[None, :]
    return (jnp.cos(angles), jnp.sin(angles))


def rotate(head_array, cosine, sine_table):
    half_dim = head_array.shape[-1] // 2
    former = head_array[..., :half_dim]
    latter = head_array[..., half_dim:]
    cos_part = cosine[:, None, :]
    sin_part = sine_table[:, None, :]
    return jnp.concatenate(
        [former * cos_part - latter * sin_part, latter * cos_part + former * sin_part], axis=-1
    )


def on_device(
    tokens, w_query, w_key, w_value, w_out, w_gate, w_up, w_down, gain_attn, gain_mlp, cotangent
):
    seq_count = lax.axis_size("seq")
    seq_place = lax.axis_index("seq")
    inputs = tokens[0].astype(jnp.float32)
    row_count = inputs.shape[0]
    length = row_count * seq_count
    local_heads = HEADS // seq_count
    local_kv = max(1, KV_HEADS // seq_count)
    copies = seq_count * local_kv // KV_HEADS
    spread = local_heads // local_kv
    width_q = local_heads * HEAD_DIM
    width_kv = local_kv * HEAD_DIM
    score_scale = 1.0 / math.sqrt(HEAD_DIM)
    block_rows = min(512, length)
    blocks = length // block_rows
    f32 = jnp.float32
    bf16 = jnp.bfloat16
    attn_set = (
        lax.all_gather(w_query, "shard", axis=0, tiled=True),
        lax.all_gather(w_key, "shard", axis=0, tiled=True),
        lax.all_gather(w_value, "shard", axis=0, tiled=True),
        lax.all_gather(w_out, "shard", axis=0, tiled=True),
        lax.all_gather(gain_attn, "shard", axis=0, tiled=True),
    )
    full_query, full_key, full_value, full_out, full_gain_a = attn_set
    gain_first = full_gain_a.astype(f32)
    normed = scaled_norm(inputs, gain_first).astype(bf16)
    positions = (seq_place * row_count + jnp.arange(row_count)).astype(f32)
    cosine, sine_table = rope_angles(positions)
    query_lin = jnp.dot(normed, full_query, preferred_element_type=f32).reshape(
        row_count, HEADS, HEAD_DIM
    )
    key_lin = jnp.dot(normed, full_key, preferred_element_type=f32).reshape(
        row_count, KV_HEADS, HEAD_DIM
    )
    value_lin = jnp.dot(normed, full_value, preferred_element_type=f32).reshape(
        row_count, KV_HEADS, HEAD_DIM
    )
    queries = rotate(query_lin, cosine, sine_table).astype(bf16)
    key_heads = rotate(key_lin, cosine, sine_table).astype(bf16)
    value_heads = value_lin.astype(bf16)
    key_copies = jnp.repeat(key_heads, copies, axis=1)
    value_copies = jnp.repeat(value_heads, copies, axis=1)
    query_send = queries.reshape(row_count, seq_count, width_q)
    pair_send = jnp.concatenate([key_copies, value_copies], axis=-1)
    query_group, pair_group = (
        lax.all_to_all(query_send, "seq", split_axis=1, concat_axis=0, tiled=True),
        lax.all_to_all(pair_send, "seq", split_axis=1, concat_axis=0, tiled=True),
    )
    key_group = pair_group[:, 0, :width_kv].reshape(length, local_kv, HEAD_DIM)
    value_group = pair_group[:, 0, width_kv:].reshape(length, local_kv, HEAD_DIM)
    query_blocks = query_group.reshape(blocks, block_rows, local_kv, spread, HEAD_DIM)
    starts = jnp.arange(blocks) * block_rows
    columns = jnp.arange(length)

    def masked_scores(query_block, start_row):
        scores = (
            jnp.einsum("qkgd,ckd->kgqc", query_block, key_group, preferred_element_type=f32)
            * score_scale
        )
        places = start_row + jnp.arange(block_rows)
        allowed = places[:, None] >= columns[None, :]
        return jnp.where(allowed, scores, -1e30)

    def forward_block(couple):
        query_block, start_row = couple
        scores = masked_scores(query_block, start_row)
        highest = jnp.max(scores, axis=-1, keepdims=True)
        exponent = jnp.exp(scores - highest)
        denominator = jnp.sum(exponent, axis=-1, keepdims=True)
        probs_low = (exponent / denominator).astype(bf16)
        result = jnp.einsum(
            "kgqc,ckd->qkgd", probs_low, value_group, preferred_element_type=f32
        ).astype(bf16)
        return (result, (highest + jnp.log(denominator))[..., 0])

    attended_blocks, logsum_blocks = lax.map(forward_block, (query_blocks, starts))
    attended_group = attended_blocks.reshape(length, 1, width_q)
    attended = lax.all_to_all(
        attended_group, "seq", split_axis=0, concat_axis=1, tiled=True
    ).reshape(row_count, HEADS * HEAD_DIM)
    middle = inputs + jnp.dot(attended, full_out, preferred_element_type=f32)
    mlp_set = (
        lax.all_gather(w_gate, "shard", axis=0, tiled=True),
        lax.all_gather(w_up, "shard", axis=0, tiled=True),
        lax.all_gather(w_down, "shard", axis=0, tiled=True),
        lax.all_gather(gain_mlp, "shard", axis=0, tiled=True),
    )
    full_gate, full_up, full_down, full_gain_m = mlp_set
    gain_second = full_gain_m.astype(f32)
    normed_mlp = scaled_norm(middle, gain_second).astype(bf16)
    gate_lin = jnp.dot(normed_mlp, full_gate, preferred_element_type=f32)
    upward = jnp.dot(normed_mlp, full_up, preferred_element_type=f32)
    sigmoid_gate = jax.nn.sigmoid(gate_lin)
    silu_gate = gate_lin * sigmoid_gate
    hidden = (silu_gate * upward).astype(bf16)
    result_rows = middle + jnp.dot(hidden, full_down, preferred_element_type=f32)
    output = result_rows.astype(bf16)[None]
    out_grad = cotangent[0].astype(f32)
    back_mlp = out_grad.astype(bf16)
    back_hidden = (
        jnp.einsum("td,fd->tf", back_mlp, full_down, preferred_element_type=f32)
        .astype(bf16)
        .astype(f32)
    )
    back_gate = (
        back_hidden * upward * sigmoid_gate * (1.0 + gate_lin * (1.0 - sigmoid_gate))
    ).astype(bf16)
    back_up = (back_hidden * silu_gate).astype(bf16)
    back_normed_mlp = jnp.einsum("tf,df->td", back_gate, full_gate, preferred_element_type=f32)
    back_normed_mlp = back_normed_mlp + jnp.einsum(
        "tf,df->td", back_up, full_up, preferred_element_type=f32
    )
    middle_norm_back, gain_m_part = norm_back(middle, gain_second, back_normed_mlp)
    back_middle = out_grad + middle_norm_back
    down_part = jnp.einsum("tf,td->fd", hidden, back_mlp, preferred_element_type=f32)
    gate_part = jnp.einsum("td,tf->df", normed_mlp, back_gate, preferred_element_type=f32)
    up_part = jnp.einsum("td,tf->df", normed_mlp, back_up, preferred_element_type=f32)
    gate_owned, up_owned, down_owned, gain_m_owned = (
        lax.psum_scatter(
            gate_part.astype(jnp.bfloat16), "shard", scatter_dimension=0, tiled=True
        ).astype(jnp.float32),
        lax.psum_scatter(
            up_part.astype(jnp.bfloat16), "shard", scatter_dimension=0, tiled=True
        ).astype(jnp.float32),
        lax.psum_scatter(
            down_part.astype(jnp.bfloat16), "shard", scatter_dimension=0, tiled=True
        ).astype(jnp.float32),
        lax.psum_scatter(
            gain_m_part.astype(jnp.bfloat16), "shard", scatter_dimension=0, tiled=True
        ).astype(jnp.float32),
    )
    back_branch = back_middle.astype(bf16)
    back_attended = jnp.einsum(
        "td,qd->tq", back_branch, full_out, preferred_element_type=f32
    ).astype(bf16)
    back_group = lax.all_to_all(
        back_attended.reshape(row_count, seq_count, width_q),
        "seq",
        split_axis=1,
        concat_axis=0,
        tiled=True,
    )
    back_blocks = back_group.reshape(blocks, block_rows, local_kv, spread, HEAD_DIM)

    def backward_block(running, bundle):
        query_block, back_block, logsum_block, start_row = bundle
        scores = masked_scores(query_block, start_row)
        attn_probs = jnp.exp(scores - logsum_block[..., None])
        back_probs = jnp.einsum(
            "qkgd,ckd->kgqc", back_block, value_group, preferred_element_type=f32
        )
        row_terms = jnp.sum(back_probs * attn_probs, axis=-1, keepdims=True)
        back_scores = (attn_probs * (back_probs - row_terms)).astype(bf16)
        probs_low = attn_probs.astype(bf16)
        back_query = (
            jnp.einsum("kgqc,ckd->qkgd", back_scores, key_group, preferred_element_type=f32)
            * score_scale
        )
        back_keys = (
            jnp.einsum("kgqc,qkgd->ckd", back_scores, query_block, preferred_element_type=f32)
            * score_scale
        )
        back_vals = jnp.einsum("kgqc,qkgd->ckd", probs_low, back_block, preferred_element_type=f32)
        return ((running[0] + back_keys, running[1] + back_vals), back_query.astype(bf16))

    zero_pair = jnp.zeros((length, local_kv, HEAD_DIM), f32)
    (key_group_back, value_group_back), query_back_blocks = lax.scan(
        backward_block, (zero_pair, zero_pair), (query_blocks, back_blocks, logsum_blocks, starts)
    )
    query_back_send = query_back_blocks.reshape(length, 1, width_q)
    pair_back_send = jnp.concatenate(
        [
            key_group_back.astype(bf16).reshape(length, width_kv),
            value_group_back.astype(bf16).reshape(length, width_kv),
        ],
        axis=-1,
    ).reshape(length, 1, 2 * width_kv)
    query_back_rows, pair_back_rows = (
        lax.all_to_all(query_back_send, "seq", split_axis=0, concat_axis=1, tiled=True),
        lax.all_to_all(pair_back_send, "seq", split_axis=0, concat_axis=1, tiled=True),
    )
    key_copy_back = (
        pair_back_rows[:, :, :width_kv].astype(f32).reshape(row_count, KV_HEADS, copies, HEAD_DIM)
    )
    value_copy_back = (
        pair_back_rows[:, :, width_kv:].astype(f32).reshape(row_count, KV_HEADS, copies, HEAD_DIM)
    )
    back_keys_rows = jnp.sum(key_copy_back, axis=2).astype(bf16).astype(f32)
    back_values = (
        jnp.sum(value_copy_back, axis=2).astype(bf16).reshape(row_count, KV_HEADS * HEAD_DIM)
    )
    back_query_heads = query_back_rows.reshape(row_count, HEADS, HEAD_DIM).astype(f32)
    back_query_lin = (
        rotate(back_query_heads, cosine, -sine_table)
        .astype(bf16)
        .reshape(row_count, HEADS * HEAD_DIM)
    )
    back_key_lin = (
        rotate(back_keys_rows, cosine, -sine_table)
        .astype(bf16)
        .reshape(row_count, KV_HEADS * HEAD_DIM)
    )
    back_normed = jnp.einsum("tq,dq->td", back_query_lin, full_query, preferred_element_type=f32)
    back_normed = back_normed + jnp.einsum(
        "tk,dk->td", back_key_lin, full_key, preferred_element_type=f32
    )
    back_normed = back_normed + jnp.einsum(
        "tk,dk->td", back_values, full_value, preferred_element_type=f32
    )
    input_norm_back, gain_a_part = norm_back(inputs, gain_first, back_normed)
    grad_tokens = (back_middle + input_norm_back)[None]
    out_part = jnp.einsum("tq,td->qd", attended, back_branch, preferred_element_type=f32)
    query_part = jnp.einsum("td,tq->dq", normed, back_query_lin, preferred_element_type=f32)
    key_part = jnp.einsum("td,tk->dk", normed, back_key_lin, preferred_element_type=f32)
    value_part = jnp.einsum("td,tk->dk", normed, back_values, preferred_element_type=f32)
    query_owned, key_owned, value_owned, out_owned, gain_a_owned = (
        lax.psum_scatter(
            query_part.astype(jnp.bfloat16), "shard", scatter_dimension=0, tiled=True
        ).astype(jnp.float32),
        lax.psum_scatter(
            key_part.astype(jnp.bfloat16), "shard", scatter_dimension=0, tiled=True
        ).astype(jnp.float32),
        lax.psum_scatter(
            value_part.astype(jnp.bfloat16), "shard", scatter_dimension=0, tiled=True
        ).astype(jnp.float32),
        lax.psum_scatter(
            out_part.astype(jnp.bfloat16), "shard", scatter_dimension=0, tiled=True
        ).astype(jnp.float32),
        lax.psum_scatter(
            gain_a_part.astype(jnp.bfloat16), "shard", scatter_dimension=0, tiled=True
        ).astype(jnp.float32),
    )
    summed = (
        lax.psum(query_owned.astype(jnp.bfloat16), "seq").astype(jnp.float32),
        lax.psum(key_owned.astype(jnp.bfloat16), "seq").astype(jnp.float32),
        lax.psum(value_owned.astype(jnp.bfloat16), "seq").astype(jnp.float32),
        lax.psum(out_owned.astype(jnp.bfloat16), "seq").astype(jnp.float32),
        lax.psum(gate_owned.astype(jnp.bfloat16), "seq").astype(jnp.float32),
        lax.psum(up_owned.astype(jnp.bfloat16), "seq").astype(jnp.float32),
        lax.psum(down_owned.astype(jnp.bfloat16), "seq").astype(jnp.float32),
        lax.psum(gain_a_owned.astype(jnp.bfloat16), "seq").astype(jnp.float32),
        lax.psum(gain_m_owned.astype(jnp.bfloat16), "seq").astype(jnp.float32),
    )
    (
        grad_query,
        grad_key,
        grad_value,
        grad_out,
        grad_gate,
        grad_up,
        grad_down,
        grad_gain_attn,
        grad_gain_mlp,
    ) = summed
    return (
        output,
        grad_tokens,
        grad_query,
        grad_key,
        grad_value,
        grad_out,
        grad_gate,
        grad_up,
        grad_down,
        grad_gain_attn,
        grad_gain_mlp,
    )


def solution(mesh):
    in_specs = (
        P("shard", "seq", None),
        P("shard", None),
        P("shard", None),
        P("shard", None),
        P("shard", None),
        P("shard", None),
        P("shard", None),
        P("shard", None),
        P("shard"),
        P("shard"),
        P("shard", "seq", None),
    )
    out_specs = (
        P("shard", "seq", None),
        P("shard", "seq", None),
        P("shard", None),
        P("shard", None),
        P("shard", None),
        P("shard", None),
        P("shard", None),
        P("shard", None),
        P("shard", None),
        P("shard"),
        P("shard"),
    )
    return jax.shard_map(
        on_device, mesh=mesh, in_specs=in_specs, out_specs=out_specs, check_vma=False
    )
```

profile of v0, /device:TPU:0, one launch (start us, length us, event | category | flops | bytes accessed | tf_op | source)
XLA Modules:
  0.0 2191.0 jit_solution(3335142946585991256)
XLA Ops:
  11.9 13.5 all-gather
  36.0 21.9 all-gather.14.cloned.1.call-done
  64.9 76.3 %all-gather.10.cloned.1.call-done = bf16[2048,2048]{1,0:T(8,128)(2,1)} async-done(((bf16[256,2048]{1,0:T(8,128)(2,1)}), bf16[2048,2048]{1,0:T(8,128)(2,1)}) %all-gather.10.cloned.1.call-update) | async-done | bytes 8388624 | tf_op jit(solution)/shard_map/all_gather | solution.py:70
  141.2 12.4 copy.71
  166.1 12.9 all-to-all-done
  180.8 31.6 %while.28 = (s32[]{:T(128)}, bf16[2,512,1,8,64]{1,4,3,2,0:T(8,128)(2,1)S(1)}, f32[2,1,8,512]{3,2,1,0:T(8,128)}, s32[2]{0:T(128)S(1)}, bf16[2,512,1,8,64]{1,4,3,2...) while((s32[]{:T(128)}, ...), condition=%wide.region_4.5_spmd.clone, body=%wide.region_1.4_spmd.clone.sunk | while | flops 1124856320 | bytes 53875308 | solution.py:128
  238.7 9.3 all-gather.1
  267.1 159.0 %all-gather.18.cloned.1.call-done = bf16[2048,5632]{1,0:T(8,128)(2,1)} async-done(((bf16[256,5632]{1,0:T(8,128)(2,1)}), bf16[2048,5632]{1,0:T(8,128)(2,1)}) %all-gather.18.cloned.1.call-update) | async-done | bytes 23068688 | tf_op jit(solution)/shard_map/all_gather | solution.py:135
  426.0 15.0 fusion.103
  441.0 187.4 %all-gather.20.cloned.1.call-done = bf16[2048,5632]{1,0:T(8,128)(2,1)} async-done(((bf16[256,5632]{1,0:T(8,128)(2,1)}), bf16[2048,5632]{1,0:T(8,128)(2,1)}) %all-gather.20.cloned.1.call-update) | async-done | bytes 23068688 | tf_op jit(solution)/shard_map/all_gather | solution.py:136
  628.4 14.9 fusion.104
  643.3 187.7 %all-gather.22.cloned.1.call-done = bf16[5632,2048]{1,0:T(8,128)(2,1)} async-done(((bf16[704,2048]{1,0:T(8,128)(2,1)}), bf16[5632,2048]{1,0:T(8,128)(2,1)}) %all-gather.22.cloned.1.call-update) | async-done | bytes 23068688 | tf_op jit(solution)/shard_map/all_gather | solution.py:137
  831.0 25.6 %multiply_convert_fusion = (bf16[256,5632]{1,0:T(8,128)(2,1)}, bf16[256,5632]{1,0:T(8,128)(2,1)}, bf16[256,5632]{1,0:T(8,128)(2,1)}) fusion(f32[256,5632]{1,0:T(8,128)} %fusion.103, f32[256,5632]{1,0:T(8,128)} %fusion.104, bf16[5632,2048]{1,0:T(8,128)(2,1)} %all-gather.22.cloned.1.call-done, bf16[1,256,2048]{2,1,0:T(8,128)(2,1)S(1)} %copy-done.16), kind=kOutput, calls=%fused_computation.71 | convolution fusion | flops 5930090496 | bytes 44302336 | tf_op jit(solution)/shard_map/td,fd->tf/dot_general | solution.py:153
  856.6 12.9 fusion.105
  869.5 13.7 multiply_reduce_fusion
  897.7 14.2 all-to-all-done.3
  916.1 89.7 %while.29 = (s32[]{:T(128)}, f32[1024,1,64]{0,2,1:T(8,128)}, f32[1024,1,64]{0,2,1:T(8,128)}, bf16[2,512,1,8,64]{1,4,3,2,0:T(8,128)(2,1)}, bf16[2,512,1,8,64]{1,4...) while((s32[]{:T(128)}, f32[1024,1,64]{0,2,1:T(8,128)}, ...), condition=%wide.region_9.10_spmd.clone, body=%wide.region_7.9_spmd.clone.sunk | while | flops 2723475968 | bytes 173102448 | solution.py:219
  922.5 10.4 fusion.174
  967.4 10.4 fusion.174
  1052.8 17.0 all_to_all.91
  1089.0 12.9 convolution_convert_fusion.2
  1101.9 12.7 convolution_convert_fusion.1
  1115.0 12.7 convolution_convert_fusion
  1127.8 44.6 %reduce-scatter.14.cloned.1.call-done = bf16[256,2048]{1,0:T(8,128)(2,1)} async-done(((bf16[2048,2048]{1,0:T(8,128)(2,1)}), bf16[256,2048]{1,0:T(8,128)(2,1)}) %reduce-scatter.14.cloned.1.call-update) | async-done | bytes 1048592 | tf_op jit(solution)/shard_map/reduce_scatter | solution.py:278
  1172.5 90.3 %reduce-scatter.8.cloned.1.call-done = bf16[256,2048]{1,0:T(8,128)(2,1)} async-done(((bf16[2048,2048]{1,0:T(8,128)(2,1)}), bf16[256,2048]{1,0:T(8,128)(2,1)}) %reduce-scatter.8.cloned.1.call-update) | async-done | bytes 1048592 | tf_op jit(solution)/shard_map/reduce_scatter | solution.py:269
  1262.8 228.0 %reduce-scatter.16.cloned.1.call-done = bf16[256,5632]{1,0:T(8,128)(2,1)} async-done(((bf16[2048,5632]{1,0:T(8,128)(2,1)}), bf16[256,5632]{1,0:T(8,128)(2,1)}) %reduce-scatter.16.cloned.1.call-update) | async-done | bytes 2883600 | tf_op jit(solution)/shard_map/reduce_scatter | solution.py:171
  1490.8 228.2 %reduce-scatter.18.cloned.1.call-done = bf16[256,5632]{1,0:T(8,128)(2,1)} async-done(((bf16[2048,5632]{1,0:T(8,128)(2,1)}), bf16[256,5632]{1,0:T(8,128)(2,1)}) %reduce-scatter.18.cloned.1.call-update) | async-done | bytes 2883600 | tf_op jit(solution)/shard_map/reduce_scatter | solution.py:174
  1719.0 228.0 %reduce-scatter.20.cloned.1.call-done = bf16[704,2048]{1,0:T(8,128)(2,1)} async-done(((bf16[5632,2048]{1,0:T(8,128)(2,1)}), bf16[704,2048]{1,0:T(8,128)(2,1)}) %reduce-scatter.20.cloned.1.call-update) | async-done | bytes 2883600 | tf_op jit(solution)/shard_map/reduce_scatter | solution.py:177
  1948.9 14.3 fusion.70
  1973.2 13.9 all-reduce.2
  1987.3 9.7 all-reduce.3
  2001.6 166.1 %all-reduce.7.cloned.1.call-done = (bf16[256,2048]{1,0:T(8,128)(2,1)}, bf16[256,256]{1,0:T(8,128)(2,1)}, bf16[256,256]{1,0:T(8,128)(2,1)}, bf16[256,2048]{1,0:T(...) async-done(((bf16[256,2048]{1,0:T(8,128)(2,1)}, bf16[256,256]{1,0:T(8,128)(2,1)}, bf16[256,256]{1,0:T(8,128)(2,1)}, ...) | async-done | bytes 11010064 | tf_op jit(solution)/shard_map/psum | solution.py:286
  (260 shorter events, 299.1 us)
Async XLA Ops:
  7.2 27.3 %all-gather.12.cloned.1.call-start = ((), (), s32[]{:S(2)}) async-start(), calls=%async_computation.14 | async-start | bytes 1179648 | tf_op jit(solution)/shard_map/all_gather | solution.py:71
  7.9 49.9 %all-gather.14.cloned.1.call-start = ((), (), s32[]{:S(2)}) async-start(), calls=%async_computation.15 | async-start | bytes 1179648 | tf_op jit(solution)/shard_map/all_gather | solution.py:72
  8.7 132.5 %all-gather.10.cloned.1.call-start = ((), (), s32[]{:S(2)}) async-start(), calls=%async_computation.13 | async-start | bytes 9437184 | tf_op jit(solution)/shard_map/all_gather | solution.py:70
  9.4 249.7 %all-gather.16.cloned.1.call-start = ((), (), s32[]{:S(2)}) async-start(), calls=%async_computation.16 | async-start | bytes 9437184 | tf_op jit(solution)/shard_map/all_gather | solution.py:73
  10.0 416.1 %all-gather.18.cloned.1.call-start = ((), (), s32[]{:S(2)}) async-start(), calls=%async_computation.17 | async-start | bytes 25952256 | tf_op jit(solution)/shard_map/all_gather | solution.py:135
  10.6 14.9 copy-start.2
  10.6 617.9 %all-gather.20.cloned.1.call-start = ((), (), s32[]{:S(2)}) async-start(), calls=%async_computation.18 | async-start | bytes 25952256 | tf_op jit(solution)/shard_map/all_gather | solution.py:136
  11.2 819.8 %all-gather.22.cloned.1.call-start = ((), (), s32[]{:S(2)}) async-start(), calls=%async_computation.19 | async-start | bytes 25952256 | tf_op jit(solution)/shard_map/all_gather | solution.py:137
  25.4 128.1 %copy-start.28 = (f32[8,1,256]{2,1,0:T(1,128)}, f32[8,1,256]{2,1,0:T(1,128)S(1)}, u32[]{:S(2)}) copy-start(f32[8,1,256]{2,1,0:T(1,128)S(1)} %convert_element_type.304) | copy-start | bytes 24580
  25.7 32.1 %copy-start.35 = (f32[256]{0:T(256)}, f32[256]{0:T(256)S(1)}, u32[]{:S(2)}) copy-start(f32[256]{0:T(256)S(1)} %fusion.71) | copy-start | bytes 3076
  25.8 127.8 %copy-start.33 = (f32[256]{0:T(256)}, f32[256]{0:T(256)S(1)}, u32[]{:S(2)}) copy-start(f32[256]{0:T(256)S(1)} %fusion.93) | copy-start | bytes 3076
  26.6 132.8 %copy-start.25 = (f32[256,32]{0,1:T(8,128)}, f32[256,32]{0,1:T(8,128)S(1)}, u32[]{:S(2)}) copy-start(f32[256,32]{0,1:T(8,128)S(1)} %get-tuple-element.290) | copy-start | bytes 98308
  61.2 99.6 %all-to-all-start.1 = ((bf16[256,4,128]{0,2,1:T(8,128)(2,1)}), bf16[256,4,128]{0,2,1:T(8,128)(2,1)S(1)}, u32[]{:S(2)}, u32[]{:S(2)}) async-start(bf16[256,4,128]{0,2,1:T(8,128)(2,1)} %pad_maximum_fusion.1), calls=%async_computation.1 | async-start | bytes 524288 | tf_op jit(solution)/shard_map/all_to_all | solution.py:99
  160.8 18.1 all-to-all-start
  235.2 17.0 all-to-all-start.2
  267.1 361.4 %copy-start.10 = (bf16[256,2048]{1,0:T(8,128)(2,1)}, bf16[256,2048]{1,0:T(8,128)(2,1)S(1)}, u32[]{:S(2)}) copy-start(bf16[256,2048]{1,0:T(8,128)(2,1)S(1)} %multiply_convert_fusion.3) | copy-start | bytes 3145732
  441.0 390.0 %copy-start.16 = (bf16[1,256,2048]{2,1,0:T(8,128)(2,1)S(1)}, bf16[1,256,2048]{2,1,0:T(8,128)(2,1)}, u32[]{:S(2)}) copy-start(bf16[1,256,2048]{2,1,0:T(8,128)(2,1)} %param.25) | copy-start | bytes 3145732
  856.6 12.9 copy-start.8
  894.1 17.8 all-to-all-start.3
  897.7 230.1 %reduce-scatter.10.cloned.1.call-start = ((), (), s32[]{:S(2)}) async-start(), calls=%async_computation.21 | async-start | bytes 1179648 | tf_op jit(solution)/shard_map/reduce_scatter | solution.py:272
  1006.9 11.1 copy-start.26
  1006.9 11.1 copy-start.27
  1008.0 10.0 copy-start.4
  1019.7 108.2 %reduce-scatter.12.cloned.1.call-start = ((), (), s32[]{:S(2)}) async-start(), calls=%async_computation.22 | async-start | bytes 1179648 | tf_op jit(solution)/shard_map/reduce_scatter | solution.py:275
  1021.3 151.1 %reduce-scatter.14.cloned.1.call-start = ((), (), s32[]{:S(2)}) async-start(), calls=%async_computation.23 | async-start | bytes 9437184 | tf_op jit(solution)/shard_map/reduce_scatter | solution.py:278
  1028.5 234.2 %reduce-scatter.8.cloned.1.call-start = ((), (), s32[]{:S(2)}) async-start(), calls=%async_computation.20 | async-start | bytes 9437184 | tf_op jit(solution)/shard_map/reduce_scatter | solution.py:269
  1088.9 401.9 %reduce-scatter.16.cloned.1.call-start = ((), (), s32[]{:S(2)}) async-start(), calls=%async_computation.24 | async-start | bytes 25952256 | tf_op jit(solution)/shard_map/reduce_scatter | solution.py:171
  1101.9 617.1 %reduce-scatter.18.cloned.1.call-start = ((), (), s32[]{:S(2)}) async-start(), calls=%async_computation.25 | async-start | bytes 25952256 | tf_op jit(solution)/shard_map/reduce_scatter | solution.py:174
  1114.7 832.3 %reduce-scatter.20.cloned.1.call-start = ((), (), s32[]{:S(2)}) async-start(), calls=%async_computation.26 | async-start | bytes 25952256 | tf_op jit(solution)/shard_map/reduce_scatter | solution.py:177
  1127.7 1040.0 %all-reduce.7.cloned.1.call-start = ((), (), s32[]{:S(2)}) async-start(), calls=%async_computation.27 | async-start | bytes 22020096 | tf_op jit(solution)/shard_map/psum | solution.py:286
  1948.9 14.4 copy-start.20
  1971.0 27.2 %copy-start.36 = (f32[256]{0:T(256)S(1)}, f32[256]{0:T(256)}, u32[]{:S(2)}) copy-start(f32[256]{0:T(256)} %copy-done.35) | copy-start | bytes 3076
  (35 other events, 140.9 us)
Sparse Core Ops, SparseCore 0:
  9.6 24.8 all-gather.11
  36.1 21.7 all-gather.13
  59.4 81.6 all-gather.9
  142.6 80.5 all-gather.15
  224.7 201.2 all-gather.17
  427.5 200.8 all-gather.19
  630.1 200.8 all-gather.21
  1019.8 29.1 reduce-scatter.9
  1051.8 30.5 reduce-scatter.11
  1084.6 87.8 reduce-scatter.13
  1174.8 87.9 reduce-scatter.7
  1265.0 225.7 reduce-scatter.15
  1493.2 225.7 reduce-scatter.17
  1721.2 225.7 reduce-scatter.19
  1951.6 216.1 all-reduce.6
where the time goes:
time: 2200 us; the launch traced here: 2190 us
  waiting for transfers between devices  1660 us (75%)
  matrix products  259 us (12%)
  local copies, waits for them, and re-layouts  89.8 us (4%)
  other arithmetic  77.8 us (4%)
  blocking collectives  71.6 us (3%)
    reduce_scatter x1, waiting for transfers between devices, on_device(): lax.psum_scatter(up_part.astype(jnp.bfloat16), 'shard', scatter_dimension...  228 us
    reduce_scatter x1, waiting for transfers between devices, on_device(): lax.psum_scatter(down_part.astype(jnp.bfloat16), 'shard', scatter_dimensi...  228 us
    reduce_scatter x1, waiting for transfers between devices, on_device(): lax.psum_scatter(gate_part.astype(jnp.bfloat16), 'shard', scatter_dimensi...  228 us
    all_gather x1, waiting for transfers between devices, on_device(): lax.all_gather(w_down, 'shard', axis=0, tiled=True)  188 us
    all_gather x1, waiting for transfers between devices, on_device(): lax.all_gather(w_up, 'shard', axis=0, tiled=True)  187 us
    psum x1, waiting for transfers between devices, on_device(): lax.psum(query_owned.astype(jnp.bfloat16), 'seq').astype(jnp.float32)  166 us
    all_gather x1, waiting for transfers between devices, on_device(): lax.all_gather(w_gate, 'shard', axis=0, tiled=True)  159 us
    reduce_scatter x1, waiting for transfers between devices, on_device(): lax.psum_scatter(query_part.astype(jnp.bfloat16), 'shard', scatter_dimens...  90.3 us
  transfers between devices with their start and end apart: 19, of which 15 were waited for; matrix products, arithmetic and copies ran while one was open for 11% of the time, Pallas kernels for 0%

commit v1 on v0

v1 whole, which is shorter than its diff:
```python
import functools
import math

import jax
import jax.numpy as jnp
from jax import lax
from jax.experimental import pallas as pl
from jax.experimental.pallas import tpu as pltpu
from jax.sharding import PartitionSpec as P

HEADS = 32
KV_HEADS = 4
HEAD_DIM = 64
PAIR = 2 * HEAD_DIM

EPSILON = 1e-05
THETA = 10000.0
MASKED = -1e30

f32 = jnp.float32
bf16 = jnp.bfloat16

NT = (((1,), (1,)), ((), ()))


def hop(value, bit):
    count = lax.axis_size("seq")
    return lax.ppermute(value, "seq", [(i, i ^ bit) for i in range(count)])


def gather_seq(block):
    count = lax.axis_size("seq")
    blocks = [block]
    if count >= 2:
        near = hop(block, 1)
        blocks.append(near)
    if count >= 4:
        other = hop(block, 2)
        half = block.shape[0] // 2
        far = jnp.concatenate([hop(near[:half], 2), hop(other[half:], 1)], axis=0)
        blocks += [other, far]
    bit = 4
    while bit < count:
        blocks += [hop(one, bit) for one in blocks]
        bit *= 2
    return blocks


def add_low(first, second):
    return (first.astype(f32) + second.astype(f32)).astype(bf16)


def scatter_seq(parts):
    count = lax.axis_size("seq")
    bit = count // 2
    while bit >= 4:
        there = [hop(parts[bit + r], bit) for r in range(bit)]
        parts = [add_low(parts[r], there[r]) for r in range(bit)]
        bit //= 2
    total = parts[0].astype(f32)
    if count >= 4:
        half = parts[3].shape[0] // 2
        upper = hop(parts[3][:half], 1)
        lower = hop(parts[3][half:], 2)
        kept_x = hop(parts[1][:half], 1)
        kept_y = hop(parts[2][half:], 2)
        sent_y = hop(add_low(parts[2][:half], upper), 2)
        sent_x = hop(add_low(parts[1][half:], lower), 1)
        total = total + jnp.concatenate([kept_x, sent_x], axis=0).astype(f32)
        total = total + jnp.concatenate([sent_y, kept_y], axis=0).astype(f32)
    elif count == 2:
        total = total + hop(parts[1], 1).astype(f32)
    return total


def in_order(stacked):
    count = stacked.shape[0]
    place = lax.axis_index("seq")
    bit = 1
    while bit < count:
        shaped = stacked.reshape((count // (2 * bit), 2, bit) + stacked.shape[1:])
        stacked = jnp.where((place & bit) != 0, shaped[:, ::-1], shaped).reshape(stacked.shape)
        bit *= 2
    return stacked


def rms_scale(values):
    return lax.rsqrt(jnp.mean(values * values, axis=-1, keepdims=True) + EPSILON)


def lane_in_first_half(shape):
    return lax.broadcasted_iota(jnp.int32, shape, 1) < HEAD_DIM


def swap_quarters(values):
    quarter = HEAD_DIM // 2
    lane = lax.broadcasted_iota(jnp.int32, values.shape, 1)
    return jnp.where(
        lane % HEAD_DIM < quarter,
        pltpu.roll(values, PAIR - quarter, 1),
        pltpu.roll(values, quarter, 1),
    )


def project_kernel(width_q, x_ref, gain_ref, w_ref, cos_ref, sin_ref, n_ref, q_ref, k_ref, v_ref):
    values = x_ref[0].astype(f32)
    scale = lax.rsqrt(jnp.mean(values * values, axis=-1, keepdims=True) + EPSILON)
    normed = (values * scale * gain_ref[...].astype(f32)).astype(bf16)
    n_ref[0] = normed
    lin = jnp.dot(normed, w_ref[...], preferred_element_type=f32)
    cosine, sine = cos_ref[0], sin_ref[0]
    for at in range(0, width_q, PAIR):
        part = lin[:, at : at + PAIR]
        turned = (part * cosine + swap_quarters(part) * sine).astype(bf16)
        q_ref[0, :, at : at + PAIR] = (turned.astype(f32) * HEAD_DIM**-0.5).astype(bf16)
    both = lin[:, width_q : width_q + PAIR]
    swapped = pltpu.roll(both, HEAD_DIM, 1)
    first = lane_in_first_half(both.shape)
    keys = jnp.where(first, both, swapped)
    k_ref[0] = (keys * cosine + swap_quarters(keys) * sine).astype(bf16)
    v_ref[0] = jnp.where(first, swapped, both).astype(bf16)


def project(x, gain, weights, cosine, sine, width_q):
    count, rows, width = x.shape
    row_block = lambda last: pl.BlockSpec((1, rows, last), lambda i: (i, 0, 0))
    whole = lambda shape: pl.BlockSpec(shape, lambda i: (0,) * len(shape))
    shape = lambda last: jax.ShapeDtypeStruct((count, rows, last), bf16)
    return pl.pallas_call(
        functools.partial(project_kernel, width_q),
        grid=(count,),
        in_specs=[
            row_block(width),
            whole((1, width)),
            whole(weights.shape),
            row_block(PAIR),
            row_block(PAIR),
        ],
        out_specs=[row_block(width), row_block(width_q), row_block(PAIR), row_block(PAIR)],
        out_shape=[shape(width), shape(width_q), shape(PAIR), shape(PAIR)],
        compiler_params=pltpu.CompilerParams(vmem_limit_bytes=40 * 2**20),
        cost_estimate=pl.CostEstimate(
            flops=2 * count * rows * width * (width_q + PAIR),
            bytes_accessed=6 * count * rows * width,
            transcendentals=0,
        ),
        name="project",
    )(x, gain, weights, cosine, sine)


def take_keys(count, rows, place, k_ref, v_ref, keys_of, values_of):
    for r in range(count):
        at = pl.multiple_of((place ^ r) * rows, rows)
        keys, values = k_ref[r], v_ref[r]
        first = lane_in_first_half(keys.shape)
        zero = jnp.zeros_like(keys)
        keys_of(0, at, jnp.where(first, keys, zero))
        keys_of(1, at, jnp.where(first, zero, keys))
        values_of(0, at, jnp.where(first, values, zero))
        values_of(1, at, jnp.where(first, zero, values))


def attend_kernel(
    count, rows, place_ref, q_ref, k_ref, v_ref, o_ref, l_ref, key_s, value_s, score_s
):
    block = pl.program_id(1)

    @pl.when((pl.program_id(0) == 0) & (block == 0))
    def _():
        def keys_of(h, at, value):
            key_s[h, pl.ds(at, rows), :] = value

        def values_of(h, at, value):
            value_s[h, :, pl.ds(at, rows)] = value.astype(f32).T.astype(bf16)

        take_keys(count, rows, place_ref[0], k_ref, v_ref, keys_of, values_of)

    key_at = lax.broadcasted_iota(jnp.int32, (rows, rows), 0)
    query_at = lax.broadcasted_iota(jnp.int32, (rows, rows), 1)
    allowed = key_at <= query_at

    for c in range(count):

        @pl.when(block == c)
        def _(c=c):
            queries = q_ref[0]
            total = None
            for h in range(2):
                highest = None
                for t in range(c + 1):
                    scores = lax.dot_general(
                        key_s[h, t * rows : (t + 1) * rows, :],
                        queries,
                        NT,
                        preferred_element_type=f32,
                    )
                    if t == c:
                        scores = jnp.where(allowed, scores, MASKED)
                    score_s[h, t * rows : (t + 1) * rows, :] = scores
                    top = jnp.max(scores, axis=0, keepdims=True)
                    highest = top if highest is None else jnp.maximum(highest, top)
                weight = None
                result = None
                for t in range(c + 1):
                    exponent = jnp.exp(score_s[h, t * rows : (t + 1) * rows, :] - highest)
                    one = jnp.sum(exponent, axis=0, keepdims=True)
                    weight = one if weight is None else weight + one
                    part = jnp.dot(
                        value_s[h, :, t * rows : (t + 1) * rows],
                        exponent.astype(bf16),
                        preferred_element_type=f32,
                    )
                    result = part if result is None else result + part
                l_ref[0, 0, h : h + 1, :] = highest + jnp.log(weight)
                result = result / weight
                total = result if total is None else total + result
            o_ref[0] = total.T.astype(bf16)


def attend(place, queries, keys, values):
    count, rows, width = queries.shape
    pairs = width // PAIR
    length = count * rows
    whole = pl.BlockSpec((count, rows, PAIR), lambda p, i, at: (0, 0, 0))
    mine = pl.BlockSpec((1, rows, PAIR), lambda p, i, at: (i ^ at[0], 0, p))
    return pl.pallas_call(
        functools.partial(attend_kernel, count, rows),
        grid_spec=pltpu.PrefetchScalarGridSpec(
            num_scalar_prefetch=1,
            grid=(pairs, count),
            in_specs=[mine, whole, whole],
            out_specs=[mine, pl.BlockSpec((1, 1, 8, rows), lambda p, i, at: (p, i, 0, 0))],
            scratch_shapes=[
                pltpu.VMEM((2, length, PAIR), bf16),
                pltpu.VMEM((2, PAIR, length), bf16),
                pltpu.VMEM((2, length, rows), f32),
            ],
        ),
        out_shape=[
            jax.ShapeDtypeStruct(queries.shape, bf16),
            jax.ShapeDtypeStruct((pairs, count, 8, rows), f32),
        ],
        compiler_params=pltpu.CompilerParams(vmem_limit_bytes=40 * 2**20),
        cost_estimate=pl.CostEstimate(
            flops=4 * pairs * length * length * PAIR,
            bytes_accessed=4 * length * width,
            transcendentals=pairs * length * length,
        ),
        name="attend",
    )(place, queries, keys, values)


def attend_back_kernel(
    count,
    rows,
    place_ref,
    q_ref,
    k_ref,
    v_ref,
    o_ref,
    d_ref,
    l_ref,
    cos_ref,
    sin_ref,
    dq_ref,
    dkv_ref,
    key_s,
    flat_s,
    value_s,
    dk_s,
    dv_s,
):
    pair, block = pl.program_id(0), pl.program_id(1)
    place = place_ref[0]

    @pl.when((pair == 0) & (block == 0))
    def _():
        def keys_of(h, at, value):
            key_s[h, pl.ds(at, rows), :] = value
            flat_s[h, :, pl.ds(at, rows)] = value.astype(f32).T.astype(bf16)

        def values_of(h, at, value):
            value_s[h, pl.ds(at, rows), :] = value

        take_keys(count, rows, place, k_ref, v_ref, keys_of, values_of)
        dk_s[...] = jnp.zeros_like(dk_s)
        dv_s[...] = jnp.zeros_like(dv_s)

    key_at = lax.broadcasted_iota(jnp.int32, (rows, rows), 0)
    query_at = lax.broadcasted_iota(jnp.int32, (rows, rows), 1)
    allowed = key_at <= query_at

    for c in range(count):

        @pl.when(block == c)
        def _(c=c):
            queries, back = q_ref[0], d_ref[0]
            first = lane_in_first_half(queries.shape)
            zero = jnp.zeros_like(queries)
            terms = (back.astype(f32) * o_ref[0].astype(f32)).T
            total = None
            for h in range(2):
                row_term = jnp.sum(
                    terms[h * HEAD_DIM : (h + 1) * HEAD_DIM, :], axis=0, keepdims=True
                )
                query_h = jnp.where(first, queries, zero) if h == 0 else jnp.where(first, zero, queries)
                back_h = jnp.where(first, back, zero) if h == 0 else jnp.where(first, zero, back)
                logsum = l_ref[0, 0, h : h + 1, :]
                for t in range(c + 1):
                    at = slice(t * rows, (t + 1) * rows)
                    scores = lax.dot_general(
                        key_s[h, at, :], queries, NT, preferred_element_type=f32
                    )
                    if t == c:
                        scores = jnp.where(allowed, scores, MASKED)
                    probs = jnp.exp(scores - logsum)
                    back_probs = lax.dot_general(
                        value_s[h, at, :], back, NT, preferred_element_type=f32
                    )
                    back_scores = (probs * (back_probs - row_term)).astype(bf16)
                    dv_s[at, :] += jnp.dot(
                        probs.astype(bf16), back_h, preferred_element_type=f32
                    )
                    dk_s[at, :] += jnp.dot(back_scores, query_h, preferred_element_type=f32)
                    part = jnp.dot(flat_s[h, :, at], back_scores, preferred_element_type=f32)
                    total = part if total is None else total + part
            turned = (total.T * HEAD_DIM**-0.5).astype(bf16).astype(f32)
            dq_ref[0] = (
                turned * cos_ref[block ^ place] - swap_quarters(turned) * sin_ref[block ^ place]
            ).astype(bf16)

    @pl.when((pair == pl.num_programs(0) - 1) & (block == pl.num_programs(1) - 1))
    def _():
        for r in range(count):
            at = pl.multiple_of((place ^ r) * rows, rows)
            keys = dk_s[pl.ds(at, rows), :]
            values = dv_s[pl.ds(at, rows), :]
            keys = (keys + pltpu.roll(keys, HEAD_DIM, 1)).astype(bf16).astype(f32)
            values = values + pltpu.roll(values, HEAD_DIM, 1)
            keys = keys * cos_ref[r] - swap_quarters(keys) * sin_ref[r]
            dkv_ref[r] = jnp.where(lane_in_first_half(keys.shape), keys, values).astype(bf16)


def attend_back(place, queries, keys, values, attended, back, logsum, cosine, sine):
    count, rows, width = queries.shape
    pairs = width // PAIR
    length = count * rows
    whole = pl.BlockSpec((count, rows, PAIR), lambda p, i, at: (0, 0, 0))
    mine = pl.BlockSpec((1, rows, PAIR), lambda p, i, at: (i ^ at[0], 0, p))
    return pl.pallas_call(
        functools.partial(attend_back_kernel, count, rows),
        grid_spec=pltpu.PrefetchScalarGridSpec(
            num_scalar_prefetch=1,
            grid=(pairs, count),
            in_specs=[
                mine,
                whole,
                whole,
                mine,
                mine,
                pl.BlockSpec((1, 1, 8, rows), lambda p, i, at: (p, i, 0, 0)),
                whole,
                whole,
            ],
            out_specs=[mine, whole],
            scratch_shapes=[
                pltpu.VMEM((2, length, PAIR), bf16),
                pltpu.VMEM((2, PAIR, length), bf16),
                pltpu.VMEM((2, length, PAIR), bf16),
                pltpu.VMEM((length, PAIR), f32),
                pltpu.VMEM((length, PAIR), f32),
            ],
        ),
        out_shape=[
            jax.ShapeDtypeStruct(queries.shape, bf16),
            jax.ShapeDtypeStruct((count, rows, PAIR), bf16),
        ],
        compiler_params=pltpu.CompilerParams(vmem_limit_bytes=40 * 2**20),
        cost_estimate=pl.CostEstimate(
            flops=10 * pairs * length * length * PAIR,
            bytes_accessed=8 * length * width,
            transcendentals=pairs * length * length,
        ),
        name="attend_back",
    )(place, queries, keys, values, attended, back, logsum, cosine, sine)


def on_device(
    tokens, w_query, w_key, w_value, w_out, w_gate, w_up, w_down, gain_attn, gain_mlp, cotangent
):
    count = lax.axis_size("seq")
    shards = lax.axis_size("shard")
    place = lax.axis_index("seq")
    mine = tokens[0]
    rows, width = mine.shape
    length = rows * count
    width_q = HEADS * HEAD_DIM // count
    local_kv = max(1, KV_HEADS // count)
    copies = count * local_kv // KV_HEADS
    width_kv = local_kv * HEAD_DIM
    assert width_kv == HEAD_DIM
    ff = w_gate.shape[1]
    piece = ff // (shards * count)
    width_f = shards * piece
    place_arg = place.reshape(1).astype(jnp.int32)

    def columns(weight, start, size):
        return lax.dynamic_slice_in_dim(weight, start, size, axis=1)

    def hidden_columns(weight):
        split = weight.reshape(weight.shape[0], shards, count, piece)
        return lax.dynamic_index_in_dim(split, place, axis=2, keepdims=False).reshape(
            weight.shape[0], width_f
        )

    def from_shards(block):
        return lax.all_gather(block, "shard", axis=0, tiled=True)

    kv_start = (place * local_kv // copies) * HEAD_DIM
    gains = lax.all_gather(jnp.stack([gain_attn, gain_mlp]), "shard", axis=1, tiled=True)
    gain_first, gain_second = gains[0:1], gains[1:2].astype(f32)
    w_qkv = from_shards(
        jnp.concatenate(
            [
                columns(w_query, place * width_q, width_q),
                columns(w_key, kv_start, width_kv),
                columns(w_value, kv_start, width_kv),
            ],
            axis=1,
        )
    )
    part_d = width // count
    w_o_columns = from_shards(columns(w_out, place * part_d, part_d))
    w_gu = from_shards(jnp.concatenate([hidden_columns(w_gate), hidden_columns(w_up)], axis=1))
    w_dn = from_shards(lax.dynamic_slice_in_dim(w_down, place * piece, piece, axis=0))

    inputs = jnp.stack(gather_seq(mine))
    back_mlp = jnp.concatenate(gather_seq(cotangent[0]))

    w_o = jnp.zeros((width_q, width), bf16)
    for r in range(count):
        rows_r = lax.dynamic_slice_in_dim(w_o_columns, (place ^ r) * width_q, width_q, axis=0)
        rows_r = hop(rows_r, r) if r else rows_r
        w_o = lax.dynamic_update_slice_in_dim(w_o, rows_r, (place ^ r) * part_d, axis=1)

    blocks_at = place ^ jnp.arange(count)
    positions = (blocks_at[:, None] * rows + jnp.arange(rows)[None, :]).astype(f32)
    half_dim = HEAD_DIM // 2
    lanes = jnp.arange(PAIR)
    frequency = jnp.exp(
        -math.log(THETA) * (lanes % half_dim).astype(f32) * 2.0 / HEAD_DIM
    )
    angles = positions[:, :, None] * frequency
    cosine = jnp.cos(angles)
    sine = jnp.sin(angles) * jnp.where(lanes % HEAD_DIM < half_dim, -1.0, 1.0)

    normed, queries, keys, values = project(inputs, gain_first, w_qkv, cosine, sine, width_q)
    attended, logsum = attend(place_arg, queries, keys, values)
    attended_rows = attended.reshape(length, width_q)

    def split(array):
        array = array.astype(bf16)
        return [array[r * rows : (r + 1) * rows] for r in range(count)]

    middle = mine.astype(f32) + scatter_seq(
        split(jnp.dot(attended_rows, w_o, preferred_element_type=f32))
    )
    scale_mid = rms_scale(middle)
    normed_mid = middle * scale_mid
    normed_mlp = jnp.concatenate(gather_seq((normed_mid * gain_second).astype(bf16)))

    gate_up = jnp.dot(normed_mlp, w_gu, preferred_element_type=f32)
    gate_lin, upward = gate_up[:, :width_f], gate_up[:, width_f:]
    sigmoid_gate = jax.nn.sigmoid(gate_lin)
    silu_gate = gate_lin * sigmoid_gate
    hidden = (silu_gate * upward).astype(bf16)
    back_hidden = (
        jnp.einsum("td,fd->tf", back_mlp, w_dn, preferred_element_type=f32).astype(bf16).astype(f32)
    )
    back_gate = back_hidden * upward * sigmoid_gate * (1.0 + gate_lin * (1.0 - sigmoid_gate))
    back_up = back_hidden * silu_gate
    back_gu = jnp.concatenate([back_gate.astype(bf16), back_up.astype(bf16)], axis=1)

    back_normed_mlp = scatter_seq(
        split(jnp.einsum("tf,df->td", back_gu, w_gu, preferred_element_type=f32))
    )
    output = middle + scatter_seq(split(jnp.dot(hidden, w_dn, preferred_element_type=f32)))
    output = output.astype(bf16)[None]

    def norm_back(values_in, scale, gain, back):
        branch = back * gain
        return scale * (
            branch - values_in * scale * scale * jnp.mean(branch * values_in, -1, keepdims=True)
        )

    out_grad = cotangent[0].astype(f32)
    gain_m_part = jnp.sum(back_normed_mlp * normed_mid, axis=0)
    back_middle = out_grad + norm_back(middle, scale_mid, gain_second, back_normed_mlp)
    back_branch = jnp.concatenate(gather_seq(back_middle.astype(bf16)))

    def to_owners(part):
        return lax.psum_scatter(part.astype(bf16), "shard", scatter_dimension=0, tiled=True)

    def token_sum(left, right):
        return jnp.einsum("tf,td->fd", left, right, preferred_element_type=f32)

    def whole_rows(owned):
        return in_order(jnp.stack(gather_seq(owned))).astype(f32)

    def whole_columns(owned):
        return jnp.swapaxes(whole_rows(owned), 0, 1)

    grad_down = whole_rows(to_owners(token_sum(hidden, back_mlp)))
    grad_down = grad_down.reshape(count * piece, width)
    own_gu = to_owners(token_sum(normed_mlp, back_gu))
    grad_gu = whole_rows(own_gu).reshape(count, -1, 2, shards, piece)
    grad_gu = grad_gu.transpose(2, 1, 3, 0, 4).reshape(2, -1, ff)

    back_attended = jnp.einsum("td,qd->tq", back_branch, w_o, preferred_element_type=f32)
    back_attended = back_attended.astype(bf16).reshape(count, rows, width_q)
    back_query, back_kv = attend_back(
        place_arg, queries, keys, values, attended, back_attended, logsum, cosine, sine
    )
    back_qkv = jnp.concatenate([back_query, back_kv], axis=2).reshape(length, -1)

    out_part = token_sum(attended_rows, back_branch).astype(bf16)
    out_columns = jnp.zeros((width_q * count, part_d), bf16)
    for r in range(count):
        part_r = lax.dynamic_slice_in_dim(out_part, (place ^ r) * part_d, part_d, axis=1)
        part_r = hop(part_r, r) if r else part_r
        out_columns = lax.dynamic_update_slice_in_dim(
            out_columns, part_r, (place ^ r) * width_q, axis=0
        )
    grad_out = whole_columns(to_owners(out_columns)).reshape(-1, width)

    own_qkv = to_owners(token_sum(normed.reshape(length, width), back_qkv))
    grad_qkv = whole_columns(own_qkv)
    grad_query = grad_qkv[:, :, :width_q].reshape(-1, HEADS * HEAD_DIM)

    def over_copies(part):
        part = part.reshape(-1, KV_HEADS // local_kv, copies, width_kv)
        return jnp.sum(part, axis=2).reshape(-1, KV_HEADS * HEAD_DIM)

    grad_key = over_copies(grad_qkv[:, :, width_q : width_q + width_kv])
    grad_value = over_copies(grad_qkv[:, :, width_q + width_kv :])

    back_normed = scatter_seq(
        split(jnp.einsum("tq,dq->td", back_qkv, w_qkv, preferred_element_type=f32))
    )
    mine_in = mine.astype(f32)
    scale_in = rms_scale(mine_in)
    gain_a_part = jnp.sum(back_normed * (mine_in * scale_in), axis=0)
    grad_tokens = back_middle + norm_back(
        mine_in, scale_in, gain_first.astype(f32), back_normed
    )
    gain_grads = lax.psum(jnp.stack([gain_a_part, gain_m_part]), ("seq", "shard"))
    owned = gain_attn.shape[0]
    gain_grads = lax.dynamic_slice_in_dim(
        gain_grads, lax.axis_index("shard") * owned, owned, axis=1
    )
    return (
        output,
        grad_tokens[None],
        grad_query,
        grad_key,
        grad_value,
        grad_out,
        grad_gu[0],
        grad_gu[1],
        grad_down,
        gain_grads[0],
        gain_grads[1],
    )


def solution(mesh):
    rows = P("shard", "seq", None)
    weight = P("shard", None)
    gain = P("shard")
    in_specs = (rows,) + (weight,) * 7 + (gain, gain, rows)
    out_specs = (rows, rows) + (weight,) * 7 + (gain, gain)
    return jax.shard_map(
        on_device, mesh=mesh, in_specs=in_specs, out_specs=out_specs, check_vma=False
    )
```

time: 2200 us -> 802 us (0.36)
  waiting for transfers between devices: 1660 us -> 338 us
  matrix products: 259 us -> 111 us
  starting transfers between devices: 15.8 us -> 75.4 us
  Pallas kernels: 0 us -> 50.1 us
  other arithmetic: 77.8 us -> 54.7 us
    reduce_scatter x7 -> x4, waiting for transfers between devices: 819 us -> 60.8 us  [to_owners(): lax.psum_scatter(part.astype(bf16), 'shard', scatter_dimension=0, tiled=T...]
    all_gather x7 -> x4, waiting for transfers between devices: 640 us -> 0.01 us  [from_shards(): return lax.all_gather(block, 'shard', axis=0, tiled=True)]
    ppermute x0 -> x62, waiting for transfers between devices: none -> 277 us  [hop(): return lax.ppermute(value, 'seq', [(i, i ^ bit) for i in range(count)])]
    psum x1 -> x0, waiting for transfers between devices: 166 us -> none  [on_device(): lax.psum(query_owned.astype(jnp.bfloat16), 'seq').astype(jnp.float32)]
    dot_general x35 -> x11, matrix products: 259 us -> 111 us  [the longest x4 35.5 us: token_sum(): return jnp.einsum('tf,td->fd', left, right, preferred_element_type=f32)]
    ppermute x0 -> x62, starting transfers between devices: none -> 74.5 us  [hop(): return lax.ppermute(value, 'seq', [(i, i ^ bit) for i in range(count)])]
    pallas_call x0 -> x3, Pallas kernels: none -> 50.1 us  [the longest x1 27 us: attend_back(): pl.pallas_call(functools.partial(attend_back_kernel, count, rows), grid_s...]
    all_to_all x4 -> x0, waiting for transfers between devices: 31.2 us -> none  [the longest x1 14.2 us: on_device(): lax.all_to_all(back_attended.reshape(row_count, seq_count, width_q), 'seq...]
  transfers between devices with their start and end apart: 19 -> 70, of which waited for: 15 -> 39; matrix products, arithmetic and copies ran while one was open for 11% -> 20% of each run, Pallas kernels for 0% -> 6%
where the time goes in v1:
time: 802 us; the launch traced here: 796 us
  waiting for transfers between devices  338 us (42%)
  matrix products  111 us (14%)
  local copies, waits for them, and re-layouts  102 us (13%)
  starting transfers between devices  75.4 us (9%)
  other arithmetic  54.7 us (7%)
  Pallas kernels  50.1 us (6%)
  blocking collectives  49.6 us (6%)
  between operations  15.3 us (2%)
    ppermute x62, waiting for transfers between devices, hop(): return lax.ppermute(value, 'seq', [(i, i ^ bit) for i in range(count)])  277 us
    ppermute x62, starting transfers between devices, hop(): return lax.ppermute(value, 'seq', [(i, i ^ bit) for i in range(count)])  74.5 us
    reduce_scatter x4, waiting for transfers between devices, to_owners(): lax.psum_scatter(part.astype(bf16), 'shard', scatter_dimension=0, tiled=T...  60.8 us
    unnamed x100, local copies, waits for them, and re-layouts  45.3 us
    psum x1, blocking collectives, on_device(): lax.psum(jnp.stack([gain_a_part, gain_m_part]), ('seq', 'shard'))  37.4 us
    dot_general x4, matrix products, token_sum(): return jnp.einsum('tf,td->fd', left, right, preferred_element_type=f32)  35.5 us
    pallas_call x1, Pallas kernels, attend_back(): pl.pallas_call(functools.partial(attend_back_kernel, count, rows), grid_s...  27 us
    dot_general x1, matrix products, on_device(): gate_up = jnp.dot(normed_mlp, w_gu, preferred_element_type=f32)  19 us
  transfers between devices with their start and end apart: 70, of which 39 were waited for; matrix products, arithmetic and copies ran while one was open for 20% of the time, Pallas kernels for 6%

profile of v1, /device:TPU:0, one launch (start us, length us, event | category | flops | bytes accessed | tf_op | source)
XLA Modules:
  0.0 795.5 jit_solution(5925691634154168244)
XLA Ops:
  29.4 12.1 %all_gather.15 = bf16[2,2048]{1,0:T(2,128)(2,1)S(1)} all-gather(bf16[2,256]{1,0:T(2,128)(2,1)S(1)} %pad_maximum_fusion.11), channel_id=1, replica_groups=mesh['seq'=4,'shard'=8] {'shard'}, dimensions={1}, use_global_device_ids=true | all-gather | bytes 9216 | tf_op jit(solution)/shard_map/all_gather | solution.py:420
  99.9 17.5 %attend.1 = (bf16[4,256,512]{2,1,0:T(8,128)(2,1)S(1)}, f32[4,4,8,256]{3,2,1,0:T(8,128)S(1)}) custom-call(s32[1]{0:T(128)} %bitcast.1.place_ref, bf16[4,256,512]{2,1,0:T(8,128)(2,1)S(1)} %get-tuple-element.19.q_ref, bf16[4,256,128]{2,1,0:T(8,128)(2,1)S(1)} %get-tuple-element.20.k_ref, bf16[4,256,128]{2,1,0:T(8,128)(2,1)S(1)} %get-tuple-element.21.v_ref), custom_call_target="tpu_custom_call" | custom-call | flops 2147483648 | bytes 2097152 | tf_op jit(solution)/shard_map/attend/pallas_call | solution.py:226
  127.1 9.4 %collective-permute-done.10 = bf16[128,2048]{1,0:T(8,128)(2,1)S(1)} collective-permute-done((bf16[128,2048]{1,0:T(8,128)(2,1)S(1)}, bf16[128,2048]{1,0:T(8,128)(2,1)S(1)}, u32[]{:S(2)}, u32[]{:S(2)}) %collective-permute-start.10) | collective-permute-done | bytes 524320 | tf_op jit(solution)/shard_map/ppermute | solution.py:28
  140.4 18.5 %collective-permute-done.23 = bf16[256,2048]{1,0:T(8,128)(2,1)S(1)} collective-permute-done((bf16[256,2048]{1,0:T(8,128)(2,1)S(1)}, bf16[256,2048]{1,0:T(8,128)(2,1)S(1)}, u32[]{:S(2)}, u32[]{:S(2)}) %collective-permute-start.23) | collective-permute-done | bytes 1048608 | tf_op jit(solution)/shard_map/ppermute | solution.py:28
  161.1 9.1 %collective-permute-done.7 = bf16[128,2048]{1,0:T(8,128)(2,1)S(1)} collective-permute-done((bf16[128,2048]{1,0:T(8,128)(2,1)S(1)}, bf16[128,2048]{1,0:T(8,128)(2,1)S(1)}, u32[]{:S(2)}, u32[]{:S(2)}) %collective-permute-start.7) | collective-permute-done | bytes 524320 | tf_op jit(solution)/shard_map/ppermute | solution.py:28
  170.2 8.7 %collective-permute-done.9 = bf16[128,2048]{1,0:T(8,128)(2,1)S(1)} collective-permute-done((bf16[128,2048]{1,0:T(8,128)(2,1)S(1)}, bf16[128,2048]{1,0:T(8,128)(2,1)S(1)}, u32[]{:S(2)}, u32[]{:S(2)}) %collective-permute-start.9) | collective-permute-done | bytes 524320 | tf_op jit(solution)/shard_map/ppermute | solution.py:28
  186.7 9.5 %collective-permute-done.25 = bf16[128,2048]{1,0:T(8,128)(2,1)S(1)} collective-permute-done((bf16[128,2048]{1,0:T(8,128)(2,1)S(1)}, bf16[128,2048]{1,0:T(8,128)(2,1)S(1)}, u32[]{:S(2)}, u32[]{:S(2)}) %collective-permute-start.25) | collective-permute-done | bytes 524320 | tf_op jit(solution)/shard_map/ppermute | solution.py:28
  196.3 11.7 %collective-permute-done.13 = bf16[256,2048]{1,0:T(8,128)(2,1)S(1)} collective-permute-done((bf16[256,2048]{1,0:T(8,128)(2,1)S(1)}, bf16[256,2048]{1,0:T(8,128)(2,1)S(1)}, u32[]{:S(2)}, u32[]{:S(2)}) %collective-permute-start.13) | collective-permute-done | bytes 1048608 | tf_op jit(solution)/shard_map/ppermute | solution.py:28
  229.6 19.0 %fusion.34 = f32[1024,2816]{1,0:T(8,128)} fusion(bf16[1024,2048]{1,0:T(8,128)(2,1)} %constant_dynamic-update-slice_fusion, bf16[2048,2816]{0,1:T(8,128)(2,1)} %all-gather.9.cloned.1.call-done), kind=kOutput, calls=%fused_computation.146 | convolution fusion | flops 11811160064 | bytes 27262976 | tf_op jit(solution)/shard_map/dot_general | solution.py:472
  248.7 17.3 %fusion.2 = (bf16[1024,1408]{1,0:T(8,128)(2,1)}, bf16[1024,1408]{1,0:T(8,128)(2,1)}, bf16[1024,1408]{1,0:T(8,128)(2,1)}) fusion(f32[1024,2816]{1,0:T(8,128)} %fusion.34, bf16[1024,2048]{1,0:T(8,128)(2,1)} %copy-done.31, bf16[1408,2048]{1,0:T(8,128)(2,1)} %all-gather.11.cloned.1.call-done), kind=kOutput, calls=%fused_computation.9 | convolution fusion | flops 5930090496 | bytes 30146560 | tf_op jit(solution)/shard_map/td,fd->tf/dot_general | solution.py:478
  266.0 8.4 %convolution_convert_fusion.5 = bf16[1024,2048]{1,0:T(8,128)(2,1)S(1)} fusion(bf16[1024,1408]{1,0:T(8,128)(2,1)} %get-tuple-element.53, bf16[1408,2048]{1,0:T(8,128)(2,1)S(1)} %copy-done.36), kind=kOutput, calls=%fused_computation.24 | convolution fusion | flops 5907677184 | bytes 12845056 | tf_op jit(solution)/shard_map/dot_general | solution.py:487
  277.5 16.8 %convolution_convert_fusion.2 = bf16[1024,2048]{1,0:T(8,128)(2,1)S(1)} fusion(bf16[2048,2816]{0,1:T(8,128)(2,1)} %all-gather.9.cloned.1.call-done, bf16[1024,1408]{1,0:T(8,128)(2,1)} %get-tuple-element.50, bf16[1024,1408]{1,0:T(8,128)(2,1)} %get-tuple-element.49), kind=kOutput, calls=%fused_computation.21 | convolution fusion | flops 11824791552 | bytes 21495808 | tf_op jit(solution)/shard_map/tf,df->td/dot_general | solution.py:485
  299.4 10.1 %collective-permute-done.28 = bf16[128,2048]{1,0:T(8,128)(2,1)S(1)} collective-permute-done((bf16[128,2048]{1,0:T(8,128)(2,1)S(1)}, bf16[128,2048]{1,0:T(8,128)(2,1)S(1)}, u32[]{:S(2)}, u32[]{:S(2)}) %collective-permute-start.28) | collective-permute-done | bytes 524320 | tf_op jit(solution)/shard_map/ppermute | solution.py:28
  311.1 9.8 %collective-permute-done.17 = bf16[128,2048]{1,0:T(8,128)(2,1)S(1)} collective-permute-done((bf16[128,2048]{1,0:T(8,128)(2,1)S(1)}, bf16[128,2048]{1,0:T(8,128)(2,1)S(1)}, u32[]{:S(2)}, u32[]{:S(2)}) %collective-permute-start.17) | collective-permute-done | bytes 524320 | tf_op jit(solution)/shard_map/ppermute | solution.py:28
  323.1 9.1 %collective-permute-done.27 = bf16[128,2048]{1,0:T(8,128)(2,1)S(1)} collective-permute-done((bf16[128,2048]{1,0:T(8,128)(2,1)S(1)}, bf16[128,2048]{1,0:T(8,128)(2,1)S(1)}, u32[]{:S(2)}, u32[]{:S(2)}) %collective-permute-start.27) | collective-permute-done | bytes 524320 | tf_op jit(solution)/shard_map/ppermute | solution.py:28
  334.0 9.4 %collective-permute-done.19 = bf16[128,2048]{1,0:T(8,128)(2,1)S(1)} collective-permute-done((bf16[128,2048]{1,0:T(8,128)(2,1)S(1)}, bf16[128,2048]{1,0:T(8,128)(2,1)S(1)}, u32[]{:S(2)}, u32[]{:S(2)}) %collective-permute-start.19) | collective-permute-done | bytes 524320 | tf_op jit(solution)/shard_map/ppermute | solution.py:28
  343.4 9.5 %collective-permute-done.29 = bf16[128,2048]{1,0:T(8,128)(2,1)S(1)} collective-permute-done((bf16[128,2048]{1,0:T(8,128)(2,1)S(1)}, bf16[128,2048]{1,0:T(8,128)(2,1)S(1)}, u32[]{:S(2)}, u32[]{:S(2)}) %collective-permute-start.29) | collective-permute-done | bytes 524320 | tf_op jit(solution)/shard_map/ppermute | solution.py:28
  359.7 21.4 %collective-permute-done.33 = bf16[256,2048]{1,0:T(8,128)(2,1)S(1)} collective-permute-done((bf16[256,2048]{1,0:T(8,128)(2,1)S(1)}, bf16[256,2048]{1,0:T(8,128)(2,1)S(1)}, u32[]{:S(2)}, u32[]{:S(2)}) %collective-permute-start.33) | collective-permute-done | bytes 1048608 | tf_op jit(solution)/shard_map/ppermute | solution.py:28
  384.2 8.3 %collective-permute-done.35 = bf16[128,2048]{1,0:T(8,128)(2,1)S(1)} collective-permute-done((bf16[128,2048]{1,0:T(8,128)(2,1)S(1)}, bf16[128,2048]{1,0:T(8,128)(2,1)S(1)}, u32[]{:S(2)}, u32[]{:S(2)}) %collective-permute-start.35) | collective-permute-done | bytes 524320 | tf_op jit(solution)/shard_map/ppermute | solution.py:28
  401.5 11.4 %collective-permute-done.47 = bf16[512,512]{1,0:T(8,128)(2,1)S(1)} collective-permute-done((bf16[512,512]{1,0:T(8,128)(2,1)S(1)}, bf16[512,512]{1,0:T(8,128)(2,1)S(1)}, u32[]{:S(2)}, u32[]{:S(2)}) %collective-permute-start.47) | collective-permute-done | bytes 524320 | tf_op jit(solution)/shard_map/ppermute | solution.py:28
  413.7 7.8 collective-permute-done.48
  429.2 27.0 %attend_back.1 = (bf16[4,256,512]{2,1,0:T(8,128)(2,1)S(1)}, bf16[4,256,128]{2,1,0:T(8,128)(2,1)S(1)}) custom-call(s32[1]{0:T(128)} %bitcast.1.place_ref, bf16[4,256,512]{2,1,0:T(8,128)(2,1)S(1)} %get-tuple-element.19.q_ref, bf16[4,256,128]{2,1,0:T(8,128)(2,1)S(1)} %get-tuple-element.20.k_ref, bf16[4,256,128]{2,1,0:T(8,128)(2,1)S(1)} %copy-done.8, ...), custom_call_target="tpu_custom_call" | custom-call | flops 5368709120 | bytes 4194304 | tf_op jit(solution)/shard_map/attend_back/pallas_call | solution.py:350
  462.4 10.7 %convolution_convert_fusion.1 = bf16[1408,2048]{1,0:T(8,128)(2,1)} fusion(bf16[1024,1408]{1,0:T(8,128)(2,1)S(1)} %copy-done.39, bf16[1024,2048]{1,0:T(8,128)(2,1)} %copy-done.31), kind=kOutput, calls=%fused_computation.4 | convolution fusion | flops 5908463616 | bytes 12845056 | tf_op jit(solution)/shard_map/tf,td->fd/dot_general | solution.py:505
  474.9 17.5 %convolution_convert_fusion = bf16[2048,2816]{1,0:T(8,128)(2,1)} fusion(bf16[1024,2048]{1,0:T(8,128)(2,1)} %constant_dynamic-update-slice_fusion, bf16[1024,1408]{1,0:T(8,128)(2,1)} %get-tuple-element.50, bf16[1024,1408]{1,0:T(8,128)(2,1)S(1)} %copy-done.40), kind=kOutput, calls=%fused_computation.1 | convolution fusion | flops 11828461568 | bytes 21495808 | tf_op jit(solution)/shard_map/tf,td->fd/dot_general | solution.py:505
  504.4 10.8 %collective-permute-done.38 = bf16[128,2048]{1,0:T(8,128)(2,1)S(1)} collective-permute-done((bf16[128,2048]{1,0:T(8,128)(2,1)S(1)}, bf16[128,2048]{1,0:T(8,128)(2,1)S(1)}, u32[]{:S(2)}, u32[]{:S(2)}) %collective-permute-start.38) | collective-permute-done | bytes 524320 | tf_op jit(solution)/shard_map/ppermute | solution.py:28
  518.8 7.7 collective-permute-done.37
  546.1 37.4 %psum.7 = f32[2,2048]{1,0:T(2,128)S(1)} all-reduce(f32[2,2048]{1,0:T(2,128)S(1)} %pad_maximum_fusion.10), channel_id=1, replica_groups=mesh['seq'=4,'shard'=8] {'seq','shard'}, use_global_device_ids=true, to_apply=%region_10.11 | all-reduce | flops 4096 | bytes 32768 | tf_op jit(solution)/shard_map/psum | solution.py:556
  606.4 12.3 %collective-permute-done.58 = bf16[176,2048]{1,0:T(8,128)(2,1)S(1)} collective-permute-done((bf16[176,2048]{1,0:T(8,128)(2,1)}, bf16[176,2048]{1,0:T(8,128)(2,1)S(1)}, u32[]{:S(2)}, u32[]{:S(2)}) %collective-permute-start.58) | collective-permute-done | bytes 720928 | tf_op jit(solution)/shard_map/ppermute | solution.py:28
  622.3 60.8 %reduce-scatter.9.cloned.1.call-done = bf16[256,2816]{1,0:T(8,128)(2,1)} async-done(((bf16[2048,2816]{1,0:T(8,128)(2,1)}), bf16[256,2816]{1,0:T(8,128)(2,1)}) %reduce-scatter.9.cloned.1.call-update) | async-done | bytes 1441808 | tf_op jit(solution)/shard_map/reduce_scatter | solution.py:502
  701.1 13.8 %collective-permute-done.54 = bf16[256,2816]{1,0:T(8,128)(2,1)} collective-permute-done((bf16[256,2816]{1,0:T(8,128)(2,1)}, bf16[256,2816]{1,0:T(8,128)(2,1)}, u32[]{:S(2)}, u32[]{:S(2)}) %collective-permute-start.54) | collective-permute-done | bytes 1441824 | tf_op jit(solution)/shard_map/ppermute | solution.py:28
  738.6 8.6 %copy.30 = bf16[2,2,1,256,2816]{3,4,1,0,2:T(8,128)(2,1)} copy(bf16[2,2,1,256,2816]{4,3,1,0,2:T(8,128)(2,1)} %bitcast.112) | data formatting | bytes 11534336 | tf_op jit(solution)/shard_map/reshape | solution.py:81
  759.8 7.6 fusion.27
  (326 shorter events, 311.1 us)
Async XLA Ops:
  7.2 49.3 %all-gather.7.cloned.1.call-start = ((), (), s32[]{:S(2)}) async-start(), calls=%async_computation.5 | async-start | bytes 2359296 | tf_op jit(solution)/shard_map/all_gather | solution.py:417
  9.1 81.2 %all-gather.5.cloned.1.call-start = ((), (), s32[]{:S(2)}) async-start(), calls=%async_computation.4 | async-start | bytes 2949120 | tf_op jit(solution)/shard_map/all_gather | solution.py:417
  12.0 217.7 %all-gather.9.cloned.1.call-start = ((), (), s32[]{:S(2)}) async-start(), calls=%async_computation.6 | async-start | bytes 12976128 | tf_op jit(solution)/shard_map/all_gather | solution.py:417
  23.8 224.9 %all-gather.11.cloned.1.call-start = ((), (), s32[]{:S(2)}) async-start(), calls=%async_computation.7 | async-start | bytes 6488064 | tf_op jit(solution)/shard_map/all_gather | solution.py:417
  23.8 26.5 %collective-permute-start = (bf16[256,2048]{1,0:T(8,128)(2,1)}, bf16[256,2048]{1,0:T(8,128)(2,1)}, u32[]{:S(2)}, u32[]{:S(2)}) collective-permute-start(bf16[256,2048]{1,0:T(8,128)(2,1)} %bitcast.116), channel_id=1, source_target_pairs={{0,8},{8,0},{16,24},{24,16},{1,9},{9,1},{17,25},{25,17},{2,10},{10... | collective-permute-start | bytes 3145736 | tf_op jit(solution)/shard_map/ppermute | solution.py:28
  26.8 26.4 %collective-permute-start.1 = (bf16[256,2048]{1,0:T(8,128)(2,1)}, bf16[256,2048]{1,0:T(8,128)(2,1)}, u32[]{:S(2)}, u32[]{:S(2)}) collective-permute-start(bf16[256,2048]{1,0:T(8,128)(2,1)} %bitcast.117), channel_id=1, source_target_pairs={{0,16},{8,24},{16,0},{24,8},{1,17},{9,25},{17,1},{25,9},{2,18},{10... | collective-permute-start | bytes 3145736 | tf_op jit(solution)/shard_map/ppermute | solution.py:28
  29.3 506.0 %reduce-scatter.7.cloned.1.call-start = ((), (), s32[]{:S(2)}) async-start(), calls=%async_computation.9 | async-start | bytes 2359296 | tf_op jit(solution)/shard_map/reduce_scatter | solution.py:502
  124.7 34.2 %collective-permute-start.23 = (bf16[256,2048]{1,0:T(8,128)(2,1)S(1)}, bf16[256,2048]{1,0:T(8,128)(2,1)S(1)}, u32[]{:S(2)}, u32[]{:S(2)}) collective-permute-start(bf16[256,2048]{1,0:T(8,128)(2,1)S(1)} %bitcast.125), channel_id=1, source_target_pairs={{0,8},{8,0},{16,24},{24,16},{1,9},{9,1},{17,25},{25,17},{2,10},{10... | collective-permute-start | bytes 3145736 | tf_op jit(solution)/shard_map/ppermute | solution.py:28
  125.1 35.4 %collective-permute-start.12 = (bf16[128,2048]{1,0:T(8,128)(2,1)S(1)}, bf16[128,2048]{1,0:T(8,128)(2,1)S(1)}, u32[]{:S(2)}, u32[]{:S(2)}) collective-permute-start(bf16[128,2048]{1,0:T(8,128)(2,1)S(1)} %get-tuple-element.73), channel_id=1, source_target_pairs={{0,16},{8,24},{16,0},{24,8},{1,17},{9,25},{17,1},{25,9},{2,18},{10... | collective-permute-start | bytes 1572872 | tf_op jit(solution)/shard_map/ppermute | solution.py:28
  125.7 44.5 %collective-permute-start.7 = (bf16[128,2048]{1,0:T(8,128)(2,1)S(1)}, bf16[128,2048]{1,0:T(8,128)(2,1)S(1)}, u32[]{:S(2)}, u32[]{:S(2)}) collective-permute-start(bf16[128,2048]{1,0:T(8,128)(2,1)S(1)} %get-tuple-element.72), channel_id=1, source_target_pairs={{0,8},{8,0},{16,24},{24,16},{1,9},{9,1},{17,25},{25,17},{2,10},{10... | collective-permute-start | bytes 1572872 | tf_op jit(solution)/shard_map/ppermute | solution.py:28
  138.3 31.9 %collective-permute-start.11 = (bf16[128,2048]{1,0:T(8,128)(2,1)S(1)}, bf16[128,2048]{1,0:T(8,128)(2,1)S(1)}, u32[]{:S(2)}, u32[]{:S(2)}) collective-permute-start(bf16[128,2048]{1,0:T(8,128)(2,1)S(1)} %get-tuple-element.77), channel_id=1, source_target_pairs={{0,16},{8,24},{16,0},{24,8},{1,17},{9,25},{17,1},{25,9},{2,18},{10... | collective-permute-start | bytes 1572872 | tf_op jit(solution)/shard_map/ppermute | solution.py:28
  140.0 38.9 %collective-permute-start.9 = (bf16[128,2048]{1,0:T(8,128)(2,1)S(1)}, bf16[128,2048]{1,0:T(8,128)(2,1)S(1)}, u32[]{:S(2)}, u32[]{:S(2)}) collective-permute-start(bf16[128,2048]{1,0:T(8,128)(2,1)S(1)} %get-tuple-element.76), channel_id=1, source_target_pairs={{0,8},{8,0},{16,24},{24,16},{1,9},{9,1},{17,25},{25,17},{2,10},{10... | collective-permute-start | bytes 1572872 | tf_op jit(solution)/shard_map/ppermute | solution.py:28
  158.9 26.1 %collective-permute-start.24 = (bf16[256,2048]{1,0:T(8,128)(2,1)S(1)}, bf16[256,2048]{1,0:T(8,128)(2,1)S(1)}, u32[]{:S(2)}, u32[]{:S(2)}) collective-permute-start(bf16[256,2048]{1,0:T(8,128)(2,1)S(1)} %bitcast.126), channel_id=1, source_target_pairs={{0,16},{8,24},{16,0},{24,8},{1,17},{9,25},{17,1},{25,9},{2,18},{10... | collective-permute-start | bytes 3145736 | tf_op jit(solution)/shard_map/ppermute | solution.py:28
  160.5 35.8 %collective-permute-start.25 = (bf16[128,2048]{1,0:T(8,128)(2,1)S(1)}, bf16[128,2048]{1,0:T(8,128)(2,1)S(1)}, u32[]{:S(2)}, u32[]{:S(2)}) collective-permute-start(bf16[128,2048]{1,0:T(8,128)(2,1)S(1)} %slice.280), channel_id=1, source_target_pairs={{0,16},{8,24},{16,0},{24,8},{1,17},{9,25},{17,1},{25,9},{2,18},{10... | collective-permute-start | bytes 1572872 | tf_op jit(solution)/shard_map/ppermute | solution.py:28
  181.9 26.1 %collective-permute-start.13 = (bf16[256,2048]{1,0:T(8,128)(2,1)S(1)}, bf16[256,2048]{1,0:T(8,128)(2,1)S(1)}, u32[]{:S(2)}, u32[]{:S(2)}) collective-permute-start(bf16[256,2048]{1,0:T(8,128)(2,1)S(1)} %get-tuple-element.46), channel_id=1, source_target_pairs={{0,8},{8,0},{16,24},{24,16},{1,9},{9,1},{17,25},{25,17},{2,10},{10... | collective-permute-start | bytes 3145736 | tf_op jit(solution)/shard_map/ppermute | solution.py:28
  183.2 35.5 %collective-permute-start.14 = (bf16[256,2048]{1,0:T(8,128)(2,1)S(1)}, bf16[256,2048]{1,0:T(8,128)(2,1)S(1)}, u32[]{:S(2)}, u32[]{:S(2)}) collective-permute-start(bf16[256,2048]{1,0:T(8,128)(2,1)S(1)} %get-tuple-element.46), channel_id=1, source_target_pairs={{0,16},{8,24},{16,0},{24,8},{1,17},{9,25},{17,1},{25,9},{2,18},{10... | collective-permute-start | bytes 3145736 | tf_op jit(solution)/shard_map/ppermute | solution.py:28
  185.1 30.9 %collective-permute-start.26 = (bf16[128,2048]{1,0:T(8,128)(2,1)S(1)}, bf16[128,2048]{1,0:T(8,128)(2,1)S(1)}, u32[]{:S(2)}, u32[]{:S(2)}) collective-permute-start(bf16[128,2048]{1,0:T(8,128)(2,1)S(1)} %slice.281), channel_id=1, source_target_pairs={{0,8},{8,0},{16,24},{24,16},{1,9},{9,1},{17,25},{25,17},{2,10},{10... | collective-permute-start | bytes 1572872 | tf_op jit(solution)/shard_map/ppermute | solution.py:28
  295.8 25.1 %collective-permute-start.17 = (bf16[128,2048]{1,0:T(8,128)(2,1)S(1)}, bf16[128,2048]{1,0:T(8,128)(2,1)S(1)}, u32[]{:S(2)}, u32[]{:S(2)}) collective-permute-start(bf16[128,2048]{1,0:T(8,128)(2,1)S(1)} %get-tuple-element.71), channel_id=1, source_target_pairs={{0,8},{8,0},{16,24},{24,16},{1,9},{9,1},{17,25},{25,17},{2,10},{10... | collective-permute-start | bytes 1572872 | tf_op jit(solution)/shard_map/ppermute | solution.py:28
  296.9 25.9 %collective-permute-start.22 = (bf16[128,2048]{1,0:T(8,128)(2,1)S(1)}, bf16[128,2048]{1,0:T(8,128)(2,1)S(1)}, u32[]{:S(2)}, u32[]{:S(2)}) collective-permute-start(bf16[128,2048]{1,0:T(8,128)(2,1)S(1)} %get-tuple-element.69), channel_id=1, source_target_pairs={{0,16},{8,24},{16,0},{24,8},{1,17},{9,25},{17,1},{25,9},{2,18},{10... | collective-permute-start | bytes 1572872 | tf_op jit(solution)/shard_map/ppermute | solution.py:28
  298.7 33.4 %collective-permute-start.27 = (bf16[128,2048]{1,0:T(8,128)(2,1)S(1)}, bf16[128,2048]{1,0:T(8,128)(2,1)S(1)}, u32[]{:S(2)}, u32[]{:S(2)}) collective-permute-start(bf16[128,2048]{1,0:T(8,128)(2,1)S(1)} %get-tuple-element.60), channel_id=1, source_target_pairs={{0,8},{8,0},{16,24},{24,16},{1,9},{9,1},{17,25},{25,17},{2,10},{10... | collective-permute-start | bytes 1572872 | tf_op jit(solution)/shard_map/ppermute | solution.py:28
  309.7 33.7 %collective-permute-start.19 = (bf16[128,2048]{1,0:T(8,128)(2,1)S(1)}, bf16[128,2048]{1,0:T(8,128)(2,1)S(1)}, u32[]{:S(2)}, u32[]{:S(2)}) collective-permute-start(bf16[128,2048]{1,0:T(8,128)(2,1)S(1)} %get-tuple-element.67), channel_id=1, source_target_pairs={{0,8},{8,0},{16,24},{24,16},{1,9},{9,1},{17,25},{25,17},{2,10},{10... | collective-permute-start | bytes 1572872 | tf_op jit(solution)/shard_map/ppermute | solution.py:28
  322.8 30.1 %collective-permute-start.29 = (bf16[128,2048]{1,0:T(8,128)(2,1)S(1)}, bf16[128,2048]{1,0:T(8,128)(2,1)S(1)}, u32[]{:S(2)}, u32[]{:S(2)}) collective-permute-start(bf16[128,2048]{1,0:T(8,128)(2,1)S(1)} %get-tuple-element.64), channel_id=1, source_target_pairs={{0,8},{8,0},{16,24},{24,16},{1,9},{9,1},{17,25},{25,17},{2,10},{10... | collective-permute-start | bytes 1572872 | tf_op jit(solution)/shard_map/ppermute | solution.py:28
  423.3 162.2 %reduce-scatter.5.cloned.1.call-start = ((), (), s32[]{:S(2)}) async-start(), calls=%async_computation.8 | async-start | bytes 2949120 | tf_op jit(solution)/shard_map/reduce_scatter | solution.py:502
  462.3 136.7 %reduce-scatter.11.cloned.1.call-start = ((), (), s32[]{:S(2)}) async-start(), calls=%async_computation.11 | async-start | bytes 6488064 | tf_op jit(solution)/shard_map/reduce_scatter | solution.py:502
  473.1 210.0 %reduce-scatter.9.cloned.1.call-start = ((), (), s32[]{:S(2)}) async-start(), calls=%async_computation.10 | async-start | bytes 12976128 | tf_op jit(solution)/shard_map/reduce_scatter | solution.py:502
  501.1 25.4 %collective-permute-start.37 = (bf16[128,2048]{1,0:T(8,128)(2,1)}, bf16[128,2048]{1,0:T(8,128)(2,1)}, u32[]{:S(2)}, u32[]{:S(2)}) collective-permute-start(bf16[128,2048]{1,0:T(8,128)(2,1)} %get-tuple-element.54), channel_id=1, source_target_pairs={{0,8},{8,0},{16,24},{24,16},{1,9},{9,1},{17,25},{25,17},{2,10},{10... | collective-permute-start | bytes 1572872 | tf_op jit(solution)/shard_map/ppermute | solution.py:28
  542.8 41.4 %collective-permute-start.52 = (bf16[128,512]{1,0:T(8,128)(2,1)S(1)}, bf16[128,512]{1,0:T(8,128)(2,1)S(1)}, u32[]{:S(2)}, u32[]{:S(2)}) collective-permute-start(bf16[128,512]{1,0:T(8,128)(2,1)S(1)} %slice.303), channel_id=1, source_target_pairs={{0,16},{8,24},{16,0},{24,8},{1,17},{9,25},{17,1},{25,9},{2,18},{10... | collective-permute-start | bytes 393224 | tf_op jit(solution)/shard_map/ppermute | solution.py:28
  544.6 39.6 %collective-permute-start.53 = (bf16[128,512]{1,0:T(8,128)(2,1)S(1)}, bf16[128,512]{1,0:T(8,128)(2,1)S(1)}, u32[]{:S(2)}, u32[]{:S(2)}) collective-permute-start(bf16[128,512]{1,0:T(8,128)(2,1)S(1)} %slice.304), channel_id=1, source_target_pairs={{0,8},{8,0},{16,24},{24,16},{1,9},{9,1},{17,25},{25,17},{2,10},{10... | collective-permute-start | bytes 393224 | tf_op jit(solution)/shard_map/ppermute | solution.py:28
  619.4 79.3 %collective-permute-start.60 = (bf16[88,2048]{1,0:T(8,128)(2,1)}, bf16[88,2048]{1,0:T(8,128)(2,1)}, u32[]{:S(2)}, u32[]{:S(2)}) collective-permute-start(bf16[88,2048]{1,0:T(8,128)(2,1)} %slice.309), channel_id=1, source_target_pairs={{0,16},{8,24},{16,0},{24,8},{1,17},{9,25},{17,1},{25,9},{2,18},{10... | collective-permute-start | bytes 1081352 | tf_op jit(solution)/shard_map/ppermute | solution.py:28
  620.8 77.9 %collective-permute-start.61 = (bf16[88,2048]{1,0:T(8,128)(2,1)}, bf16[88,2048]{1,0:T(8,128)(2,1)}, u32[]{:S(2)}, u32[]{:S(2)}) collective-permute-start(bf16[88,2048]{1,0:T(8,128)(2,1)} %slice.310), channel_id=1, source_target_pairs={{0,8},{8,0},{16,24},{24,16},{1,9},{9,1},{17,25},{25,17},{2,10},{10... | collective-permute-start | bytes 1081352 | tf_op jit(solution)/shard_map/ppermute | solution.py:28
  683.1 31.8 %collective-permute-start.54 = (bf16[256,2816]{1,0:T(8,128)(2,1)}, bf16[256,2816]{1,0:T(8,128)(2,1)}, u32[]{:S(2)}, u32[]{:S(2)}) collective-permute-start(bf16[256,2816]{1,0:T(8,128)(2,1)} %reduce-scatter.9.cloned.1.call-done), channel_id=1, source_target_pairs={{0,8},{8,0},{16,24},{24,16},{1,9},{9,1},{17,25},{25,17},{2,10},{10... | collective-permute-start | bytes 4325384 | tf_op jit(solution)/shard_map/ppermute | solution.py:28
  684.5 33.1 %collective-permute-start.55 = (bf16[256,2816]{1,0:T(8,128)(2,1)}, bf16[256,2816]{1,0:T(8,128)(2,1)}, u32[]{:S(2)}, u32[]{:S(2)}) collective-permute-start(bf16[256,2816]{1,0:T(8,128)(2,1)} %reduce-scatter.9.cloned.1.call-done), channel_id=1, source_target_pairs={{0,16},{8,24},{16,0},{24,8},{1,17},{9,25},{17,1},{25,9},{2,18},{10... | collective-permute-start | bytes 4325384 | tf_op jit(solution)/shard_map/ppermute | solution.py:28
  (79 other events, 1203.0 us)
Sparse Core Ops, SparseCore 0:
  10.2 31.8 all-gather.6
  44.3 33.3 all-gather.4
  79.9 107.4 all-gather.8
  189.5 58.6 all-gather.10
  423.4 32.2 reduce-scatter.6
  462.4 33.6 reduce-scatter.4
  499.0 63.8 reduce-scatter.10
  565.3 117.7 reduce-scatter.8

commit v2 on v1

--- a/solution.py
+++ b/solution.py
@@ -31,14 +31,17 @@
 def gather_seq(block):
     count = lax.axis_size("seq")
     blocks = [block]
-    if count >= 2:
-        near = hop(block, 1)
-        blocks.append(near)
+    if count == 2:
+        blocks.append(hop(block, 1))
     if count >= 4:
-        other = hop(block, 2)
         half = block.shape[0] // 2
-        far = jnp.concatenate([hop(near[:half], 2), hop(other[half:], 1)], axis=0)
-        blocks += [other, far]
+        upper, lower = block[:half], block[half:]
+        near_upper, other_lower = hop(upper, 1), hop(lower, 2)
+        near_lower, other_upper = hop(lower, 1), hop(upper, 2)
+        far_upper, far_lower = hop(near_upper, 2), hop(other_lower, 1)
+        blocks.append(jnp.concatenate([near_upper, near_lower], axis=0))
+        blocks.append(jnp.concatenate([other_upper, other_lower], axis=0))
+        blocks.append(jnp.concatenate([far_upper, far_lower], axis=0))
     bit = 4
     while bit < count:
         blocks += [hop(one, bit) for one in blocks]
@@ -50,7 +53,11 @@
     return (first.astype(f32) + second.astype(f32)).astype(bf16)
 
 
-def scatter_seq(parts):
+def tie(first, second):
+    return lax.optimization_barrier((first, second))
+
+
+def scatter_seq(parts, filler=None):
     count = lax.axis_size("seq")
     bit = count // 2
     while bit >= 4:
@@ -64,24 +71,15 @@
         lower = hop(parts[3][half:], 2)
         kept_x = hop(parts[1][:half], 1)
         kept_y = hop(parts[2][half:], 2)
+        if filler is not None:
+            (upper, lower), filler = tie((upper, lower), filler)
         sent_y = hop(add_low(parts[2][:half], upper), 2)
         sent_x = hop(add_low(parts[1][half:], lower), 1)
         total = total + jnp.concatenate([kept_x, sent_x], axis=0).astype(f32)
         total = total + jnp.concatenate([sent_y, kept_y], axis=0).astype(f32)
     elif count == 2:
         total = total + hop(parts[1], 1).astype(f32)
-    return total
-
-
-def in_order(stacked):
-    count = stacked.shape[0]
-    place = lax.axis_index("seq")
-    bit = 1
-    while bit < count:
-        shaped = stacked.reshape((count // (2 * bit), 2, bit) + stacked.shape[1:])
-        stacked = jnp.where((place & bit) != 0, shaped[:, ::-1], shaped).reshape(stacked.shape)
-        bit *= 2
-    return stacked
+    return total if filler is None else (total, filler)
 
 
 def rms_scale(values):
@@ -385,6 +383,150 @@
     )(place, queries, keys, values, attended, back, logsum, cosine, sine)
 
 
+def sort_blocks(place, blocks):
+    bit = 1
+    while bit < len(blocks):
+        flip = (place & bit) != 0
+        blocks = [
+            jnp.where(flip, blocks[r ^ bit], blocks[r]) for r in range(len(blocks))
+        ]
+        bit *= 2
+    return blocks
+
+
+def take_columns_kernel(shards, count, piece, place_ref, gate_ref, up_ref, out_ref):
+    width = shards * piece
+    for c in range(count):
+
+        @pl.when(place_ref[0] == c)
+        def _(c=c):
+            for at, ref in ((0, gate_ref), (width, up_ref)):
+                pieces = []
+                for s in range(shards):
+                    start = (s * count + c) * piece
+                    pieces.append(ref[:, start : start + piece].astype(f32))
+                out_ref[:, at : at + width] = jnp.concatenate(pieces, axis=1).astype(bf16)
+
+
+def take_columns(place, w_gate, w_up, shards, count):
+    rows, ff = w_gate.shape
+    piece = ff // (shards * count)
+    step = min(rows, 128)
+    block = lambda last: pl.BlockSpec((step, last), lambda i, at: (i, 0))
+    return pl.pallas_call(
+        functools.partial(take_columns_kernel, shards, count, piece),
+        grid_spec=pltpu.PrefetchScalarGridSpec(
+            num_scalar_prefetch=1,
+            grid=(rows // step,),
+            in_specs=[block(ff), block(ff)],
+            out_specs=block(2 * shards * piece),
+        ),
+        out_shape=jax.ShapeDtypeStruct((rows, 2 * shards * piece), bf16),
+        compiler_params=pltpu.CompilerParams(vmem_limit_bytes=40 * 2**20),
+        cost_estimate=pl.CostEstimate(
+            flops=0, bytes_accessed=6 * rows * ff, transcendentals=0
+        ),
+        name="take_columns",
+    )(place, w_gate, w_up)
+
+
+def put_columns_kernel(shards, count, piece, place_ref, *refs):
+    block_refs = refs[:count]
+    gate_w, up_w, gain_ref, gate_ref, up_ref, gain_out = refs[count:]
+    width = shards * piece
+    blocks = [ref[...].astype(f32) for ref in block_refs]
+    blocks = sort_blocks(place_ref[0], blocks)
+    total = None
+    for at, weight, out in ((0, gate_w, gate_ref), (width, up_w, up_ref)):
+        for s in range(shards):
+            pieces = [one[:, at + s * piece : at + (s + 1) * piece] for one in blocks]
+            joined = jnp.concatenate(pieces, axis=1)
+            here = slice(s * count * piece, (s + 1) * count * piece)
+            out[:, here] = joined
+            term = jnp.sum(joined * weight[:, here].astype(f32), axis=1, keepdims=True)
+            total = term if total is None else total + term
+    gain_out[...] = total / gain_ref[...].astype(f32)
+
+
+def put_columns(place, blocks, w_gate, w_up, gain, shards):
+    count = len(blocks)
+    rows, ff = w_gate.shape
+    piece = ff // (shards * count)
+    step = min(rows, 64)
+    block = lambda last: pl.BlockSpec((step, last), lambda i, at: (i, 0))
+    return pl.pallas_call(
+        functools.partial(put_columns_kernel, shards, count, piece),
+        grid_spec=pltpu.PrefetchScalarGridSpec(
+            num_scalar_prefetch=1,
+            grid=(rows // step,),
+            in_specs=[block(blocks[0].shape[1])] * count + [block(ff), block(ff), block(1)],
+            out_specs=[block(ff), block(ff), block(1)],
+        ),
+        out_shape=[
+            jax.ShapeDtypeStruct((rows, ff), f32),
+            jax.ShapeDtypeStruct((rows, ff), f32),
+            jax.ShapeDtypeStruct((rows, 1), f32),
+        ],
+        compiler_params=pltpu.CompilerParams(vmem_limit_bytes=40 * 2**20),
+        cost_estimate=pl.CostEstimate(
+            flops=0, bytes_accessed=16 * rows * ff, transcendentals=0
+        ),
+        name="put_columns",
+    )(place, *blocks, w_gate, w_up, gain)
+
+
+def put_attention_kernel(count, copies, width_q, place_ref, *refs):
+    block_refs = refs[:count]
+    q_w, k_w, v_w, gain_ref, q_ref, k_ref, v_ref, o_ref, gain_out = refs[count:]
+    blocks = [ref[...].astype(f32) for ref in block_refs]
+    blocks = sort_blocks(place_ref[0], blocks)
+    width_o = o_ref.shape[1] // count
+    for a in range(count):
+        q_ref[:, a * width_q : (a + 1) * width_q] = blocks[a][:, :width_q]
+        o_ref[:, a * width_o : (a + 1) * width_o] = blocks[a][:, width_q + PAIR :]
+    for part, out in ((0, k_ref), (HEAD_DIM, v_ref)):
+        heads = []
+        for h in range(count // copies):
+            one = None
+            for c in range(copies):
+                at = width_q + part
+                term = blocks[h * copies + c][:, at : at + HEAD_DIM]
+                one = term if one is None else one + term
+            heads.append(one)
+        out[...] = jnp.concatenate(heads, axis=1)
+    total = None
+    for weight, out in ((q_w, q_ref), (k_w, k_ref), (v_w, v_ref)):
+        term = jnp.sum(out[...] * weight[...].astype(f32), axis=1, keepdims=True)
+        total = term if total is None else total + term
+    gain_out[...] = total / gain_ref[...].astype(f32)
+
+
+def put_attention(place, blocks, w_query, w_key, w_value, gain, width, copies):
+    count = len(blocks)
+    rows, wide_q = w_query.shape
+    wide_k = w_key.shape[1]
+    step = min(rows, 64)
+    block = lambda last: pl.BlockSpec((step, last), lambda i, at: (i, 0))
+    return pl.pallas_call(
+        functools.partial(put_attention_kernel, count, copies, wide_q // count),
+        grid_spec=pltpu.PrefetchScalarGridSpec(
+            num_scalar_prefetch=1,
+            grid=(rows // step,),
+            in_specs=[block(blocks[0].shape[1])] * count
+            + [block(wide_q), block(wide_k), block(wide_k), block(1)],
+            out_specs=[block(wide_q), block(wide_k), block(wide_k), block(width), block(1)],
+        ),
+        out_shape=[
+            jax.ShapeDtypeStruct((rows, last), f32) for last in (wide_q, wide_k, wide_k, width, 1)
+        ],
+        compiler_params=pltpu.CompilerParams(vmem_limit_bytes=40 * 2**20),
+        cost_estimate=pl.CostEstimate(
+            flops=0, bytes_accessed=16 * rows * wide_q, transcendentals=0
+        ),
+        name="put_attention",
+    )(place, *blocks, w_query, w_key, w_value, gain)
+
+
 def on_device(
     tokens, w_query, w_key, w_value, w_out, w_gate, w_up, w_down, gain_attn, gain_mlp, cotangent
 ):
@@ -407,35 +549,30 @@
     def columns(weight, start, size):
         return lax.dynamic_slice_in_dim(weight, start, size, axis=1)
 
-    def hidden_columns(weight):
-        split = weight.reshape(weight.shape[0], shards, count, piece)
-        return lax.dynamic_index_in_dim(split, place, axis=2, keepdims=False).reshape(
-            weight.shape[0], width_f
-        )
-
     def from_shards(block):
         return lax.all_gather(block, "shard", axis=0, tiled=True)
 
     kv_start = (place * local_kv // copies) * HEAD_DIM
+    part_d = width // count
+    width_qkv = width_q + PAIR
     gains = lax.all_gather(jnp.stack([gain_attn, gain_mlp]), "shard", axis=1, tiled=True)
     gain_first, gain_second = gains[0:1], gains[1:2].astype(f32)
-    w_qkv = from_shards(
+    w_attn = from_shards(
         jnp.concatenate(
             [
                 columns(w_query, place * width_q, width_q),
                 columns(w_key, kv_start, width_kv),
                 columns(w_value, kv_start, width_kv),
+                columns(w_out, place * part_d, part_d),
             ],
             axis=1,
         )
     )
-    part_d = width // count
-    w_o_columns = from_shards(columns(w_out, place * part_d, part_d))
-    w_gu = from_shards(jnp.concatenate([hidden_columns(w_gate), hidden_columns(w_up)], axis=1))
+    w_qkv, w_o_columns = w_attn[:, :width_qkv], w_attn[:, width_qkv:]
+    w_gu = from_shards(take_columns(place_arg, w_gate, w_up, shards, count))
     w_dn = from_shards(lax.dynamic_slice_in_dim(w_down, place * piece, piece, axis=0))
 
     inputs = jnp.stack(gather_seq(mine))
-    back_mlp = jnp.concatenate(gather_seq(cotangent[0]))
 
     w_o = jnp.zeros((width_q, width), bf16)
     for r in range(count):
@@ -447,9 +584,7 @@
     positions = (blocks_at[:, None] * rows + jnp.arange(rows)[None, :]).astype(f32)
     half_dim = HEAD_DIM // 2
     lanes = jnp.arange(PAIR)
-    frequency = jnp.exp(
-        -math.log(THETA) * (lanes % half_dim).astype(f32) * 2.0 / HEAD_DIM
-    )
+    frequency = jnp.exp(-math.log(THETA) * (lanes % half_dim).astype(f32) * 2.0 / HEAD_DIM)
     angles = positions[:, :, None] * frequency
     cosine = jnp.cos(angles)
     sine = jnp.sin(angles) * jnp.where(lanes % HEAD_DIM < half_dim, -1.0, 1.0)
@@ -462,18 +597,36 @@
         array = array.astype(bf16)
         return [array[r * rows : (r + 1) * rows] for r in range(count)]
 
+    def token_sum(left, right):
+        return jnp.einsum("tf,td->fd", left, right, preferred_element_type=f32).astype(bf16)
+
+    def to_owners(part):
+        return lax.psum_scatter(part, "shard", scatter_dimension=0, tiled=True)
+
+    def norm_back(values_in, scale, gain, back):
+        branch = back * gain
+        return scale * (
+            branch - values_in * scale * scale * jnp.mean(branch * values_in, -1, keepdims=True)
+        )
+
     middle = mine.astype(f32) + scatter_seq(
         split(jnp.dot(attended_rows, w_o, preferred_element_type=f32))
     )
     scale_mid = rms_scale(middle)
-    normed_mid = middle * scale_mid
-    normed_mlp = jnp.concatenate(gather_seq((normed_mid * gain_second).astype(bf16)))
+    normed_blocks = gather_seq((middle * scale_mid * gain_second).astype(bf16))
+    normed_blocks, cot = tie(normed_blocks, cotangent[0])
+    normed_mlp = jnp.concatenate(normed_blocks)
+    back_mlp = jnp.concatenate(gather_seq(cot))
 
     gate_up = jnp.dot(normed_mlp, w_gu, preferred_element_type=f32)
     gate_lin, upward = gate_up[:, :width_f], gate_up[:, width_f:]
     sigmoid_gate = jax.nn.sigmoid(gate_lin)
     silu_gate = gate_lin * sigmoid_gate
     hidden = (silu_gate * upward).astype(bf16)
+    down_part = token_sum(hidden, back_mlp)
+    own_down = to_owners(down_part)
+
+    w_dn, down_part = tie(w_dn, down_part)
     back_hidden = (
         jnp.einsum("td,fd->tf", back_mlp, w_dn, preferred_element_type=f32).astype(bf16).astype(f32)
     )
@@ -481,82 +634,58 @@
     back_up = back_hidden * silu_gate
     back_gu = jnp.concatenate([back_gate.astype(bf16), back_up.astype(bf16)], axis=1)
 
-    back_normed_mlp = scatter_seq(
-        split(jnp.einsum("tf,df->td", back_gu, w_gu, preferred_element_type=f32))
-    )
-    output = middle + scatter_seq(split(jnp.dot(hidden, w_dn, preferred_element_type=f32)))
-    output = output.astype(bf16)[None]
-
-    def norm_back(values_in, scale, gain, back):
-        branch = back * gain
-        return scale * (
-            branch - values_in * scale * scale * jnp.mean(branch * values_in, -1, keepdims=True)
-        )
-
-    out_grad = cotangent[0].astype(f32)
-    gain_m_part = jnp.sum(back_normed_mlp * normed_mid, axis=0)
-    back_middle = out_grad + norm_back(middle, scale_mid, gain_second, back_normed_mlp)
-    back_branch = jnp.concatenate(gather_seq(back_middle.astype(bf16)))
-
-    def to_owners(part):
-        return lax.psum_scatter(part.astype(bf16), "shard", scatter_dimension=0, tiled=True)
-
-    def token_sum(left, right):
-        return jnp.einsum("tf,td->fd", left, right, preferred_element_type=f32)
-
-    def whole_rows(owned):
-        return in_order(jnp.stack(gather_seq(owned))).astype(f32)
-
-    def whole_columns(owned):
-        return jnp.swapaxes(whole_rows(owned), 0, 1)
-
-    grad_down = whole_rows(to_owners(token_sum(hidden, back_mlp)))
-    grad_down = grad_down.reshape(count * piece, width)
-    own_gu = to_owners(token_sum(normed_mlp, back_gu))
-    grad_gu = whole_rows(own_gu).reshape(count, -1, 2, shards, piece)
-    grad_gu = grad_gu.transpose(2, 1, 3, 0, 4).reshape(2, -1, ff)
+    parts = split(jnp.einsum("tf,df->td", back_gu, w_gu, preferred_element_type=f32))
+    back_normed_mlp, gu_part = scatter_seq(parts, token_sum(normed_mlp, back_gu))
+    own_gu = to_owners(gu_part)
+
+    back_middle = cot.astype(f32) + norm_back(middle, scale_mid, gain_second, back_normed_mlp)
+    back_blocks = gather_seq(back_middle.astype(bf16))
+    out_parts = split(jnp.dot(hidden, w_dn, preferred_element_type=f32))
+    back_blocks, (out_parts, own_down) = tie(back_blocks, (out_parts, own_down))
+    back_branch = jnp.concatenate(back_blocks)
+    output = (middle + scatter_seq(out_parts)).astype(bf16)[None]
 
     back_attended = jnp.einsum("td,qd->tq", back_branch, w_o, preferred_element_type=f32)
     back_attended = back_attended.astype(bf16).reshape(count, rows, width_q)
+    out_part = token_sum(attended_rows, back_branch)
+    back_attended, out_part = tie(back_attended, out_part)
     back_query, back_kv = attend_back(
         place_arg, queries, keys, values, attended, back_attended, logsum, cosine, sine
     )
     back_qkv = jnp.concatenate([back_query, back_kv], axis=2).reshape(length, -1)
 
-    out_part = token_sum(attended_rows, back_branch).astype(bf16)
-    out_columns = jnp.zeros((width_q * count, part_d), bf16)
+    attn_part = jnp.zeros((width, width_qkv + part_d), bf16)
     for r in range(count):
         part_r = lax.dynamic_slice_in_dim(out_part, (place ^ r) * part_d, part_d, axis=1)
         part_r = hop(part_r, r) if r else part_r
-        out_columns = lax.dynamic_update_slice_in_dim(
-            out_columns, part_r, (place ^ r) * width_q, axis=0
+        attn_part = lax.dynamic_update_slice(attn_part, part_r, ((place ^ r) * width_q, width_qkv))
+    qkv_part = token_sum(normed.reshape(length, width), back_qkv)
+    own_attn = to_owners(lax.dynamic_update_slice(attn_part, qkv_part, (0, 0)))
+
+    parts = split(jnp.einsum("tq,dq->td", back_qkv, w_qkv, preferred_element_type=f32))
+    back_normed = scatter_seq(parts)
+    mine_in = mine.astype(f32)
+    grad_tokens = back_middle + norm_back(
+        mine_in, rms_scale(mine_in), gain_first.astype(f32), back_normed
+    )
+
+    grad_down = jnp.zeros((count * piece, width), f32)
+    for r, block in enumerate(gather_seq(own_down)):
+        grad_down = lax.dynamic_update_slice_in_dim(
+            grad_down, block.astype(f32), (place ^ r) * piece, axis=0
         )
-    grad_out = whole_columns(to_owners(out_columns)).reshape(-1, width)
-
-    own_qkv = to_owners(token_sum(normed.reshape(length, width), back_qkv))
-    grad_qkv = whole_columns(own_qkv)
-    grad_query = grad_qkv[:, :, :width_q].reshape(-1, HEADS * HEAD_DIM)
-
-    def over_copies(part):
-        part = part.reshape(-1, KV_HEADS // local_kv, copies, width_kv)
-        return jnp.sum(part, axis=2).reshape(-1, KV_HEADS * HEAD_DIM)
-
-    grad_key = over_copies(grad_qkv[:, :, width_q : width_q + width_kv])
-    grad_value = over_copies(grad_qkv[:, :, width_q + width_kv :])
-
-    back_normed = scatter_seq(
-        split(jnp.einsum("tq,dq->td", back_qkv, w_qkv, preferred_element_type=f32))
-    )
-    mine_in = mine.astype(f32)
-    scale_in = rms_scale(mine_in)
-    gain_a_part = jnp.sum(back_normed * (mine_in * scale_in), axis=0)
-    grad_tokens = back_middle + norm_back(
-        mine_in, scale_in, gain_first.astype(f32), back_normed
-    )
-    gain_grads = lax.psum(jnp.stack([gain_a_part, gain_m_part]), ("seq", "shard"))
-    owned = gain_attn.shape[0]
-    gain_grads = lax.dynamic_slice_in_dim(
-        gain_grads, lax.axis_index("shard") * owned, owned, axis=1
+    grad_gate, grad_up, grad_gain_mlp = put_columns(
+        place_arg, gather_seq(own_gu), w_gate, w_up, gain_mlp.reshape(-1, 1), shards
+    )
+    grad_query, grad_key, grad_value, grad_out, grad_gain_attn = put_attention(
+        place_arg,
+        gather_seq(own_attn),
+        w_query,
+        w_key,
+        w_value,
+        gain_attn.reshape(-1, 1),
+        width,
+        copies,
     )
     return (
         output,
@@ -565,11 +694,11 @@
         grad_key,
         grad_value,
         grad_out,
-        grad_gu[0],
-        grad_gu[1],
+        grad_gate,
+        grad_up,
         grad_down,
-        gain_grads[0],
-        gain_grads[1],
+        grad_gain_attn.reshape(-1),
+        grad_gain_mlp.reshape(-1),
     )
 
 

time: 802 us -> 657 us (0.82)
  waiting for transfers between devices: 338 us -> 279 us
  local copies, waits for them, and re-layouts: 102 us -> 51.4 us
  blocking collectives: 49.6 us -> 12.7 us
  Pallas kernels: 50.1 us -> 66.6 us
  matrix products: 111 us -> 101 us
    ppermute x62 -> x72, waiting for transfers between devices: 277 us -> 206 us  [hop(): return lax.ppermute(value, 'seq', [(i, i ^ bit) for i in range(count)])]
    psum x1 -> x0, blocking collectives: 37.4 us -> none  [on_device(): lax.psum(jnp.stack([gain_a_part, gain_m_part]), ('seq', 'shard'))]
    unnamed x100 -> x137, local copies, waits for them, and re-layouts: 45.3 us -> 19.4 us
    pallas_call x0 -> x3, Pallas kernels: none -> 16.3 us  [the longest x1 12.6 us: put_columns(): pl.pallas_call(functools.partial(put_columns_kernel, shards, count, piece...]
    another operation x13 -> x0, other arithmetic: 14.8 us -> none  [the longest x8 7.87 us: whole_rows(): return in_order(jnp.stack(gather_seq(owned))).astype(f32)]
    slice x22 -> x12, local copies, waits for them, and re-layouts: 25.4 us -> 13.8 us  [the longest x7 7.99 us: gather_seq(): upper, lower = (block[:half], block[half:])]
    reshape x2, local copies, waits for them, and re-layouts: 10.1 us -> 0.19 us  [the longest x1 0.1 us: on_device(): gain_mlp.reshape(-1, 1)]
    concatenate x2 -> x12, other arithmetic: 2.01 us -> 11.5 us  [the longest x4 4.97 us: gather_seq(): blocks.append(jnp.concatenate([other_upper, other_lower], axis=0))]
  transfers between devices with their start and end apart: 70 -> 78, of which waited for: 39 -> 40; matrix products, arithmetic and copies ran while one was open for 20% -> 26% of each run, Pallas kernels for 6% -> 8%
where the time goes in v2:
time: 657 us; the launch traced here: 653 us
  waiting for transfers between devices  279 us (42%)
  matrix products  101 us (15%)
  starting transfers between devices  77.1 us (12%)
  Pallas kernels  66.6 us (10%)
  local copies, waits for them, and re-layouts  51.4 us (8%)
  other arithmetic  48.4 us (7%)
  between operations  15.6 us (2%)
  blocking collectives  12.7 us (2%)
    ppermute x72, waiting for transfers between devices, hop(): return lax.ppermute(value, 'seq', [(i, i ^ bit) for i in range(count)])  206 us
    ppermute x72, starting transfers between devices, hop(): return lax.ppermute(value, 'seq', [(i, i ^ bit) for i in range(count)])  76 us
    reduce_scatter x3, waiting for transfers between devices, to_owners(): return lax.psum_scatter(part, 'shard', scatter_dimension=0, tiled=True)  69.2 us
    dot_general x4, matrix products, token_sum(): jnp.einsum('tf,td->fd', left, right, preferred_element_type=f32)  37.3 us
    pallas_call x1, Pallas kernels, attend_back(): pl.pallas_call(functools.partial(attend_back_kernel, count, rows), grid_s...  27.2 us
    unnamed x137, local copies, waits for them, and re-layouts  19.4 us
    pallas_call x1, Pallas kernels, attend(): pl.pallas_call(functools.partial(attend_kernel, count, rows), grid_spec=p...  17.6 us
    dot_general x1, matrix products, on_device(): gate_up = jnp.dot(normed_mlp, w_gu, preferred_element_type=f32)  17.3 us
  transfers between devices with their start and end apart: 78, of which 40 were waited for; matrix products, arithmetic and copies ran while one was open for 26% of the time, Pallas kernels for 8%

profile of v2, /device:TPU:0, one launch (start us, length us, event | category | flops | bytes accessed | tf_op | source)
XLA Modules:
  0.0 652.5 jit_solution(10120463310835193360)
XLA Ops:
  23.5 12.7 %all_gather.12 = bf16[2,2048]{1,0:T(2,128)(2,1)S(1)} all-gather(bf16[2,256]{1,0:T(2,128)(2,1)S(1)} %pad_maximum_fusion.20), channel_id=1, replica_groups=mesh['seq'=4,'shard'=8] {'shard'}, dimensions={1}, use_global_device_ids=true | all-gather | bytes 9216 | tf_op jit(solution)/shard_map/all_gather | solution.py:558
  36.9 9.4 %collective-permute-done.3 = bf16[128,2048]{1,0:T(8,128)(2,1)} collective-permute-done((bf16[128,2048]{1,0:T(8,128)(2,1)}, bf16[128,2048]{1,0:T(8,128)(2,1)}, u32[]{:S(2)}, u32[]{:S(2)}) %collective-permute-start.3) | collective-permute-done | bytes 524320 | tf_op jit(solution)/shard_map/ppermute | solution.py:28
  72.6 5.6 project.1
  78.2 17.6 %attend.1 = (bf16[4,256,512]{2,1,0:T(8,128)(2,1)S(1)}, f32[4,4,8,256]{3,2,1,0:T(8,128)S(1)}) custom-call(s32[1]{0:T(128)} %bitcast.1.place_ref, bf16[4,256,512]{2,1,0:T(8,128)(2,1)S(1)} %get-tuple-element.47.q_ref, bf16[4,256,128]{2,1,0:T(8,128)(2,1)S(1)} %get-tuple-element.48.k_ref, bf16[4,256,128]{2,1,0:T(8,128)(2,1)S(1)} %get-tuple-element.49.v_ref), custom_call_target="tpu_custom_call" | custom-call | flops 2147483648 | bytes 2097152 | tf_op jit(solution)/shard_map/attend/pallas_call | solution.py:224
  102.7 10.8 %collective-permute-done.10 = bf16[128,2048]{1,0:T(8,128)(2,1)S(1)} collective-permute-done((bf16[128,2048]{1,0:T(8,128)(2,1)S(1)}, bf16[128,2048]{1,0:T(8,128)(2,1)S(1)}, u32[]{:S(2)}, u32[]{:S(2)}) %collective-permute-start.10) | collective-permute-done | bytes 524320 | tf_op jit(solution)/shard_map/ppermute | solution.py:28
  117.4 7.3 %collective-permute-done.14 = bf16[128,2048]{1,0:T(8,128)(2,1)S(1)} collective-permute-done((bf16[128,2048]{1,0:T(8,128)(2,1)S(1)}, bf16[128,2048]{1,0:T(8,128)(2,1)S(1)}, u32[]{:S(2)}, u32[]{:S(2)}) %collective-permute-start.14) | collective-permute-done | bytes 524320 | tf_op jit(solution)/shard_map/ppermute | solution.py:28
  126.2 8.1 %collective-permute-done.13 = bf16[128,2048]{1,0:T(8,128)(2,1)S(1)} collective-permute-done((bf16[128,2048]{1,0:T(8,128)(2,1)S(1)}, bf16[128,2048]{1,0:T(8,128)(2,1)S(1)}, u32[]{:S(2)}, u32[]{:S(2)}) %collective-permute-start.13) | collective-permute-done | bytes 524320 | tf_op jit(solution)/shard_map/ppermute | solution.py:28
  144.0 11.1 %collective-permute-done.18 = bf16[128,2048]{1,0:T(8,128)(2,1)} collective-permute-done((bf16[128,2048]{1,0:T(8,128)(2,1)}, bf16[128,2048]{1,0:T(8,128)(2,1)}, u32[]{:S(2)}, u32[]{:S(2)}) %collective-permute-start.18) | collective-permute-done | bytes 524320 | tf_op jit(solution)/shard_map/ppermute | solution.py:28
  158.4 8.5 %collective-permute-done.16 = bf16[128,2048]{1,0:T(8,128)(2,1)} collective-permute-done((bf16[128,2048]{1,0:T(8,128)(2,1)}, bf16[128,2048]{1,0:T(8,128)(2,1)}, u32[]{:S(2)}, u32[]{:S(2)}) %collective-permute-start.16) | collective-permute-done | bytes 524320 | tf_op jit(solution)/shard_map/ppermute | solution.py:28
  169.5 5.6 collective-permute-done.20
  182.2 9.3 %collective-permute-done.21 = bf16[128,2048]{1,0:T(8,128)(2,1)S(1)} collective-permute-done((bf16[128,2048]{1,0:T(8,128)(2,1)S(1)}, bf16[128,2048]{1,0:T(8,128)(2,1)S(1)}, u32[]{:S(2)}, u32[]{:S(2)}) %collective-permute-start.21) | collective-permute-done | bytes 524320 | tf_op jit(solution)/shard_map/ppermute | solution.py:28
  192.9 11.2 %collective-permute-done.24 = bf16[128,2048]{1,0:T(8,128)(2,1)S(1)} collective-permute-done((bf16[128,2048]{1,0:T(8,128)(2,1)S(1)}, bf16[128,2048]{1,0:T(8,128)(2,1)S(1)}, u32[]{:S(2)}, u32[]{:S(2)}) %collective-permute-start.24) | collective-permute-done | bytes 524320 | tf_op jit(solution)/shard_map/ppermute | solution.py:28
  214.2 17.3 %fusion.34 = f32[1024,2816]{1,0:T(8,128)S(1)} fusion(bf16[1024,2048]{1,0:T(8,128)(2,1)} %copy-done.52, bf16[2048,2816]{1,0:T(8,128)(2,1)} %all-gather.8.cloned.1.call-done), kind=kOutput, calls=%fused_computation.144 | convolution fusion | flops 11811160064 | bytes 27262976 | tf_op jit(solution)/shard_map/dot_general | solution.py:621
  235.7 11.7 %convolution_convert_fusion.1 = bf16[1408,2048]{1,0:T(8,128)(2,1)} fusion(bf16[1024,1408]{1,0:T(8,128)(2,1)S(1)} %multiply_convert_fusion, bf16[1024,2048]{1,0:T(8,128)(2,1)} %constant_dynamic-update-slice_fusion), kind=kOutput, calls=%fused_computation.1 | convolution fusion | flops 5908463616 | bytes 12845056 | tf_op jit(solution)/shard_map/tf,td->fd/dot_general | solution.py:601
  247.9 14.6 %fusion.2 = (bf16[1024,1408]{1,0:T(8,128)(2,1)S(1)}, bf16[1024,1408]{1,0:T(8,128)(2,1)S(1)}) fusion(f32[1024,2816]{1,0:T(8,128)} %copy-done.29, bf16[1024,2048]{1,0:T(8,128)(2,1)} %constant_dynamic-update-slice_fusion, bf16[1408,2048]{1,0:T(8,128)(2,1)} %all-gather.6.cloned.1.call-done), kind=kOutput, calls=%fused_computation.6 | convolution fusion | flops 5927206912 | bytes 27262976 | tf_op jit(solution)/shard_map/td,fd->tf/dot_general | solution.py:631
  262.6 15.0 %convolution_convert_fusion.2 = bf16[1024,2048]{1,0:T(8,128)(2,1)S(1)} fusion(bf16[2048,2816]{1,0:T(8,128)(2,1)} %all-gather.8.cloned.1.call-done, bf16[1024,1408]{1,0:T(8,128)(2,1)S(1)} %get-tuple-element.90, bf16[1024,1408]{1,0:T(8,128)(2,1)S(1)} %get-tuple-element.89), kind=kOutput, calls=%fused_computation.14 | convolution fusion | flops 11824791552 | bytes 21495808 | tf_op jit(solution)/shard_map/tf,df->td/dot_general | solution.py:637
  281.0 18.4 %convolution_convert_fusion = bf16[2048,2816]{1,0:T(8,128)(2,1)} fusion(bf16[1024,2048]{1,0:T(8,128)(2,1)} %copy-done.52, bf16[1024,1408]{1,0:T(8,128)(2,1)S(1)} %get-tuple-element.90, bf16[1024,1408]{1,0:T(8,128)(2,1)S(1)} %get-tuple-element.89), kind=kOutput, calls=%fused_computation | convolution fusion | flops 11828461568 | bytes 21495808 | tf_op jit(solution)/shard_map/tf,td->fd/dot_general | solution.py:601
  305.6 7.2 %collective-permute-done.32 = bf16[128,2048]{1,0:T(8,128)(2,1)S(1)} collective-permute-done((bf16[128,2048]{1,0:T(8,128)(2,1)}, bf16[128,2048]{1,0:T(8,128)(2,1)S(1)}, u32[]{:S(2)}, u32[]{:S(2)}) %collective-permute-start.32) | collective-permute-done | bytes 524320 | tf_op jit(solution)/shard_map/ppermute | solution.py:28
  327.8 6.9 %convolution_convert_fusion.5 = bf16[1024,2048]{1,0:T(8,128)(2,1)S(1)} fusion(bf16[1024,1408]{1,0:T(8,128)(2,1)S(1)} %copy-done.47, bf16[1408,2048]{1,0:T(8,128)(2,1)S(1)} %bitcast.66), kind=kOutput, calls=%fused_computation.17 | convolution fusion | flops 5907677184 | bytes 12845056 | tf_op jit(solution)/shard_map/dot_general | solution.py:643
  345.4 6.1 collective-permute-done.34
  373.1 27.2 %attend_back.1 = (bf16[4,256,512]{2,1,0:T(8,128)(2,1)S(1)}, bf16[4,256,128]{2,1,0:T(8,128)(2,1)S(1)}) custom-call(s32[1]{0:T(128)} %bitcast.1.place_ref, bf16[4,256,512]{2,1,0:T(8,128)(2,1)S(1)} %copy-done.19, bf16[4,256,128]{2,1,0:T(8,128)(2,1)S(1)} %copy-done.21, bf16[4,256,128]{2,1,0:T(8,128)(2,1)S(1)} %copy-done.23, bf16[4,256,512]{2,1,0:T(8,128)(2,1)S(1)} %copy-done.15, ...), custom_call_target="tpu_custom_call" | custom-call | flops 5368709120 | bytes 4194304 | tf_op jit(solution)/shard_map/attend_back/pallas_call | solution.py:348
  413.7 5.6 convolution_convert_fusion.4
  434.0 7.0 %collective-permute-done.46 = bf16[128,2048]{1,0:T(8,128)(2,1)S(1)} collective-permute-done((bf16[128,2048]{1,0:T(8,128)(2,1)S(1)}, bf16[128,2048]{1,0:T(8,128)(2,1)S(1)}, u32[]{:S(2)}, u32[]{:S(2)}) %collective-permute-start.46) | collective-permute-done | bytes 524320 | tf_op jit(solution)/shard_map/ppermute | solution.py:28
  443.4 8.8 %collective-permute-done.40 = bf16[128,2048]{1,0:T(8,128)(2,1)S(1)} collective-permute-done((bf16[128,2048]{1,0:T(8,128)(2,1)S(1)}, bf16[128,2048]{1,0:T(8,128)(2,1)S(1)}, u32[]{:S(2)}, u32[]{:S(2)}) %collective-permute-start.40) | collective-permute-done | bytes 524320 | tf_op jit(solution)/shard_map/ppermute | solution.py:28
  454.5 13.0 %collective-permute-done.71 = bf16[88,2048]{1,0:T(8,128)(2,1)S(1)} collective-permute-done((bf16[88,2048]{1,0:T(8,128)(2,1)S(1)}, bf16[88,2048]{1,0:T(8,128)(2,1)S(1)}, u32[]{:S(2)}, u32[]{:S(2)}) %collective-permute-start.71) | collective-permute-done | bytes 360480 | tf_op jit(solution)/shard_map/ppermute | solution.py:28
  474.9 7.5 %collective-permute-done.49 = bf16[128,2048]{1,0:T(8,128)(2,1)S(1)} collective-permute-done((bf16[128,2048]{1,0:T(8,128)(2,1)S(1)}, bf16[128,2048]{1,0:T(8,128)(2,1)S(1)}, u32[]{:S(2)}, u32[]{:S(2)}) %collective-permute-start.49) | collective-permute-done | bytes 524320 | tf_op jit(solution)/shard_map/ppermute | solution.py:28
  494.5 8.1 %collective-permute-done.41 = bf16[128,2048]{1,0:T(8,128)(2,1)} collective-permute-done((bf16[128,2048]{1,0:T(8,128)(2,1)S(1)}, bf16[128,2048]{1,0:T(8,128)(2,1)}, u32[]{:S(2)}, u32[]{:S(2)}) %collective-permute-start.41) | collective-permute-done | bytes 524320 | tf_op jit(solution)/shard_map/ppermute | solution.py:28
  512.3 69.2 %reduce-scatter.8.cloned.1.call-done.refs_0_ = bf16[256,2816]{1,0:T(8,128)(2,1)} async-done(((bf16[2048,2816]{1,0:T(8,128)(2,1)}), bf16[256,2816]{1,0:T(8,128)(2,1)}) %reduce-scatter.8.cloned.1.call-update) | async-done | bytes 1441808 | tf_op jit(solution)/shard_map/reduce_scatter | solution.py:604
  595.1 9.7 %collective-permute-done.63 = bf16[128,2816]{1,0:T(8,128)(2,1)} collective-permute-done((bf16[128,2816]{1,0:T(8,128)(2,1)}, bf16[128,2816]{1,0:T(8,128)(2,1)}, u32[]{:S(2)}, u32[]{:S(2)}) %collective-permute-start.63) | collective-permute-done | bytes 720928 | tf_op jit(solution)/shard_map/ppermute | solution.py:28
  605.4 13.4 %collective-permute-done.60 = bf16[128,2816]{1,0:T(8,128)(2,1)} collective-permute-done((bf16[128,2816]{1,0:T(8,128)(2,1)}, bf16[128,2816]{1,0:T(8,128)(2,1)}, u32[]{:S(2)}, u32[]{:S(2)}) %collective-permute-start.60) | collective-permute-done | bytes 720928 | tf_op jit(solution)/shard_map/ppermute | solution.py:28
  623.5 7.4 %collective-permute-done.65 = bf16[128,2816]{1,0:T(8,128)(2,1)S(1)} collective-permute-done((bf16[128,2816]{1,0:T(8,128)(2,1)}, bf16[128,2816]{1,0:T(8,128)(2,1)S(1)}, u32[]{:S(2)}, u32[]{:S(2)}) %collective-permute-start.65) | collective-permute-done | bytes 720928 | tf_op jit(solution)/shard_map/ppermute | solution.py:28
  632.1 12.6 %put_columns.1 = (f32[256,5632]{1,0:T(8,128)}, f32[256,5632]{1,0:T(8,128)}, f32[256,1]{1,0:T(8,128)S(1)}) custom-call(s32[1]{0:T(128)} %bitcast.1.place_ref, bf16[256,2816]{1,0:T(8,128)(2,1)S(1)} %copy-done.7, bf16[256,2816]{1,0:T(8,128)(2,1)S(1)} %pad_maximum_fusion.4.refs_1_, bf16[256,2816]{1,0:T(8,128)(2,1)S(1)} %pad_maximum_fusion.5.refs_2_, ...), custom_call_target="tpu_custom_call" | custom-call | bytes 23068672 | tf_op jit(solution)/shard_map/put_columns/pallas_call | solution.py:457
  (372 shorter events, 233.0 us)
Async XLA Ops:
  7.2 57.8 %all-gather.4.cloned.1.call-start = ((), (), s32[]{:S(2)}) async-start(), calls=%async_computation.3 | async-start | bytes 5308416 | tf_op jit(solution)/shard_map/all_gather | solution.py:553
  10.5 203.7 %all-gather.8.cloned.1.call-start = ((), (), s32[]{:S(2)}) async-start(), calls=%async_computation.5 | async-start | bytes 12976128 | tf_op jit(solution)/shard_map/all_gather | solution.py:553
  16.0 231.9 %all-gather.6.cloned.1.call-start = ((), (), s32[]{:S(2)}) async-start(), calls=%async_computation.4 | async-start | bytes 6488064 | tf_op jit(solution)/shard_map/all_gather | solution.py:553
  18.3 28.3 %collective-permute-start = (bf16[128,2048]{1,0:T(8,128)(2,1)}, bf16[128,2048]{1,0:T(8,128)(2,1)}, u32[]{:S(2)}, u32[]{:S(2)}) collective-permute-start(bf16[128,2048]{1,0:T(8,128)(2,1)} %get-tuple-element.131), channel_id=1, source_target_pairs={{0,8},{8,0},{16,24},{24,16},{1,9},{9,1},{17,25},{25,17},{2,10},{10... | collective-permute-start | bytes 1572872 | tf_op jit(solution)/shard_map/ppermute | solution.py:28
  21.3 29.9 %collective-permute-start.2 = (bf16[128,2048]{1,0:T(8,128)(2,1)}, bf16[128,2048]{1,0:T(8,128)(2,1)}, u32[]{:S(2)}, u32[]{:S(2)}) collective-permute-start(bf16[128,2048]{1,0:T(8,128)(2,1)} %get-tuple-element.131), channel_id=1, source_target_pairs={{0,16},{8,24},{16,0},{24,8},{1,17},{9,25},{17,1},{25,9},{2,18},{10... | collective-permute-start | bytes 1572872 | tf_op jit(solution)/shard_map/ppermute | solution.py:28
  23.4 30.2 %collective-permute-start.1 = (bf16[128,2048]{1,0:T(8,128)(2,1)}, bf16[128,2048]{1,0:T(8,128)(2,1)}, u32[]{:S(2)}, u32[]{:S(2)}) collective-permute-start(bf16[128,2048]{1,0:T(8,128)(2,1)} %get-tuple-element.132), channel_id=1, source_target_pairs={{0,8},{8,0},{16,24},{24,16},{1,9},{9,1},{17,25},{25,17},{2,10},{10... | collective-permute-start | bytes 1572872 | tf_op jit(solution)/shard_map/ppermute | solution.py:28
  68.1 27.7 %collective-permute-start.6 = (bf16[512,512]{1,0:T(8,128)(2,1)S(1)}, bf16[512,512]{1,0:T(8,128)(2,1)S(1)}, u32[]{:S(2)}, u32[]{:S(2)}) collective-permute-start(bf16[512,512]{1,0:T(8,128)(2,1)S(1)} %get-tuple-element.119), channel_id=1, source_target_pairs={{0,8},{8,0},{16,24},{24,16},{1,9},{9,1},{17,25},{25,17},{2,10},{10... | collective-permute-start | bytes 1572872 | tf_op jit(solution)/shard_map/ppermute | solution.py:28
  70.2 25.6 %collective-permute-start.7 = (bf16[512,512]{1,0:T(8,128)(2,1)S(1)}, bf16[512,512]{1,0:T(8,128)(2,1)S(1)}, u32[]{:S(2)}, u32[]{:S(2)}) collective-permute-start(bf16[512,512]{1,0:T(8,128)(2,1)S(1)} %get-tuple-element.118), channel_id=1, source_target_pairs={{0,16},{8,24},{16,0},{24,8},{1,17},{9,25},{17,1},{25,9},{2,18},{10... | collective-permute-start | bytes 1572872 | tf_op jit(solution)/shard_map/ppermute | solution.py:28
  141.9 24.9 %collective-permute-start.16 = (bf16[128,2048]{1,0:T(8,128)(2,1)}, bf16[128,2048]{1,0:T(8,128)(2,1)}, u32[]{:S(2)}, u32[]{:S(2)}) collective-permute-start(bf16[128,2048]{1,0:T(8,128)(2,1)} %get-tuple-element.130), channel_id=1, source_target_pairs={{0,8},{8,0},{16,24},{24,16},{1,9},{9,1},{17,25},{25,17},{2,10},{10... | collective-permute-start | bytes 1572872 | tf_op jit(solution)/shard_map/ppermute | solution.py:28
  142.5 25.8 %collective-permute-start.17 = (bf16[128,2048]{1,0:T(8,128)(2,1)}, bf16[128,2048]{1,0:T(8,128)(2,1)}, u32[]{:S(2)}, u32[]{:S(2)}) collective-permute-start(bf16[128,2048]{1,0:T(8,128)(2,1)} %get-tuple-element.129), channel_id=1, source_target_pairs={{0,16},{8,24},{16,0},{24,8},{1,17},{9,25},{17,1},{25,9},{2,18},{10... | collective-permute-start | bytes 1572872 | tf_op jit(solution)/shard_map/ppermute | solution.py:28
  158.1 200.8 %reduce-scatter.4.cloned.1.call-start = ((), (), s32[]{:S(2)}) async-start(), calls=%async_computation.6 | async-start | bytes 6488064 | tf_op jit(solution)/shard_map/reduce_scatter | solution.py:604
  178.1 28.3 %collective-permute-start.23 = (bf16[128,2048]{1,0:T(8,128)(2,1)S(1)}, bf16[128,2048]{1,0:T(8,128)(2,1)S(1)}, u32[]{:S(2)}, u32[]{:S(2)}) collective-permute-start(bf16[128,2048]{1,0:T(8,128)(2,1)S(1)} %get-tuple-element.128), channel_id=1, source_target_pairs={{0,16},{8,24},{16,0},{24,8},{1,17},{9,25},{17,1},{25,9},{2,18},{10... | collective-permute-start | bytes 1572872 | tf_op jit(solution)/shard_map/ppermute | solution.py:28
  179.5 26.0 %collective-permute-start.22 = (bf16[128,2048]{1,0:T(8,128)(2,1)S(1)}, bf16[128,2048]{1,0:T(8,128)(2,1)S(1)}, u32[]{:S(2)}, u32[]{:S(2)}) collective-permute-start(bf16[128,2048]{1,0:T(8,128)(2,1)S(1)} %get-tuple-element.127), channel_id=1, source_target_pairs={{0,8},{8,0},{16,24},{24,16},{1,9},{9,1},{17,25},{25,17},{2,10},{10... | collective-permute-start | bytes 1572872 | tf_op jit(solution)/shard_map/ppermute | solution.py:28
  247.4 238.4 %reduce-scatter.6.cloned.1.call-start = ((), (), s32[]{:S(2)}) async-start(), calls=%async_computation.7 | async-start | bytes 5308416 | tf_op jit(solution)/shard_map/reduce_scatter | solution.py:604
  369.6 30.9 %collective-permute-start.51 = (bf16[512,512]{1,0:T(8,128)(2,1)S(1)}, bf16[512,512]{1,0:T(8,128)(2,1)S(1)}, u32[]{:S(2)}, u32[]{:S(2)}) collective-permute-start(bf16[512,512]{1,0:T(8,128)(2,1)S(1)} %get-tuple-element.115), channel_id=1, source_target_pairs={{0,8},{8,0},{16,24},{24,16},{1,9},{9,1},{17,25},{25,17},{2,10},{10... | collective-permute-start | bytes 1572872 | tf_op jit(solution)/shard_map/ppermute | solution.py:28
  370.8 30.5 %collective-permute-start.52 = (bf16[512,512]{1,0:T(8,128)(2,1)S(1)}, bf16[512,512]{1,0:T(8,128)(2,1)S(1)}, u32[]{:S(2)}, u32[]{:S(2)}) collective-permute-start(bf16[512,512]{1,0:T(8,128)(2,1)S(1)} %get-tuple-element.114), channel_id=1, source_target_pairs={{0,16},{8,24},{16,0},{24,8},{1,17},{9,25},{17,1},{25,9},{2,18},{10... | collective-permute-start | bytes 1572872 | tf_op jit(solution)/shard_map/ppermute | solution.py:28
  371.4 30.7 %collective-permute-start.53 = (bf16[512,512]{1,0:T(8,128)(2,1)S(1)}, bf16[512,512]{1,0:T(8,128)(2,1)S(1)}, u32[]{:S(2)}, u32[]{:S(2)}) collective-permute-start(bf16[512,512]{1,0:T(8,128)(2,1)S(1)} %get-tuple-element.113), channel_id=1, source_target_pairs={{0,24},{8,16},{16,8},{24,0},{1,25},{9,17},{17,9},{25,1},{2,26},{10... | collective-permute-start | bytes 1572872 | tf_op jit(solution)/shard_map/ppermute | solution.py:28
  408.4 173.0 %reduce-scatter.8.cloned.1.call-start = ((), (), s32[]{:S(2)}) async-start(), calls=%async_computation.8 | async-start | bytes 12976128 | tf_op jit(solution)/shard_map/reduce_scatter | solution.py:604
  427.9 24.3 %collective-permute-start.40 = (bf16[128,2048]{1,0:T(8,128)(2,1)S(1)}, bf16[128,2048]{1,0:T(8,128)(2,1)S(1)}, u32[]{:S(2)}, u32[]{:S(2)}) collective-permute-start(bf16[128,2048]{1,0:T(8,128)(2,1)S(1)} %get-tuple-element.124), channel_id=1, source_target_pairs={{0,16},{8,24},{16,0},{24,8},{1,17},{9,25},{17,1},{25,9},{2,18},{10... | collective-permute-start | bytes 1572872 | tf_op jit(solution)/shard_map/ppermute | solution.py:28
  431.2 41.6 %collective-permute-start.50 = (bf16[128,2048]{1,0:T(8,128)(2,1)S(1)}, bf16[128,2048]{1,0:T(8,128)(2,1)S(1)}, u32[]{:S(2)}, u32[]{:S(2)}) collective-permute-start(bf16[128,2048]{1,0:T(8,128)(2,1)S(1)} %get-tuple-element.92), channel_id=1, source_target_pairs={{0,16},{8,24},{16,0},{24,8},{1,17},{9,25},{17,1},{25,9},{2,18},{10... | collective-permute-start | bytes 1572872 | tf_op jit(solution)/shard_map/ppermute | solution.py:28
  441.0 33.9 %collective-permute-start.45 = (bf16[128,2048]{1,0:T(8,128)(2,1)S(1)}, bf16[128,2048]{1,0:T(8,128)(2,1)S(1)}, u32[]{:S(2)}, u32[]{:S(2)}) collective-permute-start(bf16[128,2048]{1,0:T(8,128)(2,1)S(1)} %get-tuple-element.91), channel_id=1, source_target_pairs={{0,8},{8,0},{16,24},{24,16},{1,9},{9,1},{17,25},{25,17},{2,10},{10... | collective-permute-start | bytes 1572872 | tf_op jit(solution)/shard_map/ppermute | solution.py:28
  441.4 26.1 %collective-permute-start.71 = (bf16[88,2048]{1,0:T(8,128)(2,1)S(1)}, bf16[88,2048]{1,0:T(8,128)(2,1)S(1)}, u32[]{:S(2)}, u32[]{:S(2)}) collective-permute-start(bf16[88,2048]{1,0:T(8,128)(2,1)S(1)} %collective-permute-done.69), channel_id=1, source_target_pairs={{0,8},{8,0},{16,24},{24,16},{1,9},{9,1},{17,25},{25,17},{2,10},{10... | collective-permute-start | bytes 1081352 | tf_op jit(solution)/shard_map/ppermute | solution.py:28
  452.4 30.0 %collective-permute-start.49 = (bf16[128,2048]{1,0:T(8,128)(2,1)S(1)}, bf16[128,2048]{1,0:T(8,128)(2,1)S(1)}, u32[]{:S(2)}, u32[]{:S(2)}) collective-permute-start(bf16[128,2048]{1,0:T(8,128)(2,1)S(1)} %get-tuple-element.96), channel_id=1, source_target_pairs={{0,16},{8,24},{16,0},{24,8},{1,17},{9,25},{17,1},{25,9},{2,18},{10... | collective-permute-start | bytes 1572872 | tf_op jit(solution)/shard_map/ppermute | solution.py:28
  474.9 27.8 %collective-permute-start.41 = (bf16[128,2048]{1,0:T(8,128)(2,1)S(1)}, bf16[128,2048]{1,0:T(8,128)(2,1)}, u32[]{:S(2)}, u32[]{:S(2)}) collective-permute-start(bf16[128,2048]{1,0:T(8,128)(2,1)S(1)} %add_convert_fusion.4), channel_id=1, source_target_pairs={{0,8},{8,0},{16,24},{24,16},{1,9},{9,1},{17,25},{25,17},{2,10},{10... | collective-permute-start | bytes 1572872 | tf_op jit(solution)/shard_map/ppermute | solution.py:28
  507.3 78.2 %collective-permute-start.55 = (bf16[128,1152]{1,0:T(8,128)(2,1)}, bf16[128,1152]{1,0:T(8,128)(2,1)S(1)}, u32[]{:S(2)}, u32[]{:S(2)}) collective-permute-start(bf16[128,1152]{1,0:T(8,128)(2,1)} %get-tuple-element.136), channel_id=1, source_target_pairs={{0,8},{8,0},{16,24},{24,16},{1,9},{9,1},{17,25},{25,17},{2,10},{10... | collective-permute-start | bytes 884744 | tf_op jit(solution)/shard_map/ppermute | solution.py:28
  508.3 78.7 %collective-permute-start.56 = (bf16[128,1152]{1,0:T(8,128)(2,1)}, bf16[128,1152]{1,0:T(8,128)(2,1)S(1)}, u32[]{:S(2)}, u32[]{:S(2)}) collective-permute-start(bf16[128,1152]{1,0:T(8,128)(2,1)} %get-tuple-element.135), channel_id=1, source_target_pairs={{0,16},{8,24},{16,0},{24,8},{1,17},{9,25},{17,1},{25,9},{2,18},{10... | collective-permute-start | bytes 884744 | tf_op jit(solution)/shard_map/ppermute | solution.py:28
  510.0 78.5 %collective-permute-start.59 = (bf16[128,1152]{1,0:T(8,128)(2,1)}, bf16[128,1152]{1,0:T(8,128)(2,1)S(1)}, u32[]{:S(2)}, u32[]{:S(2)}) collective-permute-start(bf16[128,1152]{1,0:T(8,128)(2,1)} %collective-permute-done.57), channel_id=1, source_target_pairs={{0,8},{8,0},{16,24},{24,16},{1,9},{9,1},{17,25},{25,17},{2,10},{10... | collective-permute-start | bytes 884744 | tf_op jit(solution)/shard_map/ppermute | solution.py:28
  510.9 79.3 %collective-permute-start.58 = (bf16[128,1152]{1,0:T(8,128)(2,1)}, bf16[128,1152]{1,0:T(8,128)(2,1)S(1)}, u32[]{:S(2)}, u32[]{:S(2)}) collective-permute-start(bf16[128,1152]{1,0:T(8,128)(2,1)} %collective-permute-done.54), channel_id=1, source_target_pairs={{0,16},{8,24},{16,0},{24,8},{1,17},{9,25},{17,1},{25,9},{2,18},{10... | collective-permute-start | bytes 884744 | tf_op jit(solution)/shard_map/ppermute | solution.py:28
  584.0 36.3 %collective-permute-start.61 = (bf16[128,2816]{1,0:T(8,128)(2,1)}, bf16[128,2816]{1,0:T(8,128)(2,1)}, u32[]{:S(2)}, u32[]{:S(2)}) collective-permute-start(bf16[128,2816]{1,0:T(8,128)(2,1)} %get-tuple-element.122), channel_id=1, source_target_pairs={{0,8},{8,0},{16,24},{24,16},{1,9},{9,1},{17,25},{25,17},{2,10},{10... | collective-permute-start | bytes 2162696 | tf_op jit(solution)/shard_map/ppermute | solution.py:28
  586.9 31.9 %collective-permute-start.60 = (bf16[128,2816]{1,0:T(8,128)(2,1)}, bf16[128,2816]{1,0:T(8,128)(2,1)}, u32[]{:S(2)}, u32[]{:S(2)}) collective-permute-start(bf16[128,2816]{1,0:T(8,128)(2,1)} %get-tuple-element.121), channel_id=1, source_target_pairs={{0,8},{8,0},{16,24},{24,16},{1,9},{9,1},{17,25},{25,17},{2,10},{10... | collective-permute-start | bytes 2162696 | tf_op jit(solution)/shard_map/ppermute | solution.py:28
  588.5 33.4 %collective-permute-start.62 = (bf16[128,2816]{1,0:T(8,128)(2,1)}, bf16[128,2816]{1,0:T(8,128)(2,1)}, u32[]{:S(2)}, u32[]{:S(2)}) collective-permute-start(bf16[128,2816]{1,0:T(8,128)(2,1)} %get-tuple-element.121), channel_id=1, source_target_pairs={{0,16},{8,24},{16,0},{24,8},{1,17},{9,25},{17,1},{25,9},{2,18},{10... | collective-permute-start | bytes 2162696 | tf_op jit(solution)/shard_map/ppermute | solution.py:28
  604.8 26.0 %collective-permute-start.65 = (bf16[128,2816]{1,0:T(8,128)(2,1)}, bf16[128,2816]{1,0:T(8,128)(2,1)S(1)}, u32[]{:S(2)}, u32[]{:S(2)}) collective-permute-start(bf16[128,2816]{1,0:T(8,128)(2,1)} %collective-permute-done.63), channel_id=1, source_target_pairs={{0,8},{8,0},{16,24},{24,16},{1,9},{9,1},{17,25},{25,17},{2,10},{10... | collective-permute-start | bytes 2162696 | tf_op jit(solution)/shard_map/ppermute | solution.py:28
  (109 other events, 1726.1 us)
Sparse Core Ops, SparseCore 0:
  10.6 54.4 all-gather.3
  67.3 106.8 all-gather.7
  175.8 58.7 all-gather.5
  247.6 62.7 reduce-scatter.3
  408.5 53.0 reduce-scatter.5
  463.7 117.6 reduce-scatter.7

commit v3 on v2

--- a/solution.py
+++ b/solution.py
@@ -28,7 +28,11 @@
     return lax.ppermute(value, "seq", [(i, i ^ bit) for i in range(count)])
 
 
-def gather_seq(block):
+def tie(first, second):
+    return lax.optimization_barrier((first, second))
+
+
+def gather_seq(block, filler=None):
     count = lax.axis_size("seq")
     blocks = [block]
     if count == 2:
@@ -38,6 +42,8 @@
         upper, lower = block[:half], block[half:]
         near_upper, other_lower = hop(upper, 1), hop(lower, 2)
         near_lower, other_upper = hop(lower, 1), hop(upper, 2)
+        if filler is not None:
+            (near_upper, other_lower), filler = tie((near_upper, other_lower), filler)
         far_upper, far_lower = hop(near_upper, 2), hop(other_lower, 1)
         blocks.append(jnp.concatenate([near_upper, near_lower], axis=0))
         blocks.append(jnp.concatenate([other_upper, other_lower], axis=0))
@@ -46,40 +52,55 @@
     while bit < count:
         blocks += [hop(one, bit) for one in blocks]
         bit *= 2
-    return blocks
+    return blocks if filler is None else (blocks, filler)
+
+
+def gather_direct(block):
+    return [block] + [hop(block, r) for r in range(1, lax.axis_size("seq"))]
 
 
 def add_low(first, second):
     return (first.astype(f32) + second.astype(f32)).astype(bf16)
 
 
-def tie(first, second):
-    return lax.optimization_barrier((first, second))
-
-
-def scatter_seq(parts, filler=None):
+def scatter_start(parts):
     count = lax.axis_size("seq")
     bit = count // 2
     while bit >= 4:
         there = [hop(parts[bit + r], bit) for r in range(bit)]
         parts = [add_low(parts[r], there[r]) for r in range(bit)]
         bit //= 2
-    total = parts[0].astype(f32)
-    if count >= 4:
-        half = parts[3].shape[0] // 2
-        upper = hop(parts[3][:half], 1)
-        lower = hop(parts[3][half:], 2)
-        kept_x = hop(parts[1][:half], 1)
-        kept_y = hop(parts[2][half:], 2)
-        if filler is not None:
-            (upper, lower), filler = tie((upper, lower), filler)
-        sent_y = hop(add_low(parts[2][:half], upper), 2)
-        sent_x = hop(add_low(parts[1][half:], lower), 1)
-        total = total + jnp.concatenate([kept_x, sent_x], axis=0).astype(f32)
-        total = total + jnp.concatenate([sent_y, kept_y], axis=0).astype(f32)
-    elif count == 2:
-        total = total + hop(parts[1], 1).astype(f32)
-    return total if filler is None else (total, filler)
+    if count < 4:
+        return parts, (), tuple(hop(one, 1) for one in parts[1:])
+    half = parts[3].shape[0] // 2
+    turning = (hop(parts[3][:half], 1), hop(parts[3][half:], 2))
+    straight = (hop(parts[1][:half], 1), hop(parts[2][half:], 2))
+    return parts, turning, straight
+
+
+def scatter_turn(state):
+    parts, turning, straight = state
+    if not turning:
+        return parts[0], (), straight
+    half = parts[3].shape[0] // 2
+    sent_y = hop(add_low(parts[2][:half], turning[0]), 2)
+    sent_x = hop(add_low(parts[1][half:], turning[1]), 1)
+    return parts[0], (sent_x, sent_y), straight
+
+
+def scatter_end(state):
+    kept, sent, straight = state
+    total = kept.astype(f32)
+    if not sent:
+        for one in straight:
+            total = total + one.astype(f32)
+        return total
+    total = total + jnp.concatenate([straight[0], sent[0]], axis=0).astype(f32)
+    return total + jnp.concatenate([sent[1], straight[1]], axis=0).astype(f32)
+
+
+def scatter_seq(parts):
+    return scatter_end(scatter_turn(scatter_start(parts)))
 
 
 def rms_scale(values):
@@ -130,7 +151,7 @@
         in_specs=[
             row_block(width),
             whole((1, width)),
-            whole(weights.shape),
+            whole((width, width_q + PAIR)),
             row_block(PAIR),
             row_block(PAIR),
         ],
@@ -445,29 +466,30 @@
             out[:, here] = joined
             term = jnp.sum(joined * weight[:, here].astype(f32), axis=1, keepdims=True)
             total = term if total is None else total + term
-    gain_out[...] = total / gain_ref[...].astype(f32)
+    gain_out[...] = jnp.broadcast_to(total, (total.shape[0], 128)).T[:1] / gain_ref[...].astype(f32)
 
 
 def put_columns(place, blocks, w_gate, w_up, gain, shards):
     count = len(blocks)
     rows, ff = w_gate.shape
     piece = ff // (shards * count)
-    step = min(rows, 64)
+    step = min(rows, 128)
     block = lambda last: pl.BlockSpec((step, last), lambda i, at: (i, 0))
+    flat = pl.BlockSpec((1, step), lambda i, at: (0, i))
     return pl.pallas_call(
         functools.partial(put_columns_kernel, shards, count, piece),
         grid_spec=pltpu.PrefetchScalarGridSpec(
             num_scalar_prefetch=1,
             grid=(rows // step,),
-            in_specs=[block(blocks[0].shape[1])] * count + [block(ff), block(ff), block(1)],
-            out_specs=[block(ff), block(ff), block(1)],
+            in_specs=[block(blocks[0].shape[1])] * count + [block(ff), block(ff), flat],
+            out_specs=[block(ff), block(ff), flat],
         ),
         out_shape=[
             jax.ShapeDtypeStruct((rows, ff), f32),
             jax.ShapeDtypeStruct((rows, ff), f32),
-            jax.ShapeDtypeStruct((rows, 1), f32),
+            jax.ShapeDtypeStruct((1, rows), f32),
         ],
-        compiler_params=pltpu.CompilerParams(vmem_limit_bytes=40 * 2**20),
+        compiler_params=pltpu.CompilerParams(vmem_limit_bytes=58 * 2**20),
         cost_estimate=pl.CostEstimate(
             flops=0, bytes_accessed=16 * rows * ff, transcendentals=0
         ),
@@ -498,28 +520,30 @@
     for weight, out in ((q_w, q_ref), (k_w, k_ref), (v_w, v_ref)):
         term = jnp.sum(out[...] * weight[...].astype(f32), axis=1, keepdims=True)
         total = term if total is None else total + term
-    gain_out[...] = total / gain_ref[...].astype(f32)
+    gain_out[...] = jnp.broadcast_to(total, (total.shape[0], 128)).T[:1] / gain_ref[...].astype(f32)
 
 
 def put_attention(place, blocks, w_query, w_key, w_value, gain, width, copies):
     count = len(blocks)
     rows, wide_q = w_query.shape
     wide_k = w_key.shape[1]
-    step = min(rows, 64)
+    step = min(rows, 128)
     block = lambda last: pl.BlockSpec((step, last), lambda i, at: (i, 0))
+    flat = pl.BlockSpec((1, step), lambda i, at: (0, i))
     return pl.pallas_call(
         functools.partial(put_attention_kernel, count, copies, wide_q // count),
         grid_spec=pltpu.PrefetchScalarGridSpec(
             num_scalar_prefetch=1,
             grid=(rows // step,),
             in_specs=[block(blocks[0].shape[1])] * count
-            + [block(wide_q), block(wide_k), block(wide_k), block(1)],
-            out_specs=[block(wide_q), block(wide_k), block(wide_k), block(width), block(1)],
+            + [block(wide_q), block(wide_k), block(wide_k), flat],
+            out_specs=[block(wide_q), block(wide_k), block(wide_k), block(width), flat],
         ),
         out_shape=[
-            jax.ShapeDtypeStruct((rows, last), f32) for last in (wide_q, wide_k, wide_k, width, 1)
-        ],
-        compiler_params=pltpu.CompilerParams(vmem_limit_bytes=40 * 2**20),
+            jax.ShapeDtypeStruct((rows, last), f32) for last in (wide_q, wide_k, wide_k, width)
+        ]
+        + [jax.ShapeDtypeStruct((1, rows), f32)],
+        compiler_params=pltpu.CompilerParams(vmem_limit_bytes=58 * 2**20),
         cost_estimate=pl.CostEstimate(
             flops=0, bytes_accessed=16 * rows * wide_q, transcendentals=0
         ),
@@ -568,17 +592,10 @@
             axis=1,
         )
     )
-    w_qkv, w_o_columns = w_attn[:, :width_qkv], w_attn[:, width_qkv:]
-    w_gu = from_shards(take_columns(place_arg, w_gate, w_up, shards, count))
+    input_blocks, (gate_in, up_in) = gather_seq(mine, (w_gate, w_up))
+    w_gu = from_shards(take_columns(place_arg, gate_in, up_in, shards, count))
     w_dn = from_shards(lax.dynamic_slice_in_dim(w_down, place * piece, piece, axis=0))
-
-    inputs = jnp.stack(gather_seq(mine))
-
-    w_o = jnp.zeros((width_q, width), bf16)
-    for r in range(count):
-        rows_r = lax.dynamic_slice_in_dim(w_o_columns, (place ^ r) * width_q, width_q, axis=0)
-        rows_r = hop(rows_r, r) if r else rows_r
-        w_o = lax.dynamic_update_slice_in_dim(w_o, rows_r, (place ^ r) * part_d, axis=1)
+    inputs = jnp.stack(input_blocks)
 
     blocks_at = place ^ jnp.arange(count)
     positions = (blocks_at[:, None] * rows + jnp.arange(rows)[None, :]).astype(f32)
@@ -589,7 +606,16 @@
     cosine = jnp.cos(angles)
     sine = jnp.sin(angles) * jnp.where(lanes % HEAD_DIM < half_dim, -1.0, 1.0)
 
-    normed, queries, keys, values = project(inputs, gain_first, w_qkv, cosine, sine, width_q)
+    normed, queries, keys, values = project(inputs, gain_first, w_attn, cosine, sine, width_q)
+    w_attn, queries = tie(w_attn, queries)
+    w_qkv, w_o_columns = w_attn[:, :width_qkv], w_attn[:, width_qkv:]
+
+    w_o = jnp.zeros((width_q, width), bf16)
+    for r in range(count):
+        rows_r = lax.dynamic_slice_in_dim(w_o_columns, (place ^ r) * width_q, width_q, axis=0)
+        rows_r = hop(rows_r, r) if r else rows_r
+        w_o = lax.dynamic_update_slice_in_dim(w_o, rows_r, (place ^ r) * part_d, axis=1)
+
     attended, logsum = attend(place_arg, queries, keys, values)
     attended_rows = attended.reshape(length, width_q)
 
@@ -616,9 +642,10 @@
     normed_blocks = gather_seq((middle * scale_mid * gain_second).astype(bf16))
     normed_blocks, cot = tie(normed_blocks, cotangent[0])
     normed_mlp = jnp.concatenate(normed_blocks)
-    back_mlp = jnp.concatenate(gather_seq(cot))
-
     gate_up = jnp.dot(normed_mlp, w_gu, preferred_element_type=f32)
+    back_blocks, gate_up = gather_seq(cot, gate_up)
+    back_mlp = jnp.concatenate(back_blocks)
+
     gate_lin, upward = gate_up[:, :width_f], gate_up[:, width_f:]
     sigmoid_gate = jax.nn.sigmoid(gate_lin)
     silu_gate = gate_lin * sigmoid_gate
@@ -627,6 +654,9 @@
     own_down = to_owners(down_part)
 
     w_dn, down_part = tie(w_dn, down_part)
+    out_parts = split(jnp.dot(hidden, w_dn, preferred_element_type=f32))
+    w_dn, out_parts = tie(w_dn, out_parts)
+    kept, turning, straight = scatter_start(out_parts)
     back_hidden = (
         jnp.einsum("td,fd->tf", back_mlp, w_dn, preferred_element_type=f32).astype(bf16).astype(f32)
     )
@@ -634,48 +664,62 @@
     back_up = back_hidden * silu_gate
     back_gu = jnp.concatenate([back_gate.astype(bf16), back_up.astype(bf16)], axis=1)
 
+    turning, back_gu = tie(turning, back_gu)
+    kept, sent, straight = scatter_turn((kept, turning, straight))
+
     parts = split(jnp.einsum("tf,df->td", back_gu, w_gu, preferred_element_type=f32))
-    back_normed_mlp, gu_part = scatter_seq(parts, token_sum(normed_mlp, back_gu))
+    parts, (sent, straight) = tie(parts, (sent, straight))
+    output = (middle + scatter_end((kept, sent, straight))).astype(bf16)[None]
+    parts, turning, straight = scatter_start(parts)
+    gu_part = token_sum(normed_mlp, back_gu)
+    (turning, straight), gu_part = tie((turning, straight), gu_part)
+    back_normed_mlp = scatter_end(scatter_turn((parts, turning, straight)))
     own_gu = to_owners(gu_part)
 
     back_middle = cot.astype(f32) + norm_back(middle, scale_mid, gain_second, back_normed_mlp)
     back_blocks = gather_seq(back_middle.astype(bf16))
-    out_parts = split(jnp.dot(hidden, w_dn, preferred_element_type=f32))
-    back_blocks, (out_parts, own_down) = tie(back_blocks, (out_parts, own_down))
+    back_blocks, own_down = tie(back_blocks, own_down)
     back_branch = jnp.concatenate(back_blocks)
-    output = (middle + scatter_seq(out_parts)).astype(bf16)[None]
 
     back_attended = jnp.einsum("td,qd->tq", back_branch, w_o, preferred_element_type=f32)
     back_attended = back_attended.astype(bf16).reshape(count, rows, width_q)
     out_part = token_sum(attended_rows, back_branch)
-    back_attended, out_part = tie(back_attended, out_part)
+    out_blocks = []
+    for r in range(count):
+        part_r = lax.dynamic_slice_in_dim(out_part, (place ^ r) * part_d, part_d, axis=1)
+        out_blocks.append(hop(part_r, r) if r else part_r)
+    down_blocks = gather_direct(own_down)
     back_query, back_kv = attend_back(
         place_arg, queries, keys, values, attended, back_attended, logsum, cosine, sine
     )
+    back_query, (out_blocks, down_blocks) = tie(back_query, (out_blocks, down_blocks))
     back_qkv = jnp.concatenate([back_query, back_kv], axis=2).reshape(length, -1)
 
-    attn_part = jnp.zeros((width, width_qkv + part_d), bf16)
+    attn_part = jnp.pad(
+        token_sum(normed.reshape(length, width), back_qkv), ((0, 0), (0, part_d))
+    )
     for r in range(count):
-        part_r = lax.dynamic_slice_in_dim(out_part, (place ^ r) * part_d, part_d, axis=1)
-        part_r = hop(part_r, r) if r else part_r
-        attn_part = lax.dynamic_update_slice(attn_part, part_r, ((place ^ r) * width_q, width_qkv))
-    qkv_part = token_sum(normed.reshape(length, width), back_qkv)
-    own_attn = to_owners(lax.dynamic_update_slice(attn_part, qkv_part, (0, 0)))
+        attn_part = lax.dynamic_update_slice(
+            attn_part, out_blocks[r], ((place ^ r) * width_q, width_qkv)
+        )
+    attn_part, own_gu = tie(attn_part, own_gu)
+    own_attn = to_owners(attn_part)
 
     parts = split(jnp.einsum("tq,dq->td", back_qkv, w_qkv, preferred_element_type=f32))
     back_normed = scatter_seq(parts)
+    back_normed, own_gu = tie(back_normed, own_gu)
     mine_in = mine.astype(f32)
     grad_tokens = back_middle + norm_back(
         mine_in, rms_scale(mine_in), gain_first.astype(f32), back_normed
     )
 
     grad_down = jnp.zeros((count * piece, width), f32)
-    for r, block in enumerate(gather_seq(own_down)):
+    for r, block in enumerate(down_blocks):
         grad_down = lax.dynamic_update_slice_in_dim(
             grad_down, block.astype(f32), (place ^ r) * piece, axis=0
         )
     grad_gate, grad_up, grad_gain_mlp = put_columns(
-        place_arg, gather_seq(own_gu), w_gate, w_up, gain_mlp.reshape(-1, 1), shards
+        place_arg, gather_seq(own_gu), w_gate, w_up, gain_mlp.reshape(1, -1), shards
     )
     grad_query, grad_key, grad_value, grad_out, grad_gain_attn = put_attention(
         place_arg,
@@ -683,7 +727,7 @@
         w_query,
         w_key,
         w_value,
-        gain_attn.reshape(-1, 1),
+        gain_attn.reshape(1, -1),
         width,
         copies,
     )

time: 657 us -> 568 us (0.86)
  waiting for transfers between devices: 279 us -> 190 us
  local copies, waits for them, and re-layouts: 51.4 us -> 60.3 us
    reduce_scatter x3, waiting for transfers between devices: 69.2 us -> 0.01 us  [to_owners(): return lax.psum_scatter(part, 'shard', scatter_dimension=0, tiled=True)]
    ppermute x72 -> x69, waiting for transfers between devices: 206 us -> 190 us  [hop(): return lax.ppermute(value, 'seq', [(i, i ^ bit) for i in range(count)])]
    unnamed x137 -> x153, local copies, waits for them, and re-layouts: 19.4 us -> 30 us
    ppermute x72 -> x69, starting transfers between devices: 76 us -> 71.1 us  [hop(): return lax.ppermute(value, 'seq', [(i, i ^ bit) for i in range(count)])]
  transfers between devices with their start and end apart: 78 -> 75, of which waited for: 40 -> 36; matrix products, arithmetic and copies ran while one was open for 26% -> 32% of each run, Pallas kernels for 8% -> 12%
where the time goes in v3:
time: 568 us; the launch traced here: 565 us
  waiting for transfers between devices  190 us (33%)
  matrix products  97.7 us (17%)
  starting transfers between devices  72 us (13%)
  Pallas kernels  69.9 us (12%)
  local copies, waits for them, and re-layouts  60.3 us (11%)
  other arithmetic  47.1 us (8%)
  between operations  15.6 us (3%)
  blocking collectives  12.4 us (2%)
    ppermute x69, waiting for transfers between devices, hop(): return lax.ppermute(value, 'seq', [(i, i ^ bit) for i in range(count)])  190 us
    ppermute x69, starting transfers between devices, hop(): return lax.ppermute(value, 'seq', [(i, i ^ bit) for i in range(count)])  71.1 us
    dot_general x4, matrix products, token_sum(): jnp.einsum('tf,td->fd', left, right, preferred_element_type=f32)  32.1 us
    unnamed x153, local copies, waits for them, and re-layouts  30 us
    pallas_call x1, Pallas kernels, attend_back(): pl.pallas_call(functools.partial(attend_back_kernel, count, rows), grid_s...  27.2 us
    pallas_call x1, Pallas kernels, attend(): pl.pallas_call(functools.partial(attend_kernel, count, rows), grid_spec=p...  17.5 us
    dot_general x1, matrix products, on_device(): gate_up = jnp.dot(normed_mlp, w_gu, preferred_element_type=f32)  17.3 us
    dot_general x1, matrix products, on_device(): jnp.einsum('tf,df->td', back_gu, w_gu, preferred_element_type=f32)  15 us
  transfers between devices with their start and end apart: 75, of which 36 were waited for; matrix products, arithmetic and copies ran while one was open for 32% of the time, Pallas kernels for 12%

profile of v3, /device:TPU:0, one launch (start us, length us, event | category | flops | bytes accessed | tf_op | source)
XLA Modules:
  0.0 564.8 jit_solution(16246964409732004508)
XLA Ops:
  16.3 10.4 %collective-permute-done = bf16[128,2048]{1,0:T(8,128)(2,1)S(1)} collective-permute-done((bf16[128,2048]{1,0:T(8,128)(2,1)S(1)}, bf16[128,2048]{1,0:T(8,128)(2,1)S(1)}, u32[]{:S(2)}, u32[]{:S(2)}) %collective-permute-start) | collective-permute-done | bytes 524320 | tf_op jit(solution)/shard_map/ppermute | solution.py:28
  37.2 12.4 %all_gather.13 = bf16[2,2048]{1,0:T(2,128)(2,1)S(1)} all-gather(bf16[2,256]{1,0:T(2,128)(2,1)S(1)} %pad_maximum_fusion.16), channel_id=1, replica_groups=mesh['seq'=4,'shard'=8] {'shard'}, dimensions={1}, use_global_device_ids=true | all-gather | bytes 9216 | tf_op jit(solution)/shard_map/all_gather | solution.py:582
  57.5 7.3 %collective-permute-done.4 = bf16[128,2048]{1,0:T(8,128)(2,1)} collective-permute-done((bf16[128,2048]{1,0:T(8,128)(2,1)}, bf16[128,2048]{1,0:T(8,128)(2,1)}, u32[]{:S(2)}, u32[]{:S(2)}) %collective-permute-start.4) | collective-permute-done | bytes 524320 | tf_op jit(solution)/shard_map/ppermute | solution.py:28
  71.9 7.6 %project.1 = (bf16[4,256,2048]{2,1,0:T(8,128)(2,1)S(1)}, bf16[4,256,512]{2,1,0:T(8,128)(2,1)S(1)}, bf16[4,256,128]{2,1,0:T(8,128)(2,1)S(1)}, bf16[4,256,128]{2,1,0:T(8,128)(2,1)S(1)}) custom-call(bf16[4,256,2048]{2,1,0:T(8,128)(2,1)S(1)} %copy-done.2, bf16[1,2048]{1,0:T(2,128)(2,1)S(1)} %get-tuple-element.206.gain_ref, ...), custom_call_target="tpu_custom_call" | custom-call | flops 2684354560 | bytes 12582912 | tf_op jit(solution)/shard_map/project/pallas_call | solution.py:148
  86.5 17.5 %attend.1 = (bf16[4,256,512]{2,1,0:T(8,128)(2,1)S(1)}, f32[4,4,8,256]{3,2,1,0:T(8,128)S(1)}) custom-call(s32[1]{0:T(128)} %bitcast.1.place_ref, bf16[4,256,512]{2,1,0:T(8,128)(2,1)S(1)} %get-tuple-element.84.q_ref, bf16[4,256,128]{2,1,0:T(8,128)(2,1)S(1)} %get-tuple-element.85.k_ref, bf16[4,256,128]{2,1,0:T(8,128)(2,1)S(1)} %get-tuple-element.86.v_ref), custom_call_target="tpu_custom_call" | custom-call | flops 2147483648 | bytes 2097152 | tf_op jit(solution)/shard_map/attend/pallas_call | solution.py:245
  114.7 10.8 %collective-permute-done.10 = bf16[128,2048]{1,0:T(8,128)(2,1)S(1)} collective-permute-done((bf16[128,2048]{1,0:T(8,128)(2,1)S(1)}, bf16[128,2048]{1,0:T(8,128)(2,1)S(1)}, u32[]{:S(2)}, u32[]{:S(2)}) %collective-permute-start.10) | collective-permute-done | bytes 524320 | tf_op jit(solution)/shard_map/ppermute | solution.py:28
  129.1 7.7 %collective-permute-done.14 = bf16[128,2048]{1,0:T(8,128)(2,1)S(1)} collective-permute-done((bf16[128,2048]{1,0:T(8,128)(2,1)S(1)}, bf16[128,2048]{1,0:T(8,128)(2,1)S(1)}, u32[]{:S(2)}, u32[]{:S(2)}) %collective-permute-start.14) | collective-permute-done | bytes 524320 | tf_op jit(solution)/shard_map/ppermute | solution.py:28
  138.2 7.3 %collective-permute-done.11 = bf16[128,2048]{1,0:T(8,128)(2,1)S(1)} collective-permute-done((bf16[128,2048]{1,0:T(8,128)(2,1)S(1)}, bf16[128,2048]{1,0:T(8,128)(2,1)S(1)}, u32[]{:S(2)}, u32[]{:S(2)}) %collective-permute-start.11) | collective-permute-done | bytes 524320 | tf_op jit(solution)/shard_map/ppermute | solution.py:28
  153.9 11.1 %collective-permute-done.15 = bf16[128,2048]{1,0:T(8,128)(2,1)} collective-permute-done((bf16[128,2048]{1,0:T(8,128)(2,1)}, bf16[128,2048]{1,0:T(8,128)(2,1)}, u32[]{:S(2)}, u32[]{:S(2)}) %collective-permute-start.15) | collective-permute-done | bytes 524320 | tf_op jit(solution)/shard_map/ppermute | solution.py:28
  168.7 8.8 %collective-permute-done.17 = bf16[128,2048]{1,0:T(8,128)(2,1)} collective-permute-done((bf16[128,2048]{1,0:T(8,128)(2,1)}, bf16[128,2048]{1,0:T(8,128)(2,1)}, u32[]{:S(2)}, u32[]{:S(2)}) %collective-permute-start.17) | collective-permute-done | bytes 524320 | tf_op jit(solution)/shard_map/ppermute | solution.py:28
  180.2 4.1 collective-permute-done.19
  196.2 17.3 %fusion.31 = f32[1024,2816]{1,0:T(8,128)S(1)} fusion(bf16[1024,2048]{1,0:T(8,128)(2,1)} %constant_dynamic-update-slice_fusion, bf16[2048,2816]{1,0:T(8,128)(2,1)} %all-gather.8.cloned.1.call-done), kind=kOutput, calls=%fused_computation.140 | convolution fusion | flops 11811160064 | bytes 27262976 | tf_op jit(solution)/shard_map/dot_general | solution.py:645
  226.5 8.0 %convolution_convert_fusion.1 = bf16[1408,2048]{1,0:T(8,128)(2,1)} fusion(bf16[1024,1408]{1,0:T(8,128)(2,1)S(1)} %multiply_convert_fusion, bf16[1024,2048]{1,0:T(8,128)(2,1)S(1)} %constant_dynamic-update-slice_fusion.4), kind=kOutput, calls=%fused_computation.1 | convolution fusion | flops 5908463616 | bytes 12845056 | tf_op jit(solution)/shard_map/tf,td->fd/dot_general | solution.py:627
  235.0 8.7 %convolution_convert_fusion.5 = bf16[1024,2048]{1,0:T(8,128)(2,1)S(1)} fusion(bf16[1024,1408]{1,0:T(8,128)(2,1)S(1)} %multiply_convert_fusion, bf16[1408,2048]{1,0:T(8,128)(2,1)} %all-gather.6.cloned.1.call-done), kind=kOutput, calls=%fused_computation.17 | convolution fusion | flops 5907677184 | bytes 12845056 | tf_op jit(solution)/shard_map/dot_general | solution.py:657
  248.8 14.2 %fusion.2 = (bf16[1024,1408]{1,0:T(8,128)(2,1)S(1)}, bf16[1024,1408]{1,0:T(8,128)(2,1)S(1)}) fusion(f32[1024,2816]{1,0:T(8,128)} %copy-done.23, bf16[1024,2048]{1,0:T(8,128)(2,1)} %copy-done.64, bf16[1408,2048]{1,0:T(8,128)(2,1)} %all-gather.6.cloned.1.call-done), kind=kOutput, calls=%fused_computation.6 | convolution fusion | flops 5927206912 | bytes 27262976 | tf_op jit(solution)/shard_map/td,fd->tf/dot_general | solution.py:661
  270.7 15.0 %convolution_convert_fusion.2 = bf16[1024,2048]{1,0:T(8,128)(2,1)S(1)} fusion(bf16[1024,2816]{1,0:T(8,128)(2,1)S(1)} %pad_maximum_fusion, bf16[2048,2816]{1,0:T(8,128)(2,1)} %all-gather.8.cloned.1.call-done), kind=kOutput, calls=%fused_computation.14 | convolution fusion | flops 11813257216 | bytes 21495808 | tf_op jit(solution)/shard_map/tf,df->td/dot_general | solution.py:670
  297.0 18.0 %convolution_convert_fusion = bf16[2048,2816]{1,0:T(8,128)(2,1)} fusion(bf16[1024,2048]{1,0:T(8,128)(2,1)} %constant_dynamic-update-slice_fusion, bf16[1024,2816]{1,0:T(8,128)(2,1)S(1)} %pad_maximum_fusion), kind=kOutput, calls=%fused_computation | convolution fusion | flops 11816927232 | bytes 21495808 | tf_op jit(solution)/shard_map/tf,td->fd/dot_general | solution.py:627
  321.2 8.8 %collective-permute-done.37 = bf16[128,2048]{1,0:T(8,128)(2,1)S(1)} collective-permute-done((bf16[128,2048]{1,0:T(8,128)(2,1)S(1)}, bf16[128,2048]{1,0:T(8,128)(2,1)S(1)}, u32[]{:S(2)}, u32[]{:S(2)}) %collective-permute-start.37) | collective-permute-done | bytes 524320 | tf_op jit(solution)/shard_map/ppermute | solution.py:28
  333.5 4.5 fusion.19
  342.2 10.8 %collective-permute-done.39 = bf16[128,2048]{1,0:T(8,128)(2,1)S(1)} collective-permute-done((bf16[128,2048]{1,0:T(8,128)(2,1)S(1)}, bf16[128,2048]{1,0:T(8,128)(2,1)S(1)}, u32[]{:S(2)}, u32[]{:S(2)}) %collective-permute-start.39) | collective-permute-done | bytes 524320 | tf_op jit(solution)/shard_map/ppermute | solution.py:28
  355.0 10.6 %collective-permute-done.41 = bf16[128,2048]{1,0:T(8,128)(2,1)S(1)} collective-permute-done((bf16[128,2048]{1,0:T(8,128)(2,1)S(1)}, bf16[128,2048]{1,0:T(8,128)(2,1)S(1)}, u32[]{:S(2)}, u32[]{:S(2)}) %collective-permute-start.41) | collective-permute-done | bytes 524320 | tf_op jit(solution)/shard_map/ppermute | solution.py:28
  366.9 5.0 collective-permute-done.43
  383.5 10.0 %collective-permute-done.45 = bf16[512,512]{1,0:T(8,128)(2,1)S(1)} collective-permute-done((bf16[512,512]{1,0:T(8,128)(2,1)S(1)}, bf16[512,512]{1,0:T(8,128)(2,1)S(1)}, u32[]{:S(2)}, u32[]{:S(2)}) %collective-permute-start.45) | collective-permute-done | bytes 524320 | tf_op jit(solution)/shard_map/ppermute | solution.py:28
  396.8 27.2 %attend_back.1 = (bf16[4,256,512]{2,1,0:T(8,128)(2,1)S(1)}, bf16[4,256,128]{2,1,0:T(8,128)(2,1)S(1)}) custom-call(s32[1]{0:T(128)} %bitcast.1.place_ref, bf16[4,256,512]{2,1,0:T(8,128)(2,1)S(1)} %copy-done.11, bf16[4,256,128]{2,1,0:T(8,128)(2,1)S(1)} %copy-done.13, bf16[4,256,128]{2,1,0:T(8,128)(2,1)S(1)} %copy-done.15, bf16[4,256,512]{2,1,0:T(8,128)(2,1)S(1)} %copy-done.17, ...), custom_call_target="tpu_custom_call" | custom-call | flops 5368709120 | bytes 4194304 | tf_op jit(solution)/shard_map/attend_back/pallas_call | solution.py:369
  424.0 7.2 %collective-permute-done.46 = bf16[512,512]{1,0:T(8,128)(2,1)S(1)} collective-permute-done((bf16[512,512]{1,0:T(8,128)(2,1)S(1)}, bf16[512,512]{1,0:T(8,128)(2,1)S(1)}, u32[]{:S(2)}, u32[]{:S(2)}) %collective-permute-start.46) | collective-permute-done | bytes 524320 | tf_op jit(solution)/shard_map/ppermute | solution.py:28
  441.8 5.7 %convolution_convert_fusion.4 = bf16[1024,2048]{1,0:T(8,128)(2,1)S(1)} fusion(bf16[1024,640]{1,0:T(8,128)(2,1)S(1)} %bitcast.59, bf16[2048,1152]{1,0:T(8,128)(2,1)} %all-gather.4.cloned.1.call-done.w_ref), kind=kOutput, calls=%fused_computation.16 | convolution fusion | flops 2686451712 | bytes 8126464 | tf_op jit(solution)/shard_map/tq,dq->td/dot_general | solution.py:708
  457.6 5.0 collective-permute-done.52
  472.5 9.7 %collective-permute-done.53 = bf16[128,2048]{1,0:T(8,128)(2,1)S(1)} collective-permute-done((bf16[128,2048]{1,0:T(8,128)(2,1)S(1)}, bf16[128,2048]{1,0:T(8,128)(2,1)S(1)}, u32[]{:S(2)}, u32[]{:S(2)}) %collective-permute-start.53) | collective-permute-done | bytes 524320 | tf_op jit(solution)/shard_map/ppermute | solution.py:28
  489.4 12.6 %collective-permute-done.63 = bf16[128,2816]{1,0:T(8,128)(2,1)} collective-permute-done((bf16[128,2816]{1,0:T(8,128)(2,1)S(1)}, bf16[128,2816]{1,0:T(8,128)(2,1)}, u32[]{:S(2)}, u32[]{:S(2)}) %collective-permute-start.63) | collective-permute-done | bytes 720928 | tf_op jit(solution)/shard_map/ppermute | solution.py:28
  502.1 16.4 %collective-permute-done.66 = bf16[128,2816]{1,0:T(8,128)(2,1)} collective-permute-done((bf16[128,2816]{1,0:T(8,128)(2,1)S(1)}, bf16[128,2816]{1,0:T(8,128)(2,1)}, u32[]{:S(2)}, u32[]{:S(2)}) %collective-permute-start.66) | collective-permute-done | bytes 720928 | tf_op jit(solution)/shard_map/ppermute | solution.py:28
  531.9 13.0 %put_columns.1 = (f32[256,5632]{1,0:T(8,128)}, f32[256,5632]{1,0:T(8,128)}, f32[1,256]{1,0:T(1,128)}) custom-call(s32[1]{0:T(128)} %bitcast.1.place_ref, bf16[256,2816]{1,0:T(8,128)(2,1)} %reduce-scatter.6.cloned.1.call-done.refs_0_, bf16[256,2816]{1,0:T(8,128)(2,1)} %pad_maximum_fusion.2.refs_1_, bf16[256,2816]{1,0:T(8,128)(2,1)} %pad_maximum_fusion.3.refs_2_, ...), custom_call_target="tpu_custom_call" | custom-call | bytes 23068672 | tf_op jit(solution)/shard_map/put_columns/pallas_call | solution.py:479
  553.7 3.9 put_attention.1
  (380 shorter events, 212.4 us)
Async XLA Ops:
  7.2 61.4 %all-gather.4.cloned.1.call-start = ((), (), s32[]{:S(2)}) async-start(), calls=%async_computation.3 | async-start | bytes 5308416 | tf_op jit(solution)/shard_map/all_gather | solution.py:577
  10.5 185.7 %all-gather.8.cloned.1.call-start = ((), (), s32[]{:S(2)}) async-start(), calls=%async_computation.5 | async-start | bytes 12976128 | tf_op jit(solution)/shard_map/all_gather | solution.py:577
  34.5 200.5 %all-gather.6.cloned.1.call-start = ((), (), s32[]{:S(2)}) async-start(), calls=%async_computation.4 | async-start | bytes 6488064 | tf_op jit(solution)/shard_map/all_gather | solution.py:577
  83.8 22.9 %collective-permute-start.7 = (bf16[512,512]{1,0:T(8,128)(2,1)S(1)}, bf16[512,512]{1,0:T(8,128)(2,1)S(1)}, u32[]{:S(2)}, u32[]{:S(2)}) collective-permute-start(bf16[512,512]{1,0:T(8,128)(2,1)S(1)} %get-tuple-element.185), channel_id=1, source_target_pairs={{0,16},{8,24},{16,0},{24,8},{1,17},{9,25},{17,1},{25,9},{2,18},{10... | collective-permute-start | bytes 1572872 | tf_op jit(solution)/shard_map/ppermute | solution.py:28
  85.4 22.4 %collective-permute-start.8 = (bf16[512,512]{1,0:T(8,128)(2,1)S(1)}, bf16[512,512]{1,0:T(8,128)(2,1)S(1)}, u32[]{:S(2)}, u32[]{:S(2)}) collective-permute-start(bf16[512,512]{1,0:T(8,128)(2,1)S(1)} %get-tuple-element.184), channel_id=1, source_target_pairs={{0,24},{8,16},{16,8},{24,0},{1,25},{9,17},{17,9},{25,1},{2,26},{10... | collective-permute-start | bytes 1572872 | tf_op jit(solution)/shard_map/ppermute | solution.py:28
  113.0 23.7 %collective-permute-start.14 = (bf16[128,2048]{1,0:T(8,128)(2,1)S(1)}, bf16[128,2048]{1,0:T(8,128)(2,1)S(1)}, u32[]{:S(2)}, u32[]{:S(2)}) collective-permute-start(bf16[128,2048]{1,0:T(8,128)(2,1)S(1)} %get-tuple-element.174), channel_id=1, source_target_pairs={{0,16},{8,24},{16,0},{24,8},{1,17},{9,25},{17,1},{25,9},{2,18},{10... | collective-permute-start | bytes 1572872 | tf_op jit(solution)/shard_map/ppermute | solution.py:28
  113.7 24.4 %collective-permute-start.9 = (bf16[128,2048]{1,0:T(8,128)(2,1)S(1)}, bf16[128,2048]{1,0:T(8,128)(2,1)S(1)}, u32[]{:S(2)}, u32[]{:S(2)}) collective-permute-start(bf16[128,2048]{1,0:T(8,128)(2,1)S(1)} %get-tuple-element.173), channel_id=1, source_target_pairs={{0,8},{8,0},{16,24},{24,16},{1,9},{9,1},{17,25},{25,17},{2,10},{10... | collective-permute-start | bytes 1572872 | tf_op jit(solution)/shard_map/ppermute | solution.py:28
  152.3 25.3 %collective-permute-start.17 = (bf16[128,2048]{1,0:T(8,128)(2,1)}, bf16[128,2048]{1,0:T(8,128)(2,1)}, u32[]{:S(2)}, u32[]{:S(2)}) collective-permute-start(bf16[128,2048]{1,0:T(8,128)(2,1)} %get-tuple-element.198), channel_id=1, source_target_pairs={{0,16},{8,24},{16,0},{24,8},{1,17},{9,25},{17,1},{25,9},{2,18},{10... | collective-permute-start | bytes 1572872 | tf_op jit(solution)/shard_map/ppermute | solution.py:28
  153.2 25.7 %collective-permute-start.16 = (bf16[128,2048]{1,0:T(8,128)(2,1)}, bf16[128,2048]{1,0:T(8,128)(2,1)}, u32[]{:S(2)}, u32[]{:S(2)}) collective-permute-start(bf16[128,2048]{1,0:T(8,128)(2,1)} %get-tuple-element.199), channel_id=1, source_target_pairs={{0,8},{8,0},{16,24},{24,16},{1,9},{9,1},{17,25},{25,17},{2,10},{10... | collective-permute-start | bytes 1572872 | tf_op jit(solution)/shard_map/ppermute | solution.py:28
  168.5 204.4 %reduce-scatter.4.cloned.1.call-start = ((), (), s32[]{:S(2)}) async-start(), calls=%async_computation.6 | async-start | bytes 6488064 | tf_op jit(solution)/shard_map/reduce_scatter | solution.py:630
  186.7 26.8 %collective-permute-start.22 = (bf16[128,2048]{1,0:T(8,128)(2,1)}, bf16[128,2048]{1,0:T(8,128)(2,1)}, u32[]{:S(2)}, u32[]{:S(2)}) collective-permute-start(bf16[128,2048]{1,0:T(8,128)(2,1)} %get-tuple-element.196), channel_id=1, source_target_pairs={{0,16},{8,24},{16,0},{24,8},{1,17},{9,25},{17,1},{25,9},{2,18},{10... | collective-permute-start | bytes 1572872 | tf_op jit(solution)/shard_map/ppermute | solution.py:28
  188.2 31.8 %collective-permute-start.23 = (bf16[128,2048]{1,0:T(8,128)(2,1)}, bf16[128,2048]{1,0:T(8,128)(2,1)}, u32[]{:S(2)}, u32[]{:S(2)}) collective-permute-start(bf16[128,2048]{1,0:T(8,128)(2,1)} %get-tuple-element.196), channel_id=1, source_target_pairs={{0,8},{8,0},{16,24},{24,16},{1,9},{9,1},{17,25},{25,17},{2,10},{10... | collective-permute-start | bytes 1572872 | tf_op jit(solution)/shard_map/ppermute | solution.py:28
  188.9 24.6 %collective-permute-start.21 = (bf16[128,2048]{1,0:T(8,128)(2,1)}, bf16[128,2048]{1,0:T(8,128)(2,1)}, u32[]{:S(2)}, u32[]{:S(2)}) collective-permute-start(bf16[128,2048]{1,0:T(8,128)(2,1)} %get-tuple-element.197), channel_id=1, source_target_pairs={{0,8},{8,0},{16,24},{24,16},{1,9},{9,1},{17,25},{25,17},{2,10},{10... | collective-permute-start | bytes 1572872 | tf_op jit(solution)/shard_map/ppermute | solution.py:28
  190.2 30.9 %collective-permute-start.24 = (bf16[128,2048]{1,0:T(8,128)(2,1)}, bf16[128,2048]{1,0:T(8,128)(2,1)}, u32[]{:S(2)}, u32[]{:S(2)}) collective-permute-start(bf16[128,2048]{1,0:T(8,128)(2,1)} %get-tuple-element.197), channel_id=1, source_target_pairs={{0,16},{8,24},{16,0},{24,8},{1,17},{9,25},{17,1},{25,9},{2,18},{10... | collective-permute-start | bytes 1572872 | tf_op jit(solution)/shard_map/ppermute | solution.py:28
  234.5 206.6 %reduce-scatter.6.cloned.1.call-start = ((), (), s32[]{:S(2)}) async-start(), calls=%async_computation.7 | async-start | bytes 12976128 | tf_op jit(solution)/shard_map/reduce_scatter | solution.py:630
  264.0 23.3 %collective-permute-start.31 = (bf16[128,2048]{1,0:T(8,128)(2,1)}, bf16[128,2048]{1,0:T(8,128)(2,1)S(1)}, u32[]{:S(2)}, u32[]{:S(2)}) collective-permute-start(bf16[128,2048]{1,0:T(8,128)(2,1)} %slice.212), channel_id=1, source_target_pairs={{0,8},{8,0},{16,24},{24,16},{1,9},{9,1},{17,25},{25,17},{2,10},{10... | collective-permute-start | bytes 1572872 | tf_op jit(solution)/shard_map/ppermute | solution.py:28
  268.0 22.1 %collective-permute-start.30 = (bf16[128,2048]{1,0:T(8,128)(2,1)S(1)}, bf16[128,2048]{1,0:T(8,128)(2,1)S(1)}, u32[]{:S(2)}, u32[]{:S(2)}) collective-permute-start(bf16[128,2048]{1,0:T(8,128)(2,1)S(1)} %add_convert_fusion.5), channel_id=1, source_target_pairs={{0,16},{8,24},{16,0},{24,8},{1,17},{9,25},{17,1},{25,9},{2,18},{10... | collective-permute-start | bytes 1572872 | tf_op jit(solution)/shard_map/ppermute | solution.py:28
  291.3 23.8 %collective-permute-start.33 = (bf16[128,2048]{1,0:T(8,128)(2,1)}, bf16[128,2048]{1,0:T(8,128)(2,1)S(1)}, u32[]{:S(2)}, u32[]{:S(2)}) collective-permute-start(bf16[128,2048]{1,0:T(8,128)(2,1)} %get-tuple-element.193), channel_id=1, source_target_pairs={{0,8},{8,0},{16,24},{24,16},{1,9},{9,1},{17,25},{25,17},{2,10},{10... | collective-permute-start | bytes 1572872 | tf_op jit(solution)/shard_map/ppermute | solution.py:28
  292.7 22.4 %collective-permute-start.34 = (bf16[128,2048]{1,0:T(8,128)(2,1)}, bf16[128,2048]{1,0:T(8,128)(2,1)}, u32[]{:S(2)}, u32[]{:S(2)}) collective-permute-start(bf16[128,2048]{1,0:T(8,128)(2,1)} %get-tuple-element.192), channel_id=1, source_target_pairs={{0,16},{8,24},{16,0},{24,8},{1,17},{9,25},{17,1},{25,9},{2,18},{10... | collective-permute-start | bytes 1572872 | tf_op jit(solution)/shard_map/ppermute | solution.py:28
  317.1 207.0 %reduce-scatter.8.cloned.1.call-start = ((), (), s32[]{:S(2)}) async-start(), calls=%async_computation.8 | async-start | bytes 5308416 | tf_op jit(solution)/shard_map/reduce_scatter | solution.py:630
  340.1 25.5 %collective-permute-start.41 = (bf16[128,2048]{1,0:T(8,128)(2,1)S(1)}, bf16[128,2048]{1,0:T(8,128)(2,1)S(1)}, u32[]{:S(2)}, u32[]{:S(2)}) collective-permute-start(bf16[128,2048]{1,0:T(8,128)(2,1)S(1)} %get-tuple-element.190), channel_id=1, source_target_pairs={{0,16},{8,24},{16,0},{24,8},{1,17},{9,25},{17,1},{25,9},{2,18},{10... | collective-permute-start | bytes 1572872 | tf_op jit(solution)/shard_map/ppermute | solution.py:28
  341.6 24.2 %collective-permute-start.40 = (bf16[128,2048]{1,0:T(8,128)(2,1)S(1)}, bf16[128,2048]{1,0:T(8,128)(2,1)S(1)}, u32[]{:S(2)}, u32[]{:S(2)}) collective-permute-start(bf16[128,2048]{1,0:T(8,128)(2,1)S(1)} %get-tuple-element.191), channel_id=1, source_target_pairs={{0,8},{8,0},{16,24},{24,16},{1,9},{9,1},{17,25},{25,17},{2,10},{10... | collective-permute-start | bytes 1572872 | tf_op jit(solution)/shard_map/ppermute | solution.py:28
  379.5 51.8 %collective-permute-start.48 = (bf16[176,2048]{1,0:T(8,128)(2,1)S(1)}, bf16[176,2048]{1,0:T(8,128)(2,1)S(1)}, u32[]{:S(2)}, u32[]{:S(2)}) collective-permute-start(bf16[176,2048]{1,0:T(8,128)(2,1)S(1)} %copy-done.42), channel_id=1, source_target_pairs={{0,8},{8,0},{16,24},{24,16},{1,9},{9,1},{17,25},{25,17},{2,10},{10... | collective-permute-start | bytes 2162696 | tf_op jit(solution)/shard_map/ppermute | solution.py:28
  380.7 50.5 %collective-permute-start.49 = (bf16[176,2048]{1,0:T(8,128)(2,1)S(1)}, bf16[176,2048]{1,0:T(8,128)(2,1)S(1)}, u32[]{:S(2)}, u32[]{:S(2)}) collective-permute-start(bf16[176,2048]{1,0:T(8,128)(2,1)S(1)} %copy-done.42), channel_id=1, source_target_pairs={{0,16},{8,24},{16,0},{24,8},{1,17},{9,25},{17,1},{25,9},{2,18},{10... | collective-permute-start | bytes 2162696 | tf_op jit(solution)/shard_map/ppermute | solution.py:28
  381.3 50.0 %collective-permute-start.50 = (bf16[176,2048]{1,0:T(8,128)(2,1)S(1)}, bf16[176,2048]{1,0:T(8,128)(2,1)S(1)}, u32[]{:S(2)}, u32[]{:S(2)}) collective-permute-start(bf16[176,2048]{1,0:T(8,128)(2,1)S(1)} %copy-done.42), channel_id=1, source_target_pairs={{0,24},{8,16},{16,8},{24,0},{1,25},{9,17},{17,9},{25,1},{2,26},{10... | collective-permute-start | bytes 2162696 | tf_op jit(solution)/shard_map/ppermute | solution.py:28
  383.0 48.3 %collective-permute-start.46 = (bf16[512,512]{1,0:T(8,128)(2,1)S(1)}, bf16[512,512]{1,0:T(8,128)(2,1)S(1)}, u32[]{:S(2)}, u32[]{:S(2)}) collective-permute-start(bf16[512,512]{1,0:T(8,128)(2,1)S(1)} %get-tuple-element.180), channel_id=1, source_target_pairs={{0,16},{8,24},{16,0},{24,8},{1,17},{9,25},{17,1},{25,9},{2,18},{10... | collective-permute-start | bytes 1572872 | tf_op jit(solution)/shard_map/ppermute | solution.py:28
  393.6 37.7 %collective-permute-start.47 = (bf16[512,512]{1,0:T(8,128)(2,1)S(1)}, bf16[512,512]{1,0:T(8,128)(2,1)S(1)}, u32[]{:S(2)}, u32[]{:S(2)}) collective-permute-start(bf16[512,512]{1,0:T(8,128)(2,1)S(1)} %get-tuple-element.179), channel_id=1, source_target_pairs={{0,24},{8,16},{16,8},{24,0},{1,25},{9,17},{17,9},{25,1},{2,26},{10... | collective-permute-start | bytes 1572872 | tf_op jit(solution)/shard_map/ppermute | solution.py:28
  449.4 23.0 %collective-permute-start.51 = (bf16[128,2048]{1,0:T(8,128)(2,1)S(1)}, bf16[128,2048]{1,0:T(8,128)(2,1)S(1)}, u32[]{:S(2)}, u32[]{:S(2)}) collective-permute-start(bf16[128,2048]{1,0:T(8,128)(2,1)S(1)} %get-tuple-element.164), channel_id=1, source_target_pairs={{0,8},{8,0},{16,24},{24,16},{1,9},{9,1},{17,25},{25,17},{2,10},{10... | collective-permute-start | bytes 1572872 | tf_op jit(solution)/shard_map/ppermute | solution.py:28
  483.9 35.6 %collective-permute-start.65 = (bf16[128,2816]{1,0:T(8,128)(2,1)S(1)}, bf16[128,2816]{1,0:T(8,128)(2,1)S(1)}, u32[]{:S(2)}, u32[]{:S(2)}) collective-permute-start(bf16[128,2816]{1,0:T(8,128)(2,1)S(1)} %get-tuple-element.188), channel_id=1, source_target_pairs={{0,16},{8,24},{16,0},{24,8},{1,17},{9,25},{17,1},{25,9},{2,18},{10... | collective-permute-start | bytes 2162696 | tf_op jit(solution)/shard_map/ppermute | solution.py:28
  485.1 33.4 %collective-permute-start.66 = (bf16[128,2816]{1,0:T(8,128)(2,1)S(1)}, bf16[128,2816]{1,0:T(8,128)(2,1)}, u32[]{:S(2)}, u32[]{:S(2)}) collective-permute-start(bf16[128,2816]{1,0:T(8,128)(2,1)S(1)} %get-tuple-element.189), channel_id=1, source_target_pairs={{0,16},{8,24},{16,0},{24,8},{1,17},{9,25},{17,1},{25,9},{2,18},{10... | collective-permute-start | bytes 2162696 | tf_op jit(solution)/shard_map/ppermute | solution.py:28
  485.9 35.9 %collective-permute-start.64 = (bf16[128,2816]{1,0:T(8,128)(2,1)S(1)}, bf16[128,2816]{1,0:T(8,128)(2,1)S(1)}, u32[]{:S(2)}, u32[]{:S(2)}) collective-permute-start(bf16[128,2816]{1,0:T(8,128)(2,1)S(1)} %get-tuple-element.189), channel_id=1, source_target_pairs={{0,8},{8,0},{16,24},{24,16},{1,9},{9,1},{17,25},{25,17},{2,10},{10... | collective-permute-start | bytes 2162696 | tf_op jit(solution)/shard_map/ppermute | solution.py:28
  502.0 27.7 %collective-permute-start.67 = (bf16[128,2816]{1,0:T(8,128)(2,1)}, bf16[128,2816]{1,0:T(8,128)(2,1)S(1)}, u32[]{:S(2)}, u32[]{:S(2)}) collective-permute-start(bf16[128,2816]{1,0:T(8,128)(2,1)} %collective-permute-done.63), channel_id=1, source_target_pairs={{0,16},{8,24},{16,0},{24,8},{1,17},{9,25},{17,1},{25,9},{2,18},{10... | collective-permute-start | bytes 2162696 | tf_op jit(solution)/shard_map/ppermute | solution.py:28
  (114 other events, 1486.3 us)
Sparse Core Ops, SparseCore 0:
  10.6 54.4 all-gather.3
  67.3 106.8 all-gather.7
  175.8 58.7 all-gather.5
  237.3 63.5 reduce-scatter.3
  317.2 116.3 reduce-scatter.5
  441.2 52.7 reduce-scatter.7

commit v4 on v3

--- a/solution.py
+++ b/solution.py
@@ -16,6 +16,7 @@
 EPSILON = 1e-05
 THETA = 10000.0
 MASKED = -1e30
+MIB = 2**20
 
 f32 = jnp.float32
 bf16 = jnp.bfloat16
@@ -34,12 +35,15 @@
 
 def gather_seq(block, filler=None):
     count = lax.axis_size("seq")
+    pieces = block if isinstance(block, tuple) else None
+    if pieces is not None:
+        block = jnp.concatenate(pieces, axis=0)
     blocks = [block]
     if count == 2:
         blocks.append(hop(block, 1))
     if count >= 4:
         half = block.shape[0] // 2
-        upper, lower = block[:half], block[half:]
+        upper, lower = pieces or (block[:half], block[half:])
         near_upper, other_lower = hop(upper, 1), hop(lower, 2)
         near_lower, other_upper = hop(lower, 1), hop(upper, 2)
         if filler is not None:
@@ -55,8 +59,24 @@
     return blocks if filler is None else (blocks, filler)
 
 
-def gather_direct(block):
-    return [block] + [hop(block, r) for r in range(1, lax.axis_size("seq"))]
+def gather_halves(upper, lower):
+    if lax.axis_size("seq") != 4:
+        return gather_seq(jnp.concatenate([upper, lower], axis=0))
+    near_upper, other_lower = hop(upper, 1), hop(lower, 2)
+    near_lower, other_upper = hop(lower, 1), hop(upper, 2)
+    far_upper, far_lower = hop(near_upper, 2), hop(other_lower, 1)
+    return [upper, lower, near_upper, near_lower, other_upper, other_lower, far_upper, far_lower]
+
+
+def gather_near(block):
+    return (hop(block, 1), hop(block, 2)) if lax.axis_size("seq") == 4 else ()
+
+
+def gather_far(block, near):
+    if not near:
+        return gather_seq(block), ()
+    half = block.shape[0] // 2
+    return [block, *near], (hop(near[0][:half], 2), hop(near[1][half:], 1))
 
 
 def add_low(first, second):
@@ -88,6 +108,13 @@
     return parts[0], (sent_x, sent_y), straight
 
 
+def scatter_pieces(state):
+    kept, sent, straight = state
+    if not sent:
+        return scatter_end(state), ()
+    return kept, (straight[0], sent[0], sent[1], straight[1])
+
+
 def scatter_end(state):
     kept, sent, straight = state
     total = kept.astype(f32)
@@ -121,8 +148,274 @@
     )
 
 
-def project_kernel(width_q, x_ref, gain_ref, w_ref, cos_ref, sin_ref, n_ref, q_ref, k_ref, v_ref):
-    values = x_ref[0].astype(f32)
+def branch_kernel(count, given, place_ref, w_ref, t_ref, *refs):
+    back_ref, out_refs, rows_s = refs[given], refs[given + 1 : -1], refs[-1]
+    step = pl.program_id(0)
+
+    @pl.when(step == 0)
+    def _():
+        at = 0
+        for ref in refs[:given]:
+            rows_s[at : at + ref.shape[0], :] = ref[...]
+            at += ref.shape[0]
+
+    rows = rows_s.shape[0] // count
+    part = rows_s.shape[1] // count
+    block = rows_s[pl.ds(pl.multiple_of(step * rows, rows), rows), :]
+    back_ref[0] = lax.dot_general(
+        block, w_ref[...], NT, preferred_element_type=f32
+    ).astype(bf16)
+    columns = rows_s[:, pl.ds(pl.multiple_of(step * part, part), part)]
+    result = jnp.dot(t_ref[...], columns, preferred_element_type=f32).astype(bf16)
+    for r in range(count):
+
+        @pl.when(step == place_ref[0] ^ r)
+        def _(r=r):
+            out_refs[r][...] = result
+
+
+def branch(place, pieces, w_o, attended_t):
+    count = lax.axis_size("seq")
+    width_q, length = attended_t.shape
+    width = w_o.shape[1]
+    rows, part = length // count, width // count
+    whole = lambda shape: pl.BlockSpec(shape, lambda i, at: (0,) * len(shape))
+    return pl.pallas_call(
+        functools.partial(branch_kernel, count, len(pieces)),
+        grid_spec=pltpu.PrefetchScalarGridSpec(
+            num_scalar_prefetch=1,
+            grid=(count,),
+            in_specs=[whole(w_o.shape), whole(attended_t.shape)]
+            + [whole(one.shape) for one in pieces],
+            out_specs=[pl.BlockSpec((1, rows, width_q), lambda i, at: (i, 0, 0))]
+            + [whole((width_q, part))] * count,
+            scratch_shapes=[pltpu.VMEM((length, width), bf16)],
+        ),
+        out_shape=[jax.ShapeDtypeStruct((count, rows, width_q), bf16)]
+        + [jax.ShapeDtypeStruct((width_q, part), bf16)] * count,
+        compiler_params=pltpu.CompilerParams(vmem_limit_bytes=60 * MIB),
+        cost_estimate=pl.CostEstimate(flops=1, bytes_accessed=1, transcendentals=0),
+        name="branch",
+    )(place, w_o, attended_t, *pieces)
+
+
+def attention_grads_kernel(count, place_ref, n_ref, dq_ref, dkv_ref, *refs):
+    out_refs, part_ref, sorted_s = refs[:count], refs[count], refs[count + 1]
+
+    @pl.when(pl.program_id(0) == 0)
+    def _():
+        for r in range(count):
+            sorted_s[place_ref[0] ^ r] = out_refs[r][...]
+
+    def token_sum(left, right):
+        return lax.dot_general(
+            left, right, (((0,), (0,)), ((), ())), preferred_element_type=f32
+        ).astype(bf16)
+
+    width_q = dq_ref.shape[1]
+    normed = n_ref[...]
+    part_ref[:, :width_q] = token_sum(normed, dq_ref[...])
+    part_ref[:, width_q : width_q + PAIR] = token_sum(normed, dkv_ref[...])
+    part_ref[:, width_q + PAIR :] = sorted_s[pl.program_id(0)]
+
+
+def attention_grads(place, normed, back_query, back_kv, out_blocks):
+    count = len(out_blocks)
+    length, width = normed.shape
+    width_q = back_query.shape[1]
+    part_q, part_d = out_blocks[0].shape
+    whole = lambda shape: pl.BlockSpec(shape, lambda a, at: (0, 0))
+    wide = width_q + PAIR + part_d
+    return pl.pallas_call(
+        functools.partial(attention_grads_kernel, count),
+        grid_spec=pltpu.PrefetchScalarGridSpec(
+            num_scalar_prefetch=1,
+            grid=(count,),
+            in_specs=[
+                pl.BlockSpec((length, part_q), lambda a, at: (0, a)),
+                whole((length, width_q)),
+                whole((length, PAIR)),
+            ]
+            + [whole((part_q, part_d))] * count,
+            out_specs=pl.BlockSpec((part_q, wide), lambda a, at: (a, 0)),
+            scratch_shapes=[pltpu.VMEM((count, part_q, part_d), bf16)],
+        ),
+        out_shape=jax.ShapeDtypeStruct((width, wide), bf16),
+        compiler_params=pltpu.CompilerParams(vmem_limit_bytes=60 * MIB),
+        cost_estimate=pl.CostEstimate(flops=1, bytes_accessed=1, transcendentals=0),
+        name="attention_grads",
+    )(place, normed, back_query, back_kv, *out_blocks)
+
+
+def input_grads_kernel(count, dq_ref, dkv_ref, w_ref, *outs):
+    width_q = dq_ref.shape[1]
+    weights = w_ref[...]
+    result = lax.dot_general(
+        dq_ref[...], weights[:, :width_q], NT, preferred_element_type=f32
+    ) + lax.dot_general(dkv_ref[...], weights[:, width_q:], NT, preferred_element_type=f32)
+    at = 0
+    for out in outs:
+        out[...] = result[at : at + out.shape[0], :].astype(bf16)
+        at += out.shape[0]
+
+
+def input_grads(back_query, back_kv, weights):
+    count = lax.axis_size("seq")
+    length, width_q = back_query.shape
+    width = weights.shape[0]
+    rows = length // count
+    sizes = [rows] * (count - 1) + ([rows // 2] * 2 if count == 4 else [rows])
+    step = 512
+    whole = lambda shape: pl.BlockSpec(shape, lambda i: (0, 0))
+    return pl.pallas_call(
+        functools.partial(input_grads_kernel, count),
+        grid=(width // step,),
+        in_specs=[
+            whole(back_query.shape),
+            whole(back_kv.shape),
+            pl.BlockSpec((step, width_q + PAIR), lambda i: (i, 0)),
+        ],
+        out_specs=[pl.BlockSpec((size, step), lambda i: (0, i)) for size in sizes],
+        out_shape=[jax.ShapeDtypeStruct((size, width), bf16) for size in sizes],
+        compiler_params=pltpu.CompilerParams(vmem_limit_bytes=40 * MIB),
+        cost_estimate=pl.CostEstimate(flops=1, bytes_accessed=1, transcendentals=0),
+        name="input_grads",
+    )(back_query, back_kv, weights)
+
+
+def turn_kernel(x_ref, y_ref, upper_ref, lower_ref, to_x_ref, to_y_ref):
+    first = pl.program_id(0) == 0
+    to_x, to_y = x_ref[...].astype(f32), y_ref[...].astype(f32)
+    to_x_ref[...] = jnp.where(first, to_x, to_x + lower_ref[...].astype(f32)).astype(bf16)
+    to_y_ref[...] = jnp.where(first, to_y + upper_ref[...].astype(f32), to_y).astype(bf16)
+
+
+def turn(parts, turning):
+    half, width = turning[0].shape
+    part = pl.BlockSpec((half, width), lambda i: (i, 0))
+    fixed = pl.BlockSpec((half, width), lambda i: (0, 0))
+    return pl.pallas_call(
+        turn_kernel,
+        grid=(2,),
+        in_specs=[part, part, fixed, fixed],
+        out_specs=[part, part],
+        out_shape=[jax.ShapeDtypeStruct((2 * half, width), bf16)] * 2,
+        compiler_params=pltpu.CompilerParams(vmem_limit_bytes=60 * MIB),
+        cost_estimate=pl.CostEstimate(flops=1, bytes_accessed=1, transcendentals=0),
+        name="turn",
+    )(*parts, *turning)
+
+
+def norm_kernel(given, kept, add_ref, gain_ref, *refs):
+    arrived, (middle_ref, upper_ref, lower_ref) = refs[:given], refs[given:]
+    first = 2 * pl.program_id(0) < pl.num_programs(0)
+    values = kept[...].astype(f32) + add_ref[...].astype(f32)
+    if given == 4:
+        for upper, lower in (arrived[:2], arrived[2:]):
+            values += jnp.where(first, upper[...].astype(f32), lower[...].astype(f32))
+    middle_ref[...] = values
+    scale = lax.rsqrt(jnp.mean(values * values, axis=-1, keepdims=True) + EPSILON)
+    result = (values * scale * gain_ref[...].astype(f32)).astype(bf16)
+
+    @pl.when(first)
+    def _():
+        upper_ref[...] = result
+
+    @pl.when(jnp.logical_not(first))
+    def _():
+        lower_ref[...] = result
+
+
+def norm(kept, arrived, add, gain):
+    rows, width = add.shape
+    half = rows // 2
+    step = half // 2
+    block = pl.BlockSpec((step, width), lambda i: (i, 0))
+    fixed = pl.BlockSpec((1, width), lambda i: (0, 0))
+    upper = pl.BlockSpec((step, width), lambda i: (jnp.minimum(i, 1), 0))
+    lower = pl.BlockSpec((step, width), lambda i: (jnp.maximum(i, 2) - 2, 0))
+    pieces = [upper, lower] * 2 if len(arrived) == 4 else [block] * len(arrived)
+    low = jax.ShapeDtypeStruct((half, width), bf16)
+    return pl.pallas_call(
+        functools.partial(norm_kernel, len(arrived)),
+        grid=(4,),
+        in_specs=[block, block, fixed] + pieces,
+        out_specs=[block, upper, lower],
+        out_shape=[jax.ShapeDtypeStruct((rows, width), f32), low, low],
+        compiler_params=pltpu.CompilerParams(vmem_limit_bytes=60 * MIB),
+        cost_estimate=pl.CostEstimate(flops=1, bytes_accessed=1, transcendentals=0),
+        name="norm",
+    )(kept, add, gain, *arrived)
+
+
+def norm_back_kernel(given, *refs):
+    kept, values_ref, add_ref, gain_ref = refs[:4]
+    arrived, outs = refs[4 : 4 + given], refs[4 + given :]
+    back = kept[...].astype(f32)
+    first = 2 * pl.program_id(0) < pl.num_programs(0)
+    if given == 2:
+        back += arrived[0][...].astype(f32) + arrived[1][...].astype(f32)
+    if given == 4:
+        for upper, lower in (arrived[:2], arrived[2:]):
+            back += jnp.where(first, upper[...].astype(f32), lower[...].astype(f32))
+    values = values_ref[...].astype(f32)
+    branch = back * gain_ref[...].astype(f32)
+    scale = lax.rsqrt(jnp.mean(values * values, axis=-1, keepdims=True) + EPSILON)
+    inner = jnp.mean(branch * values, axis=-1, keepdims=True)
+    result = add_ref[...].astype(f32) + scale * (branch - values * (scale * scale * inner))
+    outs[0][...] = result
+    if len(outs) == 3:
+
+        @pl.when(first)
+        def _():
+            outs[1][...] = result.astype(bf16)
+
+        @pl.when(jnp.logical_not(first))
+        def _():
+            outs[2][...] = result.astype(bf16)
+
+
+def norm_back(kept, arrived, values, add, gain, halves):
+    rows, width = values.shape
+    half = rows // 2
+    step = half // 2
+    block = pl.BlockSpec((step, width), lambda i: (i, 0))
+    fixed = pl.BlockSpec((1, width), lambda i: (0, 0))
+    upper = pl.BlockSpec((step, width), lambda i: (jnp.minimum(i, 1), 0))
+    lower = pl.BlockSpec((step, width), lambda i: (jnp.maximum(i, 2) - 2, 0))
+    pieces = [upper, lower] * 2 if len(arrived) == 4 else [block] * len(arrived)
+    low = jax.ShapeDtypeStruct((half, width), bf16)
+    return pl.pallas_call(
+        functools.partial(norm_back_kernel, len(arrived)),
+        grid=(4,),
+        in_specs=[block, block, block, fixed] + pieces,
+        out_specs=[block] + ([upper, lower] if halves else []),
+        out_shape=[jax.ShapeDtypeStruct((rows, width), f32)] + [low] * (2 if halves else 0),
+        compiler_params=pltpu.CompilerParams(vmem_limit_bytes=60 * MIB),
+        cost_estimate=pl.CostEstimate(flops=1, bytes_accessed=1, transcendentals=0),
+        name="norm_back",
+    )(kept, values, add, gain, *arrived)
+
+
+def spread_blocks(count, refs, store):
+    for r in range(count):
+        if r == count - 1 and len(refs) > count:
+            store(r, 0, refs[r])
+            store(r, refs[r].shape[0], refs[r + 1])
+        else:
+            store(r, 0, refs[r])
+
+
+def project_kernel(count, width_q, given, *refs):
+    gain_ref, w_ref, cos_ref, sin_ref, n_ref, q_ref, k_ref, v_ref, x_s = refs[given:]
+
+    def store(r, at, ref):
+        @pl.when(pl.program_id(0) == r)
+        def _():
+            x_s[at : at + ref.shape[0], :] = ref[...]
+
+    spread_blocks(count, refs[:given], store)
+    values = x_s[...].astype(f32)
     scale = lax.rsqrt(jnp.mean(values * values, axis=-1, keepdims=True) + EPSILON)
     normed = (values * scale * gain_ref[...].astype(f32)).astype(bf16)
     n_ref[0] = normed
@@ -140,16 +433,17 @@
     v_ref[0] = jnp.where(first, swapped, both).astype(bf16)
 
 
-def project(x, gain, weights, cosine, sine, width_q):
-    count, rows, width = x.shape
+def project(blocks, gain, weights, cosine, sine, width_q):
+    count = lax.axis_size("seq")
+    rows, width = blocks[0].shape
     row_block = lambda last: pl.BlockSpec((1, rows, last), lambda i: (i, 0, 0))
     whole = lambda shape: pl.BlockSpec(shape, lambda i: (0,) * len(shape))
     shape = lambda last: jax.ShapeDtypeStruct((count, rows, last), bf16)
     return pl.pallas_call(
-        functools.partial(project_kernel, width_q),
+        functools.partial(project_kernel, count, width_q, len(blocks)),
         grid=(count,),
-        in_specs=[
-            row_block(width),
+        in_specs=[whole(one.shape) for one in blocks]
+        + [
             whole((1, width)),
             whole((width, width_q + PAIR)),
             row_block(PAIR),
@@ -157,14 +451,11 @@
         ],
         out_specs=[row_block(width), row_block(width_q), row_block(PAIR), row_block(PAIR)],
         out_shape=[shape(width), shape(width_q), shape(PAIR), shape(PAIR)],
-        compiler_params=pltpu.CompilerParams(vmem_limit_bytes=40 * 2**20),
-        cost_estimate=pl.CostEstimate(
-            flops=2 * count * rows * width * (width_q + PAIR),
-            bytes_accessed=6 * count * rows * width,
-            transcendentals=0,
-        ),
+        scratch_shapes=[pltpu.VMEM((rows, width), bf16)],
+        compiler_params=pltpu.CompilerParams(vmem_limit_bytes=60 * MIB),
+        cost_estimate=pl.CostEstimate(flops=1, bytes_accessed=1, transcendentals=0),
         name="project",
-    )(x, gain, weights, cosine, sine)
+    )(*blocks, gain, weights, cosine, sine)
 
 
 def take_keys(count, rows, place, k_ref, v_ref, keys_of, values_of):
@@ -180,7 +471,7 @@
 
 
 def attend_kernel(
-    count, rows, place_ref, q_ref, k_ref, v_ref, o_ref, l_ref, key_s, value_s, score_s
+    count, rows, place_ref, q_ref, k_ref, v_ref, o_ref, t_ref, l_ref, key_s, value_s, score_s
 ):
     block = pl.program_id(1)
 
@@ -234,6 +525,7 @@
                 result = result / weight
                 total = result if total is None else total + result
             o_ref[0] = total.T.astype(bf16)
+            t_ref[...] = total.astype(bf16)
 
 
 def attend(place, queries, keys, values):
@@ -248,7 +540,11 @@
             num_scalar_prefetch=1,
             grid=(pairs, count),
             in_specs=[mine, whole, whole],
-            out_specs=[mine, pl.BlockSpec((1, 1, 8, rows), lambda p, i, at: (p, i, 0, 0))],
+            out_specs=[
+                mine,
+                pl.BlockSpec((PAIR, rows), lambda p, i, at: (p, i ^ at[0])),
+                pl.BlockSpec((1, 1, 8, rows), lambda p, i, at: (p, i, 0, 0)),
+            ],
             scratch_shapes=[
                 pltpu.VMEM((2, length, PAIR), bf16),
                 pltpu.VMEM((2, PAIR, length), bf16),
@@ -257,14 +553,11 @@
         ),
         out_shape=[
             jax.ShapeDtypeStruct(queries.shape, bf16),
+            jax.ShapeDtypeStruct((width, length), bf16),
             jax.ShapeDtypeStruct((pairs, count, 8, rows), f32),
         ],
-        compiler_params=pltpu.CompilerParams(vmem_limit_bytes=40 * 2**20),
-        cost_estimate=pl.CostEstimate(
-            flops=4 * pairs * length * length * PAIR,
-            bytes_accessed=4 * length * width,
-            transcendentals=pairs * length * length,
-        ),
+        compiler_params=pltpu.CompilerParams(vmem_limit_bytes=24 * MIB),
+        cost_estimate=pl.CostEstimate(flops=1, bytes_accessed=1, transcendentals=0),
         name="attend",
     )(place, queries, keys, values)
 
@@ -289,10 +582,10 @@
     dk_s,
     dv_s,
 ):
-    pair, block = pl.program_id(0), pl.program_id(1)
+    pair = pl.program_id(0)
     place = place_ref[0]
 
-    @pl.when((pair == 0) & (block == 0))
+    @pl.when(pair == 0)
     def _():
         def keys_of(h, at, value):
             key_s[h, pl.ds(at, rows), :] = value
@@ -310,45 +603,39 @@
     allowed = key_at <= query_at
 
     for c in range(count):
-
-        @pl.when(block == c)
-        def _(c=c):
-            queries, back = q_ref[0], d_ref[0]
-            first = lane_in_first_half(queries.shape)
-            zero = jnp.zeros_like(queries)
-            terms = (back.astype(f32) * o_ref[0].astype(f32)).T
-            total = None
-            for h in range(2):
-                row_term = jnp.sum(
-                    terms[h * HEAD_DIM : (h + 1) * HEAD_DIM, :], axis=0, keepdims=True
+        block = place ^ c
+        queries, back = q_ref[block], d_ref[block]
+        first = lane_in_first_half(queries.shape)
+        zero = jnp.zeros_like(queries)
+        terms = (back.astype(f32) * o_ref[block].astype(f32)).T
+        total = None
+        for h in range(2):
+            row_term = jnp.sum(terms[h * HEAD_DIM : (h + 1) * HEAD_DIM, :], axis=0, keepdims=True)
+            query_h = jnp.where(first, queries, zero) if h == 0 else jnp.where(first, zero, queries)
+            back_h = jnp.where(first, back, zero) if h == 0 else jnp.where(first, zero, back)
+            logsum = l_ref[0, c, h : h + 1, :]
+            for t in range(c + 1):
+                at = slice(t * rows, (t + 1) * rows)
+                scores = lax.dot_general(
+                    key_s[h, at, :], queries, NT, preferred_element_type=f32
                 )
-                query_h = jnp.where(first, queries, zero) if h == 0 else jnp.where(first, zero, queries)
-                back_h = jnp.where(first, back, zero) if h == 0 else jnp.where(first, zero, back)
-                logsum = l_ref[0, 0, h : h + 1, :]
-                for t in range(c + 1):
-                    at = slice(t * rows, (t + 1) * rows)
-                    scores = lax.dot_general(
-                        key_s[h, at, :], queries, NT, preferred_element_type=f32
-                    )
-                    if t == c:
-                        scores = jnp.where(allowed, scores, MASKED)
-                    probs = jnp.exp(scores - logsum)
-                    back_probs = lax.dot_general(
-                        value_s[h, at, :], back, NT, preferred_element_type=f32
-                    )
-                    back_scores = (probs * (back_probs - row_term)).astype(bf16)
-                    dv_s[at, :] += jnp.dot(
-                        probs.astype(bf16), back_h, preferred_element_type=f32
-                    )
-                    dk_s[at, :] += jnp.dot(back_scores, query_h, preferred_element_type=f32)
-                    part = jnp.dot(flat_s[h, :, at], back_scores, preferred_element_type=f32)
-                    total = part if total is None else total + part
-            turned = (total.T * HEAD_DIM**-0.5).astype(bf16).astype(f32)
-            dq_ref[0] = (
-                turned * cos_ref[block ^ place] - swap_quarters(turned) * sin_ref[block ^ place]
-            ).astype(bf16)
-
-    @pl.when((pair == pl.num_programs(0) - 1) & (block == pl.num_programs(1) - 1))
+                if t == c:
+                    scores = jnp.where(allowed, scores, MASKED)
+                probs = jnp.exp(scores - logsum)
+                back_probs = lax.dot_general(
+                    value_s[h, at, :], back, NT, preferred_element_type=f32
+                )
+                back_scores = (probs * (back_probs - row_term)).astype(bf16)
+                dv_s[at, :] += jnp.dot(probs.astype(bf16), back_h, preferred_element_type=f32)
+                dk_s[at, :] += jnp.dot(back_scores, query_h, preferred_element_type=f32)
+                part = jnp.dot(flat_s[h, :, at], back_scores, preferred_element_type=f32)
+                total = part if total is None else total + part
+        turned = (total.T * HEAD_DIM**-0.5).astype(bf16).astype(f32)
+        dq_ref[block] = (
+            turned * cos_ref[block] - swap_quarters(turned) * sin_ref[block]
+        ).astype(bf16)
+
+    @pl.when(pair == pl.num_programs(0) - 1)
     def _():
         for r in range(count):
             at = pl.multiple_of((place ^ r) * rows, rows)
@@ -364,20 +651,20 @@
     count, rows, width = queries.shape
     pairs = width // PAIR
     length = count * rows
-    whole = pl.BlockSpec((count, rows, PAIR), lambda p, i, at: (0, 0, 0))
-    mine = pl.BlockSpec((1, rows, PAIR), lambda p, i, at: (i ^ at[0], 0, p))
+    whole = pl.BlockSpec((count, rows, PAIR), lambda p, at: (0, 0, 0))
+    mine = pl.BlockSpec((count, rows, PAIR), lambda p, at: (0, 0, p))
     return pl.pallas_call(
         functools.partial(attend_back_kernel, count, rows),
         grid_spec=pltpu.PrefetchScalarGridSpec(
             num_scalar_prefetch=1,
-            grid=(pairs, count),
+            grid=(pairs,),
             in_specs=[
                 mine,
                 whole,
                 whole,
                 mine,
                 mine,
-                pl.BlockSpec((1, 1, 8, rows), lambda p, i, at: (p, i, 0, 0)),
+                pl.BlockSpec((1, count, 8, rows), lambda p, at: (p, 0, 0, 0)),
                 whole,
                 whole,
             ],
@@ -394,25 +681,10 @@
             jax.ShapeDtypeStruct(queries.shape, bf16),
             jax.ShapeDtypeStruct((count, rows, PAIR), bf16),
         ],
-        compiler_params=pltpu.CompilerParams(vmem_limit_bytes=40 * 2**20),
-        cost_estimate=pl.CostEstimate(
-            flops=10 * pairs * length * length * PAIR,
-            bytes_accessed=8 * length * width,
-            transcendentals=pairs * length * length,
-        ),
+        compiler_params=pltpu.CompilerParams(vmem_limit_bytes=32 * MIB),
+        cost_estimate=pl.CostEstimate(flops=1, bytes_accessed=1, transcendentals=0),
         name="attend_back",
     )(place, queries, keys, values, attended, back, logsum, cosine, sine)
-
-
-def sort_blocks(place, blocks):
-    bit = 1
-    while bit < len(blocks):
-        flip = (place & bit) != 0
-        blocks = [
-            jnp.where(flip, blocks[r ^ bit], blocks[r]) for r in range(len(blocks))
-        ]
-        bit *= 2
-    return blocks
 
 
 def take_columns_kernel(shards, count, piece, place_ref, gate_ref, up_ref, out_ref):
@@ -443,20 +715,42 @@
             out_specs=block(2 * shards * piece),
         ),
         out_shape=jax.ShapeDtypeStruct((rows, 2 * shards * piece), bf16),
-        compiler_params=pltpu.CompilerParams(vmem_limit_bytes=40 * 2**20),
-        cost_estimate=pl.CostEstimate(
-            flops=0, bytes_accessed=6 * rows * ff, transcendentals=0
-        ),
+        compiler_params=pltpu.CompilerParams(vmem_limit_bytes=32 * MIB),
+        cost_estimate=pl.CostEstimate(flops=1, bytes_accessed=1, transcendentals=0),
         name="take_columns",
     )(place, w_gate, w_up)
 
 
-def put_columns_kernel(shards, count, piece, place_ref, *refs):
-    block_refs = refs[:count]
-    gate_w, up_w, gain_ref, gate_ref, up_ref, gain_out = refs[count:]
+def read_blocks(place, refs, sorted_s):
+    count = sorted_s.shape[0]
+    for r in range(min(count, len(refs))):
+        if r == count - 1 and len(refs) > count:
+            first = 2 * pl.program_id(0) < pl.num_programs(0)
+
+            @pl.when(first)
+            def _():
+                sorted_s[place ^ r] = refs[r][...]
+
+            @pl.when(jnp.logical_not(first))
+            def _():
+                sorted_s[place ^ r] = refs[r + 1][...]
+        else:
+            sorted_s[place ^ r] = refs[r][...]
+    return [sorted_s[a].astype(f32) for a in range(count)]
+
+
+def block_specs(step, blocks, far):
+    wide = blocks[0].shape[1]
+    half = max(1, blocks[0].shape[0] // 2 // step)
+    return [pl.BlockSpec((step, wide), lambda i, at: (i, 0))] * len(blocks) + [
+        pl.BlockSpec((step, wide), lambda i, at: (i % half, 0))
+    ] * len(far)
+
+
+def put_columns_kernel(shards, count, piece, given, place_ref, *refs):
+    gate_w, up_w, gain_ref, gate_ref, up_ref, gain_out = refs[given:-1]
     width = shards * piece
-    blocks = [ref[...].astype(f32) for ref in block_refs]
-    blocks = sort_blocks(place_ref[0], blocks)
+    blocks = read_blocks(place_ref[0], refs[:given], refs[-1])
     total = None
     for at, weight, out in ((0, gate_w, gate_ref), (width, up_w, up_ref)):
         for s in range(shards):
@@ -464,44 +758,42 @@
             joined = jnp.concatenate(pieces, axis=1)
             here = slice(s * count * piece, (s + 1) * count * piece)
             out[:, here] = joined
-            term = jnp.sum(joined * weight[:, here].astype(f32), axis=1, keepdims=True)
-            total = term if total is None else total + term
+        term = jnp.sum(out[...] * weight[...].astype(f32), axis=1, keepdims=True)
+        total = term if total is None else total + term
     gain_out[...] = jnp.broadcast_to(total, (total.shape[0], 128)).T[:1] / gain_ref[...].astype(f32)
 
 
-def put_columns(place, blocks, w_gate, w_up, gain, shards):
-    count = len(blocks)
+def put_columns(place, blocks, far, w_gate, w_up, gain, shards):
+    count = len(blocks) + (1 if far else 0)
+    given = len(blocks) + len(far)
     rows, ff = w_gate.shape
     piece = ff // (shards * count)
     step = min(rows, 128)
     block = lambda last: pl.BlockSpec((step, last), lambda i, at: (i, 0))
     flat = pl.BlockSpec((1, step), lambda i, at: (0, i))
     return pl.pallas_call(
-        functools.partial(put_columns_kernel, shards, count, piece),
+        functools.partial(put_columns_kernel, shards, count, piece, given),
         grid_spec=pltpu.PrefetchScalarGridSpec(
             num_scalar_prefetch=1,
             grid=(rows // step,),
-            in_specs=[block(blocks[0].shape[1])] * count + [block(ff), block(ff), flat],
+            in_specs=block_specs(step, blocks, far) + [block(ff), block(ff), flat],
             out_specs=[block(ff), block(ff), flat],
+            scratch_shapes=[pltpu.VMEM((count, step, blocks[0].shape[1]), bf16)],
         ),
         out_shape=[
             jax.ShapeDtypeStruct((rows, ff), f32),
             jax.ShapeDtypeStruct((rows, ff), f32),
             jax.ShapeDtypeStruct((1, rows), f32),
         ],
-        compiler_params=pltpu.CompilerParams(vmem_limit_bytes=58 * 2**20),
-        cost_estimate=pl.CostEstimate(
-            flops=0, bytes_accessed=16 * rows * ff, transcendentals=0
-        ),
+        compiler_params=pltpu.CompilerParams(vmem_limit_bytes=58 * MIB),
+        cost_estimate=pl.CostEstimate(flops=1, bytes_accessed=1, transcendentals=0),
         name="put_columns",
-    )(place, *blocks, w_gate, w_up, gain)
-
-
-def put_attention_kernel(count, copies, width_q, place_ref, *refs):
-    block_refs = refs[:count]
-    q_w, k_w, v_w, gain_ref, q_ref, k_ref, v_ref, o_ref, gain_out = refs[count:]
-    blocks = [ref[...].astype(f32) for ref in block_refs]
-    blocks = sort_blocks(place_ref[0], blocks)
+    )(place, *blocks, *far, w_gate, w_up, gain)
+
+
+def put_attention_kernel(count, copies, width_q, given, place_ref, *refs):
+    q_w, k_w, v_w, gain_ref, q_ref, k_ref, v_ref, o_ref, gain_out = refs[given:-1]
+    blocks = read_blocks(place_ref[0], refs[:given], refs[-1])
     width_o = o_ref.shape[1] // count
     for a in range(count):
         q_ref[:, a * width_q : (a + 1) * width_q] = blocks[a][:, :width_q]
@@ -523,32 +815,32 @@
     gain_out[...] = jnp.broadcast_to(total, (total.shape[0], 128)).T[:1] / gain_ref[...].astype(f32)
 
 
-def put_attention(place, blocks, w_query, w_key, w_value, gain, width, copies):
-    count = len(blocks)
+def put_attention(place, blocks, far, w_query, w_key, w_value, gain, width, copies):
+    count = len(blocks) + (1 if far else 0)
+    given = len(blocks) + len(far)
     rows, wide_q = w_query.shape
     wide_k = w_key.shape[1]
     step = min(rows, 128)
     block = lambda last: pl.BlockSpec((step, last), lambda i, at: (i, 0))
     flat = pl.BlockSpec((1, step), lambda i, at: (0, i))
     return pl.pallas_call(
-        functools.partial(put_attention_kernel, count, copies, wide_q // count),
+        functools.partial(put_attention_kernel, count, copies, wide_q // count, given),
         grid_spec=pltpu.PrefetchScalarGridSpec(
             num_scalar_prefetch=1,
             grid=(rows // step,),
-            in_specs=[block(blocks[0].shape[1])] * count
+            in_specs=block_specs(step, blocks, far)
             + [block(wide_q), block(wide_k), block(wide_k), flat],
             out_specs=[block(wide_q), block(wide_k), block(wide_k), block(width), flat],
+            scratch_shapes=[pltpu.VMEM((count, step, blocks[0].shape[1]), bf16)],
         ),
         out_shape=[
             jax.ShapeDtypeStruct((rows, last), f32) for last in (wide_q, wide_k, wide_k, width)
         ]
         + [jax.ShapeDtypeStruct((1, rows), f32)],
-        compiler_params=pltpu.CompilerParams(vmem_limit_bytes=58 * 2**20),
-        cost_estimate=pl.CostEstimate(
-            flops=0, bytes_accessed=16 * rows * wide_q, transcendentals=0
-        ),
+        compiler_params=pltpu.CompilerParams(vmem_limit_bytes=32 * MIB),
+        cost_estimate=pl.CostEstimate(flops=1, bytes_accessed=1, transcendentals=0),
         name="put_attention",
-    )(place, *blocks, w_query, w_key, w_value, gain)
+    )(place, *blocks, *far, w_query, w_key, w_value, gain)
 
 
 def on_device(
@@ -592,10 +884,11 @@
             axis=1,
         )
     )
-    input_blocks, (gate_in, up_in) = gather_seq(mine, (w_gate, w_up))
+    input_near = gather_near(mine)
+    input_near, (gate_in, up_in) = tie(input_near, (w_gate, w_up))
+    input_blocks, input_far = gather_far(mine, input_near)
     w_gu = from_shards(take_columns(place_arg, gate_in, up_in, shards, count))
     w_dn = from_shards(lax.dynamic_slice_in_dim(w_down, place * piece, piece, axis=0))
-    inputs = jnp.stack(input_blocks)
 
     blocks_at = place ^ jnp.arange(count)
     positions = (blocks_at[:, None] * rows + jnp.arange(rows)[None, :]).astype(f32)
@@ -606,17 +899,20 @@
     cosine = jnp.cos(angles)
     sine = jnp.sin(angles) * jnp.where(lanes % HEAD_DIM < half_dim, -1.0, 1.0)
 
-    normed, queries, keys, values = project(inputs, gain_first, w_attn, cosine, sine, width_q)
+    normed, queries, keys, values = project(
+        [*input_blocks, *input_far], gain_first, w_attn, cosine, sine, width_q
+    )
     w_attn, queries = tie(w_attn, queries)
-    w_qkv, w_o_columns = w_attn[:, :width_qkv], w_attn[:, width_qkv:]
 
     w_o = jnp.zeros((width_q, width), bf16)
     for r in range(count):
-        rows_r = lax.dynamic_slice_in_dim(w_o_columns, (place ^ r) * width_q, width_q, axis=0)
+        rows_r = lax.dynamic_slice(
+            w_attn, ((place ^ r) * width_q, width_qkv), (width_q, part_d)
+        )
         rows_r = hop(rows_r, r) if r else rows_r
         w_o = lax.dynamic_update_slice_in_dim(w_o, rows_r, (place ^ r) * part_d, axis=1)
 
-    attended, logsum = attend(place_arg, queries, keys, values)
+    attended, attended_t, logsum = attend(place_arg, queries, keys, values)
     attended_rows = attended.reshape(length, width_q)
 
     def split(array):
@@ -629,31 +925,24 @@
     def to_owners(part):
         return lax.psum_scatter(part, "shard", scatter_dimension=0, tiled=True)
 
-    def norm_back(values_in, scale, gain, back):
-        branch = back * gain
-        return scale * (
-            branch - values_in * scale * scale * jnp.mean(branch * values_in, -1, keepdims=True)
-        )
-
-    middle = mine.astype(f32) + scatter_seq(
-        split(jnp.dot(attended_rows, w_o, preferred_element_type=f32))
-    )
-    scale_mid = rms_scale(middle)
-    normed_blocks = gather_seq((middle * scale_mid * gain_second).astype(bf16))
-    normed_blocks, cot = tie(normed_blocks, cotangent[0])
-    normed_mlp = jnp.concatenate(normed_blocks)
+    parts = split(jnp.dot(attended_rows, w_o, preferred_element_type=f32))
+    kept, arrived = scatter_pieces(scatter_turn(scatter_start(parts)))
+    middle, upper, lower = norm(kept, arrived, mine, gains[1:2])
+    normed_mlp = jnp.concatenate(gather_halves(upper, lower), axis=0)
+    normed_mlp, cot = tie(normed_mlp, cotangent[0])
+    cot_near = gather_near(cot)
     gate_up = jnp.dot(normed_mlp, w_gu, preferred_element_type=f32)
-    back_blocks, gate_up = gather_seq(cot, gate_up)
-    back_mlp = jnp.concatenate(back_blocks)
-
+    gate_up, cot_near = tie(gate_up, cot_near)
+    cot_blocks, cot_far = gather_far(cot, cot_near)
+    back_mlp = jnp.concatenate([*cot_blocks, *cot_far], axis=0)
     gate_lin, upward = gate_up[:, :width_f], gate_up[:, width_f:]
     sigmoid_gate = jax.nn.sigmoid(gate_lin)
     silu_gate = gate_lin * sigmoid_gate
     hidden = (silu_gate * upward).astype(bf16)
     down_part = token_sum(hidden, back_mlp)
+
+    w_dn, down_part = tie(w_dn, down_part)
     own_down = to_owners(down_part)
-
-    w_dn, down_part = tie(w_dn, down_part)
     out_parts = split(jnp.dot(hidden, w_dn, preferred_element_type=f32))
     w_dn, out_parts = tie(w_dn, out_parts)
     kept, turning, straight = scatter_start(out_parts)
@@ -673,57 +962,65 @@
     parts, turning, straight = scatter_start(parts)
     gu_part = token_sum(normed_mlp, back_gu)
     (turning, straight), gu_part = tie((turning, straight), gu_part)
-    back_normed_mlp = scatter_end(scatter_turn((parts, turning, straight)))
+    state = scatter_turn((parts, turning, straight))
     own_gu = to_owners(gu_part)
-
-    back_middle = cot.astype(f32) + norm_back(middle, scale_mid, gain_second, back_normed_mlp)
-    back_blocks = gather_seq(back_middle.astype(bf16))
-    back_blocks, own_down = tie(back_blocks, own_down)
-    back_branch = jnp.concatenate(back_blocks)
-
-    back_attended = jnp.einsum("td,qd->tq", back_branch, w_o, preferred_element_type=f32)
-    back_attended = back_attended.astype(bf16).reshape(count, rows, width_q)
-    out_part = token_sum(attended_rows, back_branch)
-    out_blocks = []
-    for r in range(count):
-        part_r = lax.dynamic_slice_in_dim(out_part, (place ^ r) * part_d, part_d, axis=1)
-        out_blocks.append(hop(part_r, r) if r else part_r)
-    down_blocks = gather_direct(own_down)
+    kept, arrived = scatter_pieces(state)
+
+    back_middle, upper, lower = norm_back(kept, arrived, middle, cot, gains[1:2], True)
+    pieces, own_down = tie(gather_halves(upper, lower), own_down)
+    back_attended, *out_blocks = branch(place_arg, pieces, w_o, attended_t)
+    out_blocks = [hop(one, r) if r else one for r, one in enumerate(out_blocks)]
+    down_near = gather_near(own_down)
     back_query, back_kv = attend_back(
         place_arg, queries, keys, values, attended, back_attended, logsum, cosine, sine
     )
-    back_query, (out_blocks, down_blocks) = tie(back_query, (out_blocks, down_blocks))
-    back_qkv = jnp.concatenate([back_query, back_kv], axis=2).reshape(length, -1)
-
-    attn_part = jnp.pad(
-        token_sum(normed.reshape(length, width), back_qkv), ((0, 0), (0, part_d))
+    back_query, (out_blocks, down_near) = tie(back_query, (out_blocks, down_near))
+    back_query, back_kv = back_query.reshape(length, -1), back_kv.reshape(length, -1)
+    parts = input_grads(back_query, back_kv, w_attn)
+    down_blocks, down_far = gather_far(own_down, down_near)
+    if count == 4:
+        turning = (hop(parts[3], 1), hop(parts[4], 2))
+        parts, back_query = tie(parts, back_query)
+    attn_part = attention_grads(
+        place_arg, normed.reshape(length, width), back_query, back_kv, out_blocks
     )
-    for r in range(count):
-        attn_part = lax.dynamic_update_slice(
-            attn_part, out_blocks[r], ((place ^ r) * width_q, width_qkv)
-        )
+    if count == 4:
+        (turning, down_far), attn_part = tie((turning, down_far), attn_part)
     attn_part, own_gu = tie(attn_part, own_gu)
     own_attn = to_owners(attn_part)
-
-    parts = split(jnp.einsum("tq,dq->td", back_qkv, w_qkv, preferred_element_type=f32))
-    back_normed = scatter_seq(parts)
-    back_normed, own_gu = tie(back_normed, own_gu)
-    mine_in = mine.astype(f32)
-    grad_tokens = back_middle + norm_back(
-        mine_in, rms_scale(mine_in), gain_first.astype(f32), back_normed
+    gu_near = gather_near(own_gu)
+    if count == 4:
+        to_near = turn(parts[1:3], turning)
+        to_near, gu_near = tie(to_near, gu_near)
+        kept, arrived = parts[0], (hop(to_near[0], 1), hop(to_near[1], 2))
+    else:
+        kept, arrived = scatter_pieces(scatter_turn(scatter_start(parts)))
+    gu_blocks, gu_far = gather_far(own_gu, gu_near)
+    arrived, own_attn = tie(arrived, own_attn)
+    attn_blocks = [own_attn] + [hop(own_attn, r) for r in range(1, count)]
+    (grad_tokens,) = norm_back(kept, arrived, mine, back_middle, gain_first, False)
+    gu_far, grad_tokens = tie(gu_far, grad_tokens)
+
+    grad_down = jnp.zeros((count * piece, width), f32)
+    places = [((place ^ r) * piece, block) for r, block in enumerate(down_blocks)]
+    for at, block in enumerate(down_far):
+        places.append(((place ^ (count - 1)) * piece + at * (piece // 2), block))
+    for at, block in places:
+        grad_down = lax.dynamic_update_slice_in_dim(grad_down, block.astype(f32), at, axis=0)
+    grad_gate, grad_up, grad_gain_mlp = put_columns(
+        place_arg,
+        gu_blocks,
+        gu_far,
+        w_gate,
+        w_up,
+        gain_mlp.reshape(1, -1),
+        shards,
     )
-
-    grad_down = jnp.zeros((count * piece, width), f32)
-    for r, block in enumerate(down_blocks):
-        grad_down = lax.dynamic_update_slice_in_dim(
-            grad_down, block.astype(f32), (place ^ r) * piece, axis=0
-        )
-    grad_gate, grad_up, grad_gain_mlp = put_columns(
-        place_arg, gather_seq(own_gu), w_gate, w_up, gain_mlp.reshape(1, -1), shards
-    )
+    attn_blocks, (grad_gate, grad_up) = tie(attn_blocks, (grad_gate, grad_up))
     grad_query, grad_key, grad_value, grad_out, grad_gain_attn = put_attention(
         place_arg,
-        gather_seq(own_attn),
+        attn_blocks,
+        (),
         w_query,
         w_key,
         w_value,

time: 568 us -> 545 us (0.960)
  Pallas kernels: 69.9 us -> 108 us
  other arithmetic: 47.1 us -> 24.4 us
  matrix products: 97.7 us -> 81.5 us
  waiting for transfers between devices: 190 us -> 175 us
  starting transfers between devices: 72 us -> 62.9 us
    pallas_call x1 -> x8, Pallas kernels: 7.57 us -> 54 us  [the longest x2 11.4 us: norm_back(): pl.pallas_call(functools.partial(norm_back_kernel, len(arrived)), grid=(4...]
    concatenate x12 -> x0, other arithmetic: 14.6 us -> none  [the longest x4 5.56 us: gather_seq(): blocks.append(jnp.concatenate([near_upper, near_lower], axis=0))]
    ppermute x69 -> x59, waiting for transfers between devices: 190 us -> 175 us  [hop(): return lax.ppermute(value, 'seq', [(i, i ^ bit) for i in range(count)])]
    dot_general x4 -> x2, matrix products: 32.1 us -> 23.2 us  [token_sum(): jnp.einsum('tf,td->fd', left, right, preferred_element_type=f32)]
    ppermute x69 -> x59, starting transfers between devices: 71.1 us -> 62.7 us  [hop(): return lax.ppermute(value, 'seq', [(i, i ^ bit) for i in range(count)])]
    dot_general x3 -> x1, matrix products: 10.4 us -> 2.34 us  [on_device(): parts = split(jnp.dot(attended_rows, w_o, preferred_element_type=f32))]
    another operation x4 -> x0, other arithmetic: 6.22 us -> none  [on_device(): inputs = jnp.stack(input_blocks)]
    pallas_call x1, Pallas kernels: 27.2 us -> 21 us  [attend_back(): pl.pallas_call(functools.partial(attend_back_kernel, count, rows), grid_s...]
  transfers between devices with their start and end apart: 75 -> 65, of which waited for: 36 -> 36; matrix products, arithmetic and copies ran while one was open for 32% -> 24% of each run, Pallas kernels for 12% -> 19%
where the time goes in v4:
time: 545 us; the launch traced here: 540 us
  waiting for transfers between devices  175 us (32%)
  Pallas kernels  108 us (20%)
  matrix products  81.5 us (15%)
  starting transfers between devices  62.9 us (12%)
  local copies, waits for them, and re-layouts  60.2 us (11%)
  other arithmetic  24.4 us (4%)
  between operations  15.2 us (3%)
  blocking collectives  12.5 us (2%)
    ppermute x59, waiting for transfers between devices, hop(): return lax.ppermute(value, 'seq', [(i, i ^ bit) for i in range(count)])  175 us
    ppermute x59, starting transfers between devices, hop(): return lax.ppermute(value, 'seq', [(i, i ^ bit) for i in range(count)])  62.7 us
    unnamed x133, local copies, waits for them, and re-layouts  27.2 us
    dot_general x2, matrix products, token_sum(): jnp.einsum('tf,td->fd', left, right, preferred_element_type=f32)  23.2 us
    pallas_call x1, Pallas kernels, attend_back(): pl.pallas_call(functools.partial(attend_back_kernel, count, rows), grid_s...  21 us
    pallas_call x1, Pallas kernels, attend(): pl.pallas_call(functools.partial(attend_kernel, count, rows), grid_spec=p...  17.7 us
    dot_general x1, matrix products, on_device(): gate_up = jnp.dot(normed_mlp, w_gu, preferred_element_type=f32)  17.4 us
    dot_general x1, matrix products, on_device(): jnp.einsum('tf,df->td', back_gu, w_gu, preferred_element_type=f32)  15 us
  transfers between devices with their start and end apart: 65, of which 36 were waited for; matrix products, arithmetic and copies ran while one was open for 24% of the time, Pallas kernels for 19%

profile of v4, /device:TPU:0, one launch (start us, length us, event | category | flops | bytes accessed | tf_op | source)
XLA Modules:
  0.0 540.2 jit_solution(3891219479538059449)
XLA Ops:
  15.0 21.9 %collective-permute-done.refs_1_ = bf16[256,2048]{1,0:T(8,128)(2,1)S(1)} collective-permute-done((bf16[256,2048]{1,0:T(8,128)(2,1)}, bf16[256,2048]{1,0:T(8,128)(2,1)S(1)}, u32[]{:S(2)}, u32[]{:S(2)}) %collective-permute-start) | collective-permute-done | bytes 1048608 | tf_op jit(solution)/shard_map/ppermute | solution.py:29
  53.2 12.5 %all_gather.13 = bf16[2,2048]{1,0:T(2,128)(2,1)S(1)} all-gather(bf16[2,256]{1,0:T(2,128)(2,1)S(1)} %pad_maximum_fusion.1), channel_id=1, replica_groups=mesh['seq'=4,'shard'=8] {'shard'}, dimensions={1}, use_global_device_ids=true | all-gather | bytes 9216 | tf_op jit(solution)/shard_map/all_gather | solution.py:874
  66.4 10.1 %project.1 = (bf16[4,256,2048]{2,1,0:T(8,128)(2,1)}, bf16[4,256,512]{2,1,0:T(8,128)(2,1)}, bf16[4,256,128]{2,1,0:T(8,128)(2,1)}, bf16[4,256,128]{2,1,0:T(8,128)(2,1)}) custom-call(bf16[256,2048]{1,0:T(8,128)(2,1)} %bitcast.33, bf16[256,2048]{1,0:T(8,128)(2,1)} %copy-done.35, bf16[256,2048]{1,0:T(8,128)(2,1)} %copy-done.36, ...), custom_call_target="tpu_custom_call" | custom-call | flops 1 | bytes 1 | tf_op jit(solution)/shard_map/project/pallas_call | solution.py:442
  82.5 17.7 %attend.1 = (bf16[4,256,512]{2,1,0:T(8,128)(2,1)S(1)}, bf16[512,1024]{1,0:T(8,128)(2,1)S(1)}, f32[4,4,8,256]{3,2,1,0:T(8,128)S(1)}) custom-call(s32[1]{0:T(128)} %bitcast.place_ref, bf16[4,256,512]{2,1,0:T(8,128)(2,1)S(1)} %copy-done.8, bf16[4,256,128]{2,1,0:T(8,128)(2,1)S(1)} %copy-done.19, bf16[4,256,128]{2,1,0:T(8,128)(2,1)S(1)} %copy-done.20), custom_call_target="tpu_custom_call" | custom-call | flops 1 | bytes 1 | tf_op jit(solution)/shard_map/attend/pallas_call | solution.py:537
  101.3 4.1 collective-permute-done.5
  113.4 10.8 %collective-permute-done.10 = bf16[128,2048]{1,0:T(8,128)(2,1)S(1)} collective-permute-done((bf16[128,2048]{1,0:T(8,128)(2,1)S(1)}, bf16[128,2048]{1,0:T(8,128)(2,1)S(1)}, u32[]{:S(2)}, u32[]{:S(2)}) %collective-permute-start.10) | collective-permute-done | bytes 524320 | tf_op jit(solution)/shard_map/ppermute | solution.py:29
  130.6 4.9 collective-permute-done.7.refs_0_
  136.2 8.8 %collective-permute-done.9.refs_1_ = bf16[128,2048]{1,0:T(8,128)(2,1)} collective-permute-done((bf16[128,2048]{1,0:T(8,128)(2,1)}, bf16[128,2048]{1,0:T(8,128)(2,1)}, u32[]{:S(2)}, u32[]{:S(2)}) %collective-permute-start.9) | collective-permute-done | bytes 524320 | tf_op jit(solution)/shard_map/ppermute | solution.py:29
  145.4 5.1 norm.1
  157.8 7.8 %collective-permute-done.13 = bf16[128,2048]{1,0:T(8,128)(2,1)} collective-permute-done((bf16[128,2048]{1,0:T(8,128)(2,1)}, bf16[128,2048]{1,0:T(8,128)(2,1)}, u32[]{:S(2)}, u32[]{:S(2)}) %collective-permute-start.13) | collective-permute-done | bytes 524320 | tf_op jit(solution)/shard_map/ppermute | solution.py:29
  168.8 8.0 %collective-permute-done.14 = bf16[128,2048]{1,0:T(8,128)(2,1)S(1)} collective-permute-done((bf16[128,2048]{1,0:T(8,128)(2,1)}, bf16[128,2048]{1,0:T(8,128)(2,1)S(1)}, u32[]{:S(2)}, u32[]{:S(2)}) %collective-permute-start.14) | collective-permute-done | bytes 524320 | tf_op jit(solution)/shard_map/ppermute | solution.py:29
  179.3 7.0 %collective-permute-done.17 = bf16[128,2048]{1,0:T(8,128)(2,1)S(1)} collective-permute-done((bf16[128,2048]{1,0:T(8,128)(2,1)}, bf16[128,2048]{1,0:T(8,128)(2,1)S(1)}, u32[]{:S(2)}, u32[]{:S(2)}) %collective-permute-start.17) | collective-permute-done | bytes 524320 | tf_op jit(solution)/shard_map/ppermute | solution.py:29
  191.2 17.4 %fusion.16 = f32[1024,2816]{1,0:T(8,128)S(1)} fusion(bf16[1024,2048]{1,0:T(8,128)(2,1)} %copy-done.56, bf16[2048,2816]{1,0:T(8,128)(2,1)} %all-gather.8.cloned.1.call-done), kind=kOutput, calls=%fused_computation.72 | convolution fusion | flops 11811160064 | bytes 27262976 | tf_op jit(solution)/shard_map/dot_general | solution.py:934
  228.0 8.0 %convolution_convert_fusion.1 = bf16[1408,2048]{1,0:T(8,128)(2,1)} fusion(bf16[1024,1408]{1,0:T(8,128)(2,1)S(1)} %multiply_convert_fusion, bf16[1024,2048]{1,0:T(8,128)(2,1)S(1)} %constant_dynamic-update-slice_fusion.8), kind=kOutput, calls=%fused_computation.1 | convolution fusion | flops 5908463616 | bytes 12845056 | tf_op jit(solution)/shard_map/tf,td->fd/dot_general | solution.py:923
  236.0 8.7 %convolution_convert_fusion.4 = bf16[1024,2048]{1,0:T(8,128)(2,1)S(1)} fusion(bf16[1024,1408]{1,0:T(8,128)(2,1)S(1)} %multiply_convert_fusion, bf16[1408,2048]{1,0:T(8,128)(2,1)} %all-gather.6.cloned.1.call-done), kind=kOutput, calls=%fused_computation.14 | convolution fusion | flops 5907677184 | bytes 12845056 | tf_op jit(solution)/shard_map/dot_general | solution.py:946
  249.8 14.9 %fusion.2 = (bf16[1024,1408]{1,0:T(8,128)(2,1)S(1)}, bf16[1024,1408]{1,0:T(8,128)(2,1)S(1)}) fusion(f32[1024,2816]{1,0:T(8,128)} %copy-done.27, bf16[1024,2048]{1,0:T(8,128)(2,1)} %copy-done.55, bf16[1408,2048]{1,0:T(8,128)(2,1)} %all-gather.6.cloned.1.call-done), kind=kOutput, calls=%fused_computation.6 | convolution fusion | flops 5927206912 | bytes 27262976 | tf_op jit(solution)/shard_map/td,fd->tf/dot_general | solution.py:950
  273.3 15.0 %convolution_convert_fusion.2 = bf16[1024,2048]{1,0:T(8,128)(2,1)S(1)} fusion(bf16[1024,2816]{1,0:T(8,128)(2,1)S(1)} %pad_maximum_fusion, bf16[2048,2816]{1,0:T(8,128)(2,1)} %all-gather.8.cloned.1.call-done), kind=kOutput, calls=%fused_computation.12 | convolution fusion | flops 11813257216 | bytes 21495808 | tf_op jit(solution)/shard_map/tf,df->td/dot_general | solution.py:959
  297.3 15.2 %convolution_convert_fusion = bf16[2048,2816]{1,0:T(8,128)(2,1)} fusion(bf16[1024,2048]{1,0:T(8,128)(2,1)S(1)} %copy-done.57, bf16[1024,2816]{1,0:T(8,128)(2,1)S(1)} %pad_maximum_fusion), kind=kOutput, calls=%fused_computation | convolution fusion | flops 11816927232 | bytes 21495808 | tf_op jit(solution)/shard_map/tf,td->fd/dot_general | solution.py:923
  319.3 8.5 %collective-permute-done.33.refs_5_ = bf16[128,2048]{1,0:T(8,128)(2,1)S(1)} collective-permute-done((bf16[128,2048]{1,0:T(8,128)(2,1)S(1)}, bf16[128,2048]{1,0:T(8,128)(2,1)S(1)}, u32[]{:S(2)}, u32[]{:S(2)}) %collective-permute-start.33) | collective-permute-done | bytes 524320 | tf_op jit(solution)/shard_map/ppermute | solution.py:29
  330.0 6.2 %norm_back.2 = (f32[256,2048]{1,0:T(8,128)}, bf16[128,2048]{1,0:T(8,128)(2,1)}, bf16[128,2048]{1,0:T(8,128)(2,1)}) custom-call(bf16[256,2048]{1,0:T(8,128)(2,1)} %get-tuple-element.155.refs_0_, f32[256,2048]{1,0:T(8,128)} %get-tuple-element.131.refs_1_, bf16[256,2048]{1,0:T(8,128)(2,1)} %bitcast.37, bf16[1,2048]{1,0:T(2,128)(2,1)} %get-tuple-element.259.gain_ref.refs_3_, ...), custom_call_target="tpu_custom_call" | custom-call | flops 1 | bytes 1 | tf_op jit(solution)/shard_map/norm_back/pallas_call | solution.py:388
  340.4 11.0 %collective-permute-done.35.refs_2_ = bf16[128,2048]{1,0:T(8,128)(2,1)S(1)} collective-permute-done((bf16[128,2048]{1,0:T(8,128)(2,1)}, bf16[128,2048]{1,0:T(8,128)(2,1)S(1)}, u32[]{:S(2)}, u32[]{:S(2)}) %collective-permute-start.35) | collective-permute-done | bytes 524320 | tf_op jit(solution)/shard_map/ppermute | solution.py:29
  353.5 9.2 %collective-permute-done.36.refs_3_ = bf16[128,2048]{1,0:T(8,128)(2,1)S(1)} collective-permute-done((bf16[128,2048]{1,0:T(8,128)(2,1)}, bf16[128,2048]{1,0:T(8,128)(2,1)S(1)}, u32[]{:S(2)}, u32[]{:S(2)}) %collective-permute-start.36) | collective-permute-done | bytes 524320 | tf_op jit(solution)/shard_map/ppermute | solution.py:29
  363.9 6.8 %collective-permute-done.39.refs_6_ = bf16[128,2048]{1,0:T(8,128)(2,1)S(1)} collective-permute-done((bf16[128,2048]{1,0:T(8,128)(2,1)S(1)}, bf16[128,2048]{1,0:T(8,128)(2,1)S(1)}, u32[]{:S(2)}, u32[]{:S(2)}) %collective-permute-start.39) | collective-permute-done | bytes 524320 | tf_op jit(solution)/shard_map/ppermute | solution.py:29
  372.3 10.5 %branch.1 = (bf16[4,256,512]{2,1,0:T(8,128)(2,1)}, bf16[512,512]{1,0:T(8,128)(2,1)}, bf16[512,512]{1,0:T(8,128)(2,1)}, bf16[512,512]{1,0:T(8,128)(2,1)}, bf16[512,512]{1,0:T(8,128)(2,1)}) custom-call(s32[1]{0:T(128)} %bitcast.place_ref, bf16[512,2048]{1,0:T(8,128)(2,1)} %copy-done.29, bf16[512,1024]{1,0:T(8,128)(2,1)} %copy-done.21, ...), custom_call_target="tpu_custom_call" | custom-call | flops 1 | bytes 1 | tf_op jit(solution)/shard_map/branch/pallas_call | solution.py:183
  388.8 21.0 %attend_back.1 = (bf16[4,256,512]{2,1,0:T(8,128)(2,1)S(1)}, bf16[4,256,128]{2,1,0:T(8,128)(2,1)S(1)}) custom-call(s32[1]{0:T(128)} %bitcast.place_ref, bf16[4,256,512]{2,1,0:T(8,128)(2,1)S(1)} %copy-done.9, bf16[4,256,128]{2,1,0:T(8,128)(2,1)S(1)} %copy-done.19, bf16[4,256,128]{2,1,0:T(8,128)(2,1)S(1)} %copy-done.20, bf16[4,256,512]{2,1,0:T(8,128)(2,1)S(1)} %copy-done.13, ...), custom_call_target="tpu_custom_call" | custom-call | flops 1 | bytes 1 | tf_op jit(solution)/shard_map/attend_back/pallas_call | solution.py:656
  413.2 5.2 input_grads.1
  427.0 8.4 %attention_grads.1 = bf16[2048,1152]{1,0:T(8,128)(2,1)} custom-call(s32[1]{0:T(128)} %bitcast.place_ref, bf16[1024,2048]{1,0:T(8,128)(2,1)} %bitcast.36, bf16[1024,512]{1,0:T(8,128)(2,1)} %bitcast.27, bf16[1024,128]{1,0:T(8,128)(2,1)} %bitcast.30, bf16[512,512]{1,0:T(8,128)(2,1)} %get-tuple-element.195.refs_0_, bf16[512,512]{1,0:T(8,128)(2,1)} %copy-done.44, ...), custom_call_target="tpu_custom_call" | custom-call | flops 1 | bytes 1 | tf_op jit(solution)/shard_map/attention_grads/pallas_call | solution.py:229
  445.4 21.9 %collective-permute-done.50.refs_1_ = bf16[256,2816]{1,0:T(8,128)(2,1)} collective-permute-done((bf16[256,2816]{1,0:T(8,128)(2,1)}, bf16[256,2816]{1,0:T(8,128)(2,1)}, u32[]{:S(2)}, u32[]{:S(2)}) %collective-permute-start.50) | collective-permute-done | bytes 1441824 | tf_op jit(solution)/shard_map/ppermute | solution.py:29
  484.4 9.7 %collective-permute-done.54.refs_4_ = bf16[256,2048]{1,0:T(8,128)(2,1)S(1)} collective-permute-done((bf16[256,2048]{1,0:T(8,128)(2,1)}, bf16[256,2048]{1,0:T(8,128)(2,1)S(1)}, u32[]{:S(2)}, u32[]{:S(2)}) %collective-permute-start.54) | collective-permute-done | bytes 1048608 | tf_op jit(solution)/shard_map/ppermute | solution.py:29
  501.7 5.2 norm_back.3
  509.7 11.2 %put_columns.1 = (f32[256,5632]{1,0:T(8,128)}, f32[256,5632]{1,0:T(8,128)}, f32[1,256]{1,0:T(1,128)}) custom-call(s32[1]{0:T(128)} %bitcast.place_ref, bf16[256,2816]{1,0:T(8,128)(2,1)} %reduce-scatter.6.cloned.1.call-done.refs_0_, bf16[256,2816]{1,0:T(8,128)(2,1)} %collective-permute-done.50.refs_1_, bf16[256,2816]{1,0:T(8,128)(2,1)} %collective-permute-done.51.refs_2_, ...), custom_call_target="tpu_custom_call" | custom-call | flops 1 | bytes 1 | tf_op jit(solution)/shard_map/put_columns/pallas_call | solution.py:774
  521.8 5.9 %collective-permute-done.57.refs_2_ = bf16[256,1152]{1,0:T(8,128)(2,1)} collective-permute-done((bf16[256,1152]{1,0:T(8,128)(2,1)}, bf16[256,1152]{1,0:T(8,128)(2,1)}, u32[]{:S(2)}, u32[]{:S(2)}) %collective-permute-start.57) | collective-permute-done | bytes 589856 | tf_op jit(solution)/shard_map/ppermute | solution.py:29
  (309 shorter events, 186.4 us)
Async XLA Ops:
  7.2 59.2 %all-gather.4.cloned.1.call-start = ((), (), s32[]{:S(2)}) async-start(), calls=%async_computation.3 | async-start | bytes 5308416 | tf_op jit(solution)/shard_map/all_gather | solution.py:869
  10.5 180.8 %all-gather.8.cloned.1.call-start = ((), (), s32[]{:S(2)}) async-start(), calls=%async_computation.5 | async-start | bytes 12976128 | tf_op jit(solution)/shard_map/all_gather | solution.py:869
  10.5 26.4 %collective-permute-start = (bf16[256,2048]{1,0:T(8,128)(2,1)}, bf16[256,2048]{1,0:T(8,128)(2,1)S(1)}, u32[]{:S(2)}, u32[]{:S(2)}) collective-permute-start(bf16[256,2048]{1,0:T(8,128)(2,1)} %bitcast.31), channel_id=1, source_target_pairs={{0,8},{8,0},{16,24},{24,16},{1,9},{9,1},{17,25},{25,17},{2,10},{10... | collective-permute-start | bytes 3145736 | tf_op jit(solution)/shard_map/ppermute | solution.py:29
  13.5 24.8 %collective-permute-start.1 = (bf16[256,2048]{1,0:T(8,128)(2,1)}, bf16[256,2048]{1,0:T(8,128)(2,1)S(1)}, u32[]{:S(2)}, u32[]{:S(2)}) collective-permute-start(bf16[256,2048]{1,0:T(8,128)(2,1)} %bitcast.32), channel_id=1, source_target_pairs={{0,16},{8,24},{16,0},{24,8},{1,17},{9,25},{17,1},{25,9},{2,18},{10... | collective-permute-start | bytes 3145736 | tf_op jit(solution)/shard_map/ppermute | solution.py:29
  44.9 191.1 %all-gather.6.cloned.1.call-start = ((), (), s32[]{:S(2)}) async-start(), calls=%async_computation.4 | async-start | bytes 6488064 | tf_op jit(solution)/shard_map/all_gather | solution.py:869
  78.9 22.3 %collective-permute-start.4 = (bf16[512,512]{1,0:T(8,128)(2,1)S(1)}, bf16[512,512]{1,0:T(8,128)(2,1)S(1)}, u32[]{:S(2)}, u32[]{:S(2)}) collective-permute-start(bf16[512,512]{1,0:T(8,128)(2,1)S(1)} %get-tuple-element.239), channel_id=1, source_target_pairs={{0,8},{8,0},{16,24},{24,16},{1,9},{9,1},{17,25},{25,17},{2,10},{10... | collective-permute-start | bytes 1572872 | tf_op jit(solution)/shard_map/ppermute | solution.py:29
  80.4 25.0 %collective-permute-start.5 = (bf16[512,512]{1,0:T(8,128)(2,1)S(1)}, bf16[512,512]{1,0:T(8,128)(2,1)S(1)}, u32[]{:S(2)}, u32[]{:S(2)}) collective-permute-start(bf16[512,512]{1,0:T(8,128)(2,1)S(1)} %get-tuple-element.238), channel_id=1, source_target_pairs={{0,16},{8,24},{16,0},{24,8},{1,17},{9,25},{17,1},{25,9},{2,18},{10... | collective-permute-start | bytes 1572872 | tf_op jit(solution)/shard_map/ppermute | solution.py:29
  81.0 24.4 %collective-permute-start.6 = (bf16[512,512]{1,0:T(8,128)(2,1)S(1)}, bf16[512,512]{1,0:T(8,128)(2,1)S(1)}, u32[]{:S(2)}, u32[]{:S(2)}) collective-permute-start(bf16[512,512]{1,0:T(8,128)(2,1)S(1)} %get-tuple-element.237), channel_id=1, source_target_pairs={{0,24},{8,16},{16,8},{24,0},{1,25},{9,17},{17,9},{25,1},{2,26},{10... | collective-permute-start | bytes 1572872 | tf_op jit(solution)/shard_map/ppermute | solution.py:29
  111.3 24.2 %collective-permute-start.7 = (bf16[128,2048]{1,0:T(8,128)(2,1)}, bf16[128,2048]{1,0:T(8,128)(2,1)}, u32[]{:S(2)}, u32[]{:S(2)}) collective-permute-start(bf16[128,2048]{1,0:T(8,128)(2,1)} %get-tuple-element.252), channel_id=1, source_target_pairs={{0,8},{8,0},{16,24},{24,16},{1,9},{9,1},{17,25},{25,17},{2,10},{10... | collective-permute-start | bytes 1572872 | tf_op jit(solution)/shard_map/ppermute | solution.py:29
  112.0 24.2 %collective-permute-start.12 = (bf16[128,2048]{1,0:T(8,128)(2,1)}, bf16[128,2048]{1,0:T(8,128)(2,1)}, u32[]{:S(2)}, u32[]{:S(2)}) collective-permute-start(bf16[128,2048]{1,0:T(8,128)(2,1)} %get-tuple-element.249), channel_id=1, source_target_pairs={{0,16},{8,24},{16,0},{24,8},{1,17},{9,25},{17,1},{25,9},{2,18},{10... | collective-permute-start | bytes 1572872 | tf_op jit(solution)/shard_map/ppermute | solution.py:29
  153.5 218.0 %reduce-scatter.4.cloned.1.call-start = ((), (), s32[]{:S(2)}) async-start(), calls=%async_computation.6 | async-start | bytes 6488064 | tf_op jit(solution)/shard_map/reduce_scatter | solution.py:926
  153.6 23.2 %collective-permute-start.14 = (bf16[128,2048]{1,0:T(8,128)(2,1)}, bf16[128,2048]{1,0:T(8,128)(2,1)S(1)}, u32[]{:S(2)}, u32[]{:S(2)}) collective-permute-start(bf16[128,2048]{1,0:T(8,128)(2,1)} %get-tuple-element.133), channel_id=1, source_target_pairs={{0,8},{8,0},{16,24},{24,16},{1,9},{9,1},{17,25},{25,17},{2,10},{10... | collective-permute-start | bytes 1572872 | tf_op jit(solution)/shard_map/ppermute | solution.py:29
  249.7 185.7 %reduce-scatter.6.cloned.1.call-start = ((), (), s32[]{:S(2)}) async-start(), calls=%async_computation.7 | async-start | bytes 12976128 | tf_op jit(solution)/shard_map/reduce_scatter | solution.py:926
  265.5 24.4 %collective-permute-start.27 = (bf16[128,2048]{1,0:T(8,128)(2,1)}, bf16[128,2048]{1,0:T(8,128)(2,1)S(1)}, u32[]{:S(2)}, u32[]{:S(2)}) collective-permute-start(bf16[128,2048]{1,0:T(8,128)(2,1)} %slice.154), channel_id=1, source_target_pairs={{0,8},{8,0},{16,24},{24,16},{1,9},{9,1},{17,25},{25,17},{2,10},{10... | collective-permute-start | bytes 1572872 | tf_op jit(solution)/shard_map/ppermute | solution.py:29
  266.9 22.9 %collective-permute-start.28 = (bf16[128,2048]{1,0:T(8,128)(2,1)}, bf16[128,2048]{1,0:T(8,128)(2,1)S(1)}, u32[]{:S(2)}, u32[]{:S(2)}) collective-permute-start(bf16[128,2048]{1,0:T(8,128)(2,1)} %slice.155), channel_id=1, source_target_pairs={{0,16},{8,24},{16,0},{24,8},{1,17},{9,25},{17,1},{25,9},{2,18},{10... | collective-permute-start | bytes 1572872 | tf_op jit(solution)/shard_map/ppermute | solution.py:29
  316.1 178.3 %reduce-scatter.8.cloned.1.call-start = ((), (), s32[]{:S(2)}) async-start(), calls=%async_computation.8 | async-start | bytes 5308416 | tf_op jit(solution)/shard_map/reduce_scatter | solution.py:926
  338.1 24.6 %collective-permute-start.36 = (bf16[128,2048]{1,0:T(8,128)(2,1)}, bf16[128,2048]{1,0:T(8,128)(2,1)S(1)}, u32[]{:S(2)}, u32[]{:S(2)}) collective-permute-start(bf16[128,2048]{1,0:T(8,128)(2,1)} %get-tuple-element.167.refs_1_), channel_id=1, source_target_pairs={{0,8},{8,0},{16,24},{24,16},{1,9},{9,1},{17,25},{25,17},{2,10},{10... | collective-permute-start | bytes 1572872 | tf_op jit(solution)/shard_map/ppermute | solution.py:29
  338.7 25.3 %collective-permute-start.37 = (bf16[128,2048]{1,0:T(8,128)(2,1)}, bf16[128,2048]{1,0:T(8,128)(2,1)S(1)}, u32[]{:S(2)}, u32[]{:S(2)}) collective-permute-start(bf16[128,2048]{1,0:T(8,128)(2,1)} %get-tuple-element.166.refs_0_), channel_id=1, source_target_pairs={{0,16},{8,24},{16,0},{24,8},{1,17},{9,25},{17,1},{25,9},{2,18},{10... | collective-permute-start | bytes 1572872 | tf_op jit(solution)/shard_map/ppermute | solution.py:29
  371.6 38.3 %collective-permute-start.44 = (bf16[176,2048]{1,0:T(8,128)(2,1)}, bf16[176,2048]{1,0:T(8,128)(2,1)}, u32[]{:S(2)}, u32[]{:S(2)}) collective-permute-start(bf16[176,2048]{1,0:T(8,128)(2,1)} %reduce-scatter.4.cloned.1.call-done), channel_id=1, source_target_pairs={{0,8},{8,0},{16,24},{24,16},{1,9},{9,1},{17,25},{25,17},{2,10},{10... | collective-permute-start | bytes 2162696 | tf_op jit(solution)/shard_map/ppermute | solution.py:29
  372.1 37.8 %collective-permute-start.45 = (bf16[176,2048]{1,0:T(8,128)(2,1)}, bf16[176,2048]{1,0:T(8,128)(2,1)}, u32[]{:S(2)}, u32[]{:S(2)}) collective-permute-start(bf16[176,2048]{1,0:T(8,128)(2,1)} %reduce-scatter.4.cloned.1.call-done), channel_id=1, source_target_pairs={{0,16},{8,24},{16,0},{24,8},{1,17},{9,25},{17,1},{25,9},{2,18},{10... | collective-permute-start | bytes 2162696 | tf_op jit(solution)/shard_map/ppermute | solution.py:29
  382.8 27.0 %collective-permute-start.41 = (bf16[512,512]{1,0:T(8,128)(2,1)}, bf16[512,512]{1,0:T(8,128)(2,1)S(1)}, u32[]{:S(2)}, u32[]{:S(2)}) collective-permute-start(bf16[512,512]{1,0:T(8,128)(2,1)} %get-tuple-element.178), channel_id=1, source_target_pairs={{0,8},{8,0},{16,24},{24,16},{1,9},{9,1},{17,25},{25,17},{2,10},{10... | collective-permute-start | bytes 1572872 | tf_op jit(solution)/shard_map/ppermute | solution.py:29
  384.4 25.5 %collective-permute-start.42 = (bf16[512,512]{1,0:T(8,128)(2,1)}, bf16[512,512]{1,0:T(8,128)(2,1)S(1)}, u32[]{:S(2)}, u32[]{:S(2)}) collective-permute-start(bf16[512,512]{1,0:T(8,128)(2,1)} %get-tuple-element.179), channel_id=1, source_target_pairs={{0,16},{8,24},{16,0},{24,8},{1,17},{9,25},{17,1},{25,9},{2,18},{10... | collective-permute-start | bytes 1572872 | tf_op jit(solution)/shard_map/ppermute | solution.py:29
  386.2 23.7 %collective-permute-start.43 = (bf16[512,512]{1,0:T(8,128)(2,1)}, bf16[512,512]{1,0:T(8,128)(2,1)S(1)}, u32[]{:S(2)}, u32[]{:S(2)}) collective-permute-start(bf16[512,512]{1,0:T(8,128)(2,1)} %get-tuple-element.180), channel_id=1, source_target_pairs={{0,24},{8,16},{16,8},{24,0},{1,25},{9,17},{17,9},{25,1},{2,26},{10... | collective-permute-start | bytes 1572872 | tf_op jit(solution)/shard_map/ppermute | solution.py:29
  435.5 31.8 %collective-permute-start.50 = (bf16[256,2816]{1,0:T(8,128)(2,1)}, bf16[256,2816]{1,0:T(8,128)(2,1)}, u32[]{:S(2)}, u32[]{:S(2)}) collective-permute-start(bf16[256,2816]{1,0:T(8,128)(2,1)} %reduce-scatter.6.cloned.1.call-done.refs_0_), channel_id=1, source_target_pairs={{0,8},{8,0},{16,24},{24,16},{1,9},{9,1},{17,25},{25,17},{2,10},{10... | collective-permute-start | bytes 4325384 | tf_op jit(solution)/shard_map/ppermute | solution.py:29
  437.0 30.8 %collective-permute-start.51 = (bf16[256,2816]{1,0:T(8,128)(2,1)}, bf16[256,2816]{1,0:T(8,128)(2,1)}, u32[]{:S(2)}, u32[]{:S(2)}) collective-permute-start(bf16[256,2816]{1,0:T(8,128)(2,1)} %reduce-scatter.6.cloned.1.call-done.refs_0_), channel_id=1, source_target_pairs={{0,16},{8,24},{16,0},{24,8},{1,17},{9,25},{17,1},{25,9},{2,18},{10... | collective-permute-start | bytes 4325384 | tf_op jit(solution)/shard_map/ppermute | solution.py:29
  467.8 26.3 %collective-permute-start.54 = (bf16[256,2048]{1,0:T(8,128)(2,1)}, bf16[256,2048]{1,0:T(8,128)(2,1)S(1)}, u32[]{:S(2)}, u32[]{:S(2)}) collective-permute-start(bf16[256,2048]{1,0:T(8,128)(2,1)} %get-tuple-element.210), channel_id=1, source_target_pairs={{0,8},{8,0},{16,24},{24,16},{1,9},{9,1},{17,25},{25,17},{2,10},{10... | collective-permute-start | bytes 3145736 | tf_op jit(solution)/shard_map/ppermute | solution.py:29
  468.1 26.3 %collective-permute-start.55 = (bf16[256,2048]{1,0:T(8,128)(2,1)}, bf16[256,2048]{1,0:T(8,128)(2,1)S(1)}, u32[]{:S(2)}, u32[]{:S(2)}) collective-permute-start(bf16[256,2048]{1,0:T(8,128)(2,1)} %get-tuple-element.211), channel_id=1, source_target_pairs={{0,16},{8,24},{16,0},{24,8},{1,17},{9,25},{17,1},{25,9},{2,18},{10... | collective-permute-start | bytes 3145736 | tf_op jit(solution)/shard_map/ppermute | solution.py:29
  480.1 29.6 %collective-permute-start.52 = (bf16[128,2816]{1,0:T(8,128)(2,1)S(1)}, bf16[128,2816]{1,0:T(8,128)(2,1)}, u32[]{:S(2)}, u32[]{:S(2)}) collective-permute-start(bf16[128,2816]{1,0:T(8,128)(2,1)S(1)} %slice.164), channel_id=1, source_target_pairs={{0,16},{8,24},{16,0},{24,8},{1,17},{9,25},{17,1},{25,9},{2,18},{10... | collective-permute-start | bytes 2162696 | tf_op jit(solution)/shard_map/ppermute | solution.py:29
  482.6 27.1 %collective-permute-start.53 = (bf16[128,2816]{1,0:T(8,128)(2,1)}, bf16[128,2816]{1,0:T(8,128)(2,1)}, u32[]{:S(2)}, u32[]{:S(2)}) collective-permute-start(bf16[128,2816]{1,0:T(8,128)(2,1)} %slice.165), channel_id=1, source_target_pairs={{0,8},{8,0},{16,24},{24,16},{1,9},{9,1},{17,25},{25,17},{2,10},{10... | collective-permute-start | bytes 2162696 | tf_op jit(solution)/shard_map/ppermute | solution.py:29
  494.4 27.4 %collective-permute-start.56 = (bf16[256,1152]{1,0:T(8,128)(2,1)}, bf16[256,1152]{1,0:T(8,128)(2,1)S(1)}, u32[]{:S(2)}, u32[]{:S(2)}) collective-permute-start(bf16[256,1152]{1,0:T(8,128)(2,1)} %reduce-scatter.8.cloned.1.call-done.refs_0_), channel_id=1, source_target_pairs={{0,8},{8,0},{16,24},{24,16},{1,9},{9,1},{17,25},{25,17},{2,10},{10... | collective-permute-start | bytes 1769480 | tf_op jit(solution)/shard_map/ppermute | solution.py:29
  496.1 31.6 %collective-permute-start.57 = (bf16[256,1152]{1,0:T(8,128)(2,1)}, bf16[256,1152]{1,0:T(8,128)(2,1)}, u32[]{:S(2)}, u32[]{:S(2)}) collective-permute-start(bf16[256,1152]{1,0:T(8,128)(2,1)} %reduce-scatter.8.cloned.1.call-done.refs_0_), channel_id=1, source_target_pairs={{0,16},{8,24},{16,0},{24,8},{1,17},{9,25},{17,1},{25,9},{2,18},{10... | collective-permute-start | bytes 1769480 | tf_op jit(solution)/shard_map/ppermute | solution.py:29
  497.5 32.0 %collective-permute-start.58 = (bf16[256,1152]{1,0:T(8,128)(2,1)}, bf16[256,1152]{1,0:T(8,128)(2,1)}, u32[]{:S(2)}, u32[]{:S(2)}) collective-permute-start(bf16[256,1152]{1,0:T(8,128)(2,1)} %reduce-scatter.8.cloned.1.call-done.refs_0_), channel_id=1, source_target_pairs={{0,24},{8,16},{16,8},{24,0},{1,25},{9,17},{17,9},{25,1},{2,26},{10... | collective-permute-start | bytes 1769480 | tf_op jit(solution)/shard_map/ppermute | solution.py:29
  (94 other events, 1355.8 us)
Sparse Core Ops, SparseCore 0:
  10.6 54.4 all-gather.3
  67.3 106.8 all-gather.7
  175.8 58.7 all-gather.5
  249.9 61.8 reduce-scatter.3
  316.2 116.4 reduce-scatter.5
  435.6 55.9 reduce-scatter.7

commit v5 on v4

--- a/solution.py
+++ b/solution.py
@@ -277,7 +277,7 @@
         ],
         out_specs=[pl.BlockSpec((size, step), lambda i: (0, i)) for size in sizes],
         out_shape=[jax.ShapeDtypeStruct((size, width), bf16) for size in sizes],
-        compiler_params=pltpu.CompilerParams(vmem_limit_bytes=40 * MIB),
+        compiler_params=pltpu.CompilerParams(vmem_limit_bytes=60 * MIB),
         cost_estimate=pl.CostEstimate(flops=1, bytes_accessed=1, transcendentals=0),
         name="input_grads",
     )(back_query, back_kv, weights)
@@ -997,9 +997,11 @@
         kept, arrived = scatter_pieces(scatter_turn(scatter_start(parts)))
     gu_blocks, gu_far = gather_far(own_gu, gu_near)
     arrived, own_attn = tie(arrived, own_attn)
-    attn_blocks = [own_attn] + [hop(own_attn, r) for r in range(1, count)]
     (grad_tokens,) = norm_back(kept, arrived, mine, back_middle, gain_first, False)
-    gu_far, grad_tokens = tie(gu_far, grad_tokens)
+    attn_late, grad_tokens = tie(own_attn, grad_tokens)
+    attn_blocks = [own_attn] + [
+        hop(own_attn if r in (1, 2) else attn_late, r) for r in range(1, count)
+    ]
 
     grad_down = jnp.zeros((count * piece, width), f32)
     places = [((place ^ r) * piece, block) for r, block in enumerate(down_blocks)]

time: 545 us -> 544 us (level)
    unnamed x133 -> x121, local copies, waits for them, and re-layouts: 27.2 us -> 24.6 us
  transfers between devices with their start and end apart: 65 -> 65, of which waited for: 36 -> 35; matrix products, arithmetic and copies ran while one was open for 24% -> 24% of each run, Pallas kernels for 19% -> 20%
where the time goes in v5:
time: 544 us; the launch traced here: 539 us
  waiting for transfers between devices  175 us (32%)
  Pallas kernels  110 us (20%)
  matrix products  81.5 us (15%)
  starting transfers between devices  63.4 us (12%)
  local copies, waits for them, and re-layouts  57.6 us (11%)
  other arithmetic  24.4 us (4%)
  between operations  15.1 us (3%)
  blocking collectives  12.5 us (2%)
    ppermute x59, waiting for transfers between devices, hop(): return lax.ppermute(value, 'seq', [(i, i ^ bit) for i in range(count)])  175 us
    ppermute x59, starting transfers between devices, hop(): return lax.ppermute(value, 'seq', [(i, i ^ bit) for i in range(count)])  63.1 us
    unnamed x121, local copies, waits for them, and re-layouts  24.6 us
    dot_general x2, matrix products, token_sum(): jnp.einsum('tf,td->fd', left, right, preferred_element_type=f32)  23.2 us
    pallas_call x1, Pallas kernels, attend_back(): pl.pallas_call(functools.partial(attend_back_kernel, count, rows), grid_s...  21 us
    pallas_call x1, Pallas kernels, attend(): pl.pallas_call(functools.partial(attend_kernel, count, rows), grid_spec=p...  17.7 us
    dot_general x1, matrix products, on_device(): gate_up = jnp.dot(normed_mlp, w_gu, preferred_element_type=f32)  17.4 us
    dot_general x1, matrix products, on_device(): jnp.einsum('tf,df->td', back_gu, w_gu, preferred_element_type=f32)  15 us
  transfers between devices with their start and end apart: 65, of which 35 were waited for; matrix products, arithmetic and copies ran while one was open for 24% of the time, Pallas kernels for 20%

profile of v5, /device:TPU:0, one launch (start us, length us, event | category | flops | bytes accessed | tf_op | source)
XLA Modules:
  0.0 539.2 jit_solution(696663451012102817)
XLA Ops:
  15.0 21.9 %collective-permute-done.refs_1_ = bf16[256,2048]{1,0:T(8,128)(2,1)S(1)} collective-permute-done((bf16[256,2048]{1,0:T(8,128)(2,1)}, bf16[256,2048]{1,0:T(8,128)(2,1)S(1)}, u32[]{:S(2)}, u32[]{:S(2)}) %collective-permute-start) | collective-permute-done | bytes 1048608 | tf_op jit(solution)/shard_map/ppermute | solution.py:29
  53.2 12.5 %all_gather.13 = bf16[2,2048]{1,0:T(2,128)(2,1)S(1)} all-gather(bf16[2,256]{1,0:T(2,128)(2,1)S(1)} %pad_maximum_fusion.1), channel_id=1, replica_groups=mesh['seq'=4,'shard'=8] {'shard'}, dimensions={1}, use_global_device_ids=true | all-gather | bytes 9216 | tf_op jit(solution)/shard_map/all_gather | solution.py:874
  66.4 10.1 %project.1 = (bf16[4,256,2048]{2,1,0:T(8,128)(2,1)}, bf16[4,256,512]{2,1,0:T(8,128)(2,1)}, bf16[4,256,128]{2,1,0:T(8,128)(2,1)}, bf16[4,256,128]{2,1,0:T(8,128)(2,1)}) custom-call(bf16[256,2048]{1,0:T(8,128)(2,1)} %bitcast.33, bf16[256,2048]{1,0:T(8,128)(2,1)} %copy-done.31, bf16[256,2048]{1,0:T(8,128)(2,1)} %copy-done.32, ...), custom_call_target="tpu_custom_call" | custom-call | flops 1 | bytes 1 | tf_op jit(solution)/shard_map/project/pallas_call | solution.py:442
  82.5 17.7 %attend.1 = (bf16[4,256,512]{2,1,0:T(8,128)(2,1)S(1)}, bf16[512,1024]{1,0:T(8,128)(2,1)S(1)}, f32[4,4,8,256]{3,2,1,0:T(8,128)S(1)}) custom-call(s32[1]{0:T(128)} %bitcast.place_ref, bf16[4,256,512]{2,1,0:T(8,128)(2,1)S(1)} %copy-done.7, bf16[4,256,128]{2,1,0:T(8,128)(2,1)S(1)} %copy-done.15, bf16[4,256,128]{2,1,0:T(8,128)(2,1)S(1)} %copy-done.16), custom_call_target="tpu_custom_call" | custom-call | flops 1 | bytes 1 | tf_op jit(solution)/shard_map/attend/pallas_call | solution.py:537
  101.3 4.1 collective-permute-done.5
  113.4 10.8 %collective-permute-done.10 = bf16[128,2048]{1,0:T(8,128)(2,1)S(1)} collective-permute-done((bf16[128,2048]{1,0:T(8,128)(2,1)S(1)}, bf16[128,2048]{1,0:T(8,128)(2,1)S(1)}, u32[]{:S(2)}, u32[]{:S(2)}) %collective-permute-start.10) | collective-permute-done | bytes 524320 | tf_op jit(solution)/shard_map/ppermute | solution.py:29
  130.6 4.9 collective-permute-done.7.refs_0_
  136.2 8.8 %collective-permute-done.9.refs_1_ = bf16[128,2048]{1,0:T(8,128)(2,1)} collective-permute-done((bf16[128,2048]{1,0:T(8,128)(2,1)}, bf16[128,2048]{1,0:T(8,128)(2,1)}, u32[]{:S(2)}, u32[]{:S(2)}) %collective-permute-start.9) | collective-permute-done | bytes 524320 | tf_op jit(solution)/shard_map/ppermute | solution.py:29
  145.4 5.1 norm.1
  157.9 7.8 %collective-permute-done.13 = bf16[128,2048]{1,0:T(8,128)(2,1)} collective-permute-done((bf16[128,2048]{1,0:T(8,128)(2,1)}, bf16[128,2048]{1,0:T(8,128)(2,1)}, u32[]{:S(2)}, u32[]{:S(2)}) %collective-permute-start.13) | collective-permute-done | bytes 524320 | tf_op jit(solution)/shard_map/ppermute | solution.py:29
  168.8 8.0 %collective-permute-done.14 = bf16[128,2048]{1,0:T(8,128)(2,1)S(1)} collective-permute-done((bf16[128,2048]{1,0:T(8,128)(2,1)}, bf16[128,2048]{1,0:T(8,128)(2,1)S(1)}, u32[]{:S(2)}, u32[]{:S(2)}) %collective-permute-start.14) | collective-permute-done | bytes 524320 | tf_op jit(solution)/shard_map/ppermute | solution.py:29
  179.3 7.0 %collective-permute-done.17 = bf16[128,2048]{1,0:T(8,128)(2,1)S(1)} collective-permute-done((bf16[128,2048]{1,0:T(8,128)(2,1)}, bf16[128,2048]{1,0:T(8,128)(2,1)S(1)}, u32[]{:S(2)}, u32[]{:S(2)}) %collective-permute-start.17) | collective-permute-done | bytes 524320 | tf_op jit(solution)/shard_map/ppermute | solution.py:29
  191.2 17.4 %fusion.16 = f32[1024,2816]{1,0:T(8,128)S(1)} fusion(bf16[1024,2048]{1,0:T(8,128)(2,1)} %copy-done.50, bf16[2048,2816]{1,0:T(8,128)(2,1)} %all-gather.8.cloned.1.call-done), kind=kOutput, calls=%fused_computation.72 | convolution fusion | flops 11811160064 | bytes 27262976 | tf_op jit(solution)/shard_map/dot_general | solution.py:934
  227.9 8.0 %convolution_convert_fusion.1 = bf16[1408,2048]{1,0:T(8,128)(2,1)} fusion(bf16[1024,1408]{1,0:T(8,128)(2,1)S(1)} %multiply_convert_fusion, bf16[1024,2048]{1,0:T(8,128)(2,1)S(1)} %constant_dynamic-update-slice_fusion.8), kind=kOutput, calls=%fused_computation.1 | convolution fusion | flops 5908463616 | bytes 12845056 | tf_op jit(solution)/shard_map/tf,td->fd/dot_general | solution.py:923
  236.0 8.7 %convolution_convert_fusion.4 = bf16[1024,2048]{1,0:T(8,128)(2,1)S(1)} fusion(bf16[1024,1408]{1,0:T(8,128)(2,1)S(1)} %multiply_convert_fusion, bf16[1408,2048]{1,0:T(8,128)(2,1)} %all-gather.6.cloned.1.call-done), kind=kOutput, calls=%fused_computation.14 | convolution fusion | flops 5907677184 | bytes 12845056 | tf_op jit(solution)/shard_map/dot_general | solution.py:946
  249.8 14.9 %fusion.2 = (bf16[1024,1408]{1,0:T(8,128)(2,1)S(1)}, bf16[1024,1408]{1,0:T(8,128)(2,1)S(1)}) fusion(f32[1024,2816]{1,0:T(8,128)} %copy-done.23, bf16[1024,2048]{1,0:T(8,128)(2,1)} %copy-done.49, bf16[1408,2048]{1,0:T(8,128)(2,1)} %all-gather.6.cloned.1.call-done), kind=kOutput, calls=%fused_computation.6 | convolution fusion | flops 5927206912 | bytes 27262976 | tf_op jit(solution)/shard_map/td,fd->tf/dot_general | solution.py:950
  273.3 15.0 %convolution_convert_fusion.2 = bf16[1024,2048]{1,0:T(8,128)(2,1)S(1)} fusion(bf16[1024,2816]{1,0:T(8,128)(2,1)S(1)} %pad_maximum_fusion, bf16[2048,2816]{1,0:T(8,128)(2,1)} %all-gather.8.cloned.1.call-done), kind=kOutput, calls=%fused_computation.12 | convolution fusion | flops 11813257216 | bytes 21495808 | tf_op jit(solution)/shard_map/tf,df->td/dot_general | solution.py:959
  297.3 15.2 %convolution_convert_fusion = bf16[2048,2816]{1,0:T(8,128)(2,1)} fusion(bf16[1024,2048]{1,0:T(8,128)(2,1)S(1)} %copy-done.51, bf16[1024,2816]{1,0:T(8,128)(2,1)S(1)} %pad_maximum_fusion), kind=kOutput, calls=%fused_computation | convolution fusion | flops 11816927232 | bytes 21495808 | tf_op jit(solution)/shard_map/tf,td->fd/dot_general | solution.py:923
  319.3 8.5 %collective-permute-done.33.refs_5_ = bf16[128,2048]{1,0:T(8,128)(2,1)S(1)} collective-permute-done((bf16[128,2048]{1,0:T(8,128)(2,1)S(1)}, bf16[128,2048]{1,0:T(8,128)(2,1)S(1)}, u32[]{:S(2)}, u32[]{:S(2)}) %collective-permute-start.33) | collective-permute-done | bytes 524320 | tf_op jit(solution)/shard_map/ppermute | solution.py:29
  330.1 6.2 %norm_back.2 = (f32[256,2048]{1,0:T(8,128)}, bf16[128,2048]{1,0:T(8,128)(2,1)}, bf16[128,2048]{1,0:T(8,128)(2,1)}) custom-call(bf16[256,2048]{1,0:T(8,128)(2,1)} %get-tuple-element.154.refs_0_, f32[256,2048]{1,0:T(8,128)} %get-tuple-element.130.refs_1_, bf16[256,2048]{1,0:T(8,128)(2,1)} %bitcast.37, bf16[1,2048]{1,0:T(2,128)(2,1)} %get-tuple-element.257.gain_ref.refs_3_, ...), custom_call_target="tpu_custom_call" | custom-call | flops 1 | bytes 1 | tf_op jit(solution)/shard_map/norm_back/pallas_call | solution.py:388
  340.5 11.0 %collective-permute-done.35.refs_2_ = bf16[128,2048]{1,0:T(8,128)(2,1)S(1)} collective-permute-done((bf16[128,2048]{1,0:T(8,128)(2,1)}, bf16[128,2048]{1,0:T(8,128)(2,1)S(1)}, u32[]{:S(2)}, u32[]{:S(2)}) %collective-permute-start.35) | collective-permute-done | bytes 524320 | tf_op jit(solution)/shard_map/ppermute | solution.py:29
  353.6 9.2 %collective-permute-done.36.refs_3_ = bf16[128,2048]{1,0:T(8,128)(2,1)S(1)} collective-permute-done((bf16[128,2048]{1,0:T(8,128)(2,1)}, bf16[128,2048]{1,0:T(8,128)(2,1)S(1)}, u32[]{:S(2)}, u32[]{:S(2)}) %collective-permute-start.36) | collective-permute-done | bytes 524320 | tf_op jit(solution)/shard_map/ppermute | solution.py:29
  364.0 6.9 %collective-permute-done.39.refs_6_ = bf16[128,2048]{1,0:T(8,128)(2,1)S(1)} collective-permute-done((bf16[128,2048]{1,0:T(8,128)(2,1)S(1)}, bf16[128,2048]{1,0:T(8,128)(2,1)S(1)}, u32[]{:S(2)}, u32[]{:S(2)}) %collective-permute-start.39) | collective-permute-done | bytes 524320 | tf_op jit(solution)/shard_map/ppermute | solution.py:29
  372.5 10.5 %branch.1 = (bf16[4,256,512]{2,1,0:T(8,128)(2,1)}, bf16[512,512]{1,0:T(8,128)(2,1)}, bf16[512,512]{1,0:T(8,128)(2,1)}, bf16[512,512]{1,0:T(8,128)(2,1)}, bf16[512,512]{1,0:T(8,128)(2,1)}) custom-call(s32[1]{0:T(128)} %bitcast.place_ref, bf16[512,2048]{1,0:T(8,128)(2,1)} %copy-done.25, bf16[512,1024]{1,0:T(8,128)(2,1)} %copy-done.17, ...), custom_call_target="tpu_custom_call" | custom-call | flops 1 | bytes 1 | tf_op jit(solution)/shard_map/branch/pallas_call | solution.py:183
  388.9 21.0 %attend_back.1 = (bf16[4,256,512]{2,1,0:T(8,128)(2,1)S(1)}, bf16[4,256,128]{2,1,0:T(8,128)(2,1)S(1)}) custom-call(s32[1]{0:T(128)} %bitcast.place_ref, bf16[4,256,512]{2,1,0:T(8,128)(2,1)S(1)} %copy-done.8, bf16[4,256,128]{2,1,0:T(8,128)(2,1)S(1)} %copy-done.15, bf16[4,256,128]{2,1,0:T(8,128)(2,1)S(1)} %copy-done.16, bf16[4,256,512]{2,1,0:T(8,128)(2,1)S(1)} %copy-done.12, ...), custom_call_target="tpu_custom_call" | custom-call | flops 1 | bytes 1 | tf_op jit(solution)/shard_map/attend_back/pallas_call | solution.py:656
  411.6 6.8 %input_grads.1 = (bf16[256,2048]{1,0:T(8,128)(2,1)}, bf16[256,2048]{1,0:T(8,128)(2,1)}, bf16[256,2048]{1,0:T(8,128)(2,1)}, bf16[128,2048]{1,0:T(8,128)(2,1)}, bf16[128,2048]{1,0:T(8,128)(2,1)}) custom-call(bf16[1024,512]{1,0:T(8,128)(2,1)} %bitcast.26, bf16[1024,128]{1,0:T(8,128)(2,1)} %bitcast.29, bf16[2048,1152]{1,0:T(8,128)(2,1)} %all-gather.4.cloned.1.call-done.refs_6_.w_ref), custom_call_target="tpu_custom_call" | custom-call | flops 1 | bytes 1 | tf_op jit(solution)/shard_map/input_grads/pallas_call | solution.py:270
  426.0 8.2 %attention_grads.1 = bf16[2048,1152]{1,0:T(8,128)(2,1)} custom-call(s32[1]{0:T(128)} %bitcast.place_ref, bf16[1024,2048]{1,0:T(8,128)(2,1)} %bitcast.36, bf16[1024,512]{1,0:T(8,128)(2,1)} %bitcast.27, bf16[1024,128]{1,0:T(8,128)(2,1)} %bitcast.30, bf16[512,512]{1,0:T(8,128)(2,1)} %get-tuple-element.194.refs_0_, bf16[512,512]{1,0:T(8,128)(2,1)} %copy-done.40, ...), custom_call_target="tpu_custom_call" | custom-call | flops 1 | bytes 1 | tf_op jit(solution)/shard_map/attention_grads/pallas_call | solution.py:229
  444.2 21.1 %collective-permute-done.50.refs_1_ = bf16[256,2816]{1,0:T(8,128)(2,1)} collective-permute-done((bf16[256,2816]{1,0:T(8,128)(2,1)}, bf16[256,2816]{1,0:T(8,128)(2,1)}, u32[]{:S(2)}, u32[]{:S(2)}) %collective-permute-start.50) | collective-permute-done | bytes 1441824 | tf_op jit(solution)/shard_map/ppermute | solution.py:29
  483.9 9.7 %collective-permute-done.52.refs_4_ = bf16[256,2048]{1,0:T(8,128)(2,1)S(1)} collective-permute-done((bf16[256,2048]{1,0:T(8,128)(2,1)}, bf16[256,2048]{1,0:T(8,128)(2,1)S(1)}, u32[]{:S(2)}, u32[]{:S(2)}) %collective-permute-start.52) | collective-permute-done | bytes 1048608 | tf_op jit(solution)/shard_map/ppermute | solution.py:29
  497.4 5.2 norm_back.3
  510.0 11.2 %put_columns.1 = (f32[256,5632]{1,0:T(8,128)}, f32[256,5632]{1,0:T(8,128)}, f32[1,256]{1,0:T(1,128)}) custom-call(s32[1]{0:T(128)} %bitcast.place_ref, bf16[256,2816]{1,0:T(8,128)(2,1)} %reduce-scatter.6.cloned.1.call-done.refs_0_, bf16[256,2816]{1,0:T(8,128)(2,1)} %collective-permute-done.50.refs_1_, bf16[256,2816]{1,0:T(8,128)(2,1)} %collective-permute-done.51.refs_2_, ...), custom_call_target="tpu_custom_call" | custom-call | flops 1 | bytes 1 | tf_op jit(solution)/shard_map/put_columns/pallas_call | solution.py:774
  521.2 6.4 %collective-permute-done.55.refs_2_ = bf16[256,1152]{1,0:T(8,128)(2,1)} collective-permute-done((bf16[256,1152]{1,0:T(8,128)(2,1)}, bf16[256,1152]{1,0:T(8,128)(2,1)}, u32[]{:S(2)}, u32[]{:S(2)}) %collective-permute-start.55) | collective-permute-done | bytes 589856 | tf_op jit(solution)/shard_map/ppermute | solution.py:29
  (297 shorter events, 184.3 us)
Async XLA Ops:
  7.2 59.2 %all-gather.4.cloned.1.call-start = ((), (), s32[]{:S(2)}) async-start(), calls=%async_computation.3 | async-start | bytes 5308416 | tf_op jit(solution)/shard_map/all_gather | solution.py:869
  10.5 180.7 %all-gather.8.cloned.1.call-start = ((), (), s32[]{:S(2)}) async-start(), calls=%async_computation.5 | async-start | bytes 12976128 | tf_op jit(solution)/shard_map/all_gather | solution.py:869
  10.5 26.4 %collective-permute-start = (bf16[256,2048]{1,0:T(8,128)(2,1)}, bf16[256,2048]{1,0:T(8,128)(2,1)S(1)}, u32[]{:S(2)}, u32[]{:S(2)}) collective-permute-start(bf16[256,2048]{1,0:T(8,128)(2,1)} %bitcast.31), channel_id=1, source_target_pairs={{0,8},{8,0},{16,24},{24,16},{1,9},{9,1},{17,25},{25,17},{2,10},{10... | collective-permute-start | bytes 3145736 | tf_op jit(solution)/shard_map/ppermute | solution.py:29
  13.5 24.8 %collective-permute-start.1 = (bf16[256,2048]{1,0:T(8,128)(2,1)}, bf16[256,2048]{1,0:T(8,128)(2,1)S(1)}, u32[]{:S(2)}, u32[]{:S(2)}) collective-permute-start(bf16[256,2048]{1,0:T(8,128)(2,1)} %bitcast.32), channel_id=1, source_target_pairs={{0,16},{8,24},{16,0},{24,8},{1,17},{9,25},{17,1},{25,9},{2,18},{10... | collective-permute-start | bytes 3145736 | tf_op jit(solution)/shard_map/ppermute | solution.py:29
  44.9 191.1 %all-gather.6.cloned.1.call-start = ((), (), s32[]{:S(2)}) async-start(), calls=%async_computation.4 | async-start | bytes 6488064 | tf_op jit(solution)/shard_map/all_gather | solution.py:869
  78.9 22.3 %collective-permute-start.4 = (bf16[512,512]{1,0:T(8,128)(2,1)S(1)}, bf16[512,512]{1,0:T(8,128)(2,1)S(1)}, u32[]{:S(2)}, u32[]{:S(2)}) collective-permute-start(bf16[512,512]{1,0:T(8,128)(2,1)S(1)} %get-tuple-element.237), channel_id=1, source_target_pairs={{0,8},{8,0},{16,24},{24,16},{1,9},{9,1},{17,25},{25,17},{2,10},{10... | collective-permute-start | bytes 1572872 | tf_op jit(solution)/shard_map/ppermute | solution.py:29
  80.4 25.0 %collective-permute-start.5 = (bf16[512,512]{1,0:T(8,128)(2,1)S(1)}, bf16[512,512]{1,0:T(8,128)(2,1)S(1)}, u32[]{:S(2)}, u32[]{:S(2)}) collective-permute-start(bf16[512,512]{1,0:T(8,128)(2,1)S(1)} %get-tuple-element.236), channel_id=1, source_target_pairs={{0,16},{8,24},{16,0},{24,8},{1,17},{9,25},{17,1},{25,9},{2,18},{10... | collective-permute-start | bytes 1572872 | tf_op jit(solution)/shard_map/ppermute | solution.py:29
  81.0 24.4 %collective-permute-start.6 = (bf16[512,512]{1,0:T(8,128)(2,1)S(1)}, bf16[512,512]{1,0:T(8,128)(2,1)S(1)}, u32[]{:S(2)}, u32[]{:S(2)}) collective-permute-start(bf16[512,512]{1,0:T(8,128)(2,1)S(1)} %get-tuple-element.235), channel_id=1, source_target_pairs={{0,24},{8,16},{16,8},{24,0},{1,25},{9,17},{17,9},{25,1},{2,26},{10... | collective-permute-start | bytes 1572872 | tf_op jit(solution)/shard_map/ppermute | solution.py:29
  111.3 24.2 %collective-permute-start.7 = (bf16[128,2048]{1,0:T(8,128)(2,1)}, bf16[128,2048]{1,0:T(8,128)(2,1)}, u32[]{:S(2)}, u32[]{:S(2)}) collective-permute-start(bf16[128,2048]{1,0:T(8,128)(2,1)} %get-tuple-element.250), channel_id=1, source_target_pairs={{0,8},{8,0},{16,24},{24,16},{1,9},{9,1},{17,25},{25,17},{2,10},{10... | collective-permute-start | bytes 1572872 | tf_op jit(solution)/shard_map/ppermute | solution.py:29
  112.0 24.2 %collective-permute-start.12 = (bf16[128,2048]{1,0:T(8,128)(2,1)}, bf16[128,2048]{1,0:T(8,128)(2,1)}, u32[]{:S(2)}, u32[]{:S(2)}) collective-permute-start(bf16[128,2048]{1,0:T(8,128)(2,1)} %get-tuple-element.247), channel_id=1, source_target_pairs={{0,16},{8,24},{16,0},{24,8},{1,17},{9,25},{17,1},{25,9},{2,18},{10... | collective-permute-start | bytes 1572872 | tf_op jit(solution)/shard_map/ppermute | solution.py:29
  153.6 218.2 %reduce-scatter.4.cloned.1.call-start = ((), (), s32[]{:S(2)}) async-start(), calls=%async_computation.6 | async-start | bytes 6488064 | tf_op jit(solution)/shard_map/reduce_scatter | solution.py:926
  153.6 23.1 %collective-permute-start.14 = (bf16[128,2048]{1,0:T(8,128)(2,1)}, bf16[128,2048]{1,0:T(8,128)(2,1)S(1)}, u32[]{:S(2)}, u32[]{:S(2)}) collective-permute-start(bf16[128,2048]{1,0:T(8,128)(2,1)} %get-tuple-element.132), channel_id=1, source_target_pairs={{0,8},{8,0},{16,24},{24,16},{1,9},{9,1},{17,25},{25,17},{2,10},{10... | collective-permute-start | bytes 1572872 | tf_op jit(solution)/shard_map/ppermute | solution.py:29
  249.7 184.5 %reduce-scatter.6.cloned.1.call-start = ((), (), s32[]{:S(2)}) async-start(), calls=%async_computation.7 | async-start | bytes 12976128 | tf_op jit(solution)/shard_map/reduce_scatter | solution.py:926
  265.5 24.3 %collective-permute-start.27 = (bf16[128,2048]{1,0:T(8,128)(2,1)}, bf16[128,2048]{1,0:T(8,128)(2,1)S(1)}, u32[]{:S(2)}, u32[]{:S(2)}) collective-permute-start(bf16[128,2048]{1,0:T(8,128)(2,1)} %slice.154), channel_id=1, source_target_pairs={{0,8},{8,0},{16,24},{24,16},{1,9},{9,1},{17,25},{25,17},{2,10},{10... | collective-permute-start | bytes 1572872 | tf_op jit(solution)/shard_map/ppermute | solution.py:29
  266.9 22.9 %collective-permute-start.28 = (bf16[128,2048]{1,0:T(8,128)(2,1)}, bf16[128,2048]{1,0:T(8,128)(2,1)S(1)}, u32[]{:S(2)}, u32[]{:S(2)}) collective-permute-start(bf16[128,2048]{1,0:T(8,128)(2,1)} %slice.155), channel_id=1, source_target_pairs={{0,16},{8,24},{16,0},{24,8},{1,17},{9,25},{17,1},{25,9},{2,18},{10... | collective-permute-start | bytes 1572872 | tf_op jit(solution)/shard_map/ppermute | solution.py:29
  316.1 177.8 %reduce-scatter.8.cloned.1.call-start = ((), (), s32[]{:S(2)}) async-start(), calls=%async_computation.8 | async-start | bytes 5308416 | tf_op jit(solution)/shard_map/reduce_scatter | solution.py:926
  338.2 24.6 %collective-permute-start.36 = (bf16[128,2048]{1,0:T(8,128)(2,1)}, bf16[128,2048]{1,0:T(8,128)(2,1)S(1)}, u32[]{:S(2)}, u32[]{:S(2)}) collective-permute-start(bf16[128,2048]{1,0:T(8,128)(2,1)} %get-tuple-element.166.refs_1_), channel_id=1, source_target_pairs={{0,8},{8,0},{16,24},{24,16},{1,9},{9,1},{17,25},{25,17},{2,10},{10... | collective-permute-start | bytes 1572872 | tf_op jit(solution)/shard_map/ppermute | solution.py:29
  338.8 25.3 %collective-permute-start.37 = (bf16[128,2048]{1,0:T(8,128)(2,1)}, bf16[128,2048]{1,0:T(8,128)(2,1)S(1)}, u32[]{:S(2)}, u32[]{:S(2)}) collective-permute-start(bf16[128,2048]{1,0:T(8,128)(2,1)} %get-tuple-element.165.refs_0_), channel_id=1, source_target_pairs={{0,16},{8,24},{16,0},{24,8},{1,17},{9,25},{17,1},{25,9},{2,18},{10... | collective-permute-start | bytes 1572872 | tf_op jit(solution)/shard_map/ppermute | solution.py:29
  371.7 39.9 %collective-permute-start.44 = (bf16[176,2048]{1,0:T(8,128)(2,1)}, bf16[176,2048]{1,0:T(8,128)(2,1)}, u32[]{:S(2)}, u32[]{:S(2)}) collective-permute-start(bf16[176,2048]{1,0:T(8,128)(2,1)} %reduce-scatter.4.cloned.1.call-done), channel_id=1, source_target_pairs={{0,8},{8,0},{16,24},{24,16},{1,9},{9,1},{17,25},{25,17},{2,10},{10... | collective-permute-start | bytes 2162696 | tf_op jit(solution)/shard_map/ppermute | solution.py:29
  372.1 39.5 %collective-permute-start.45 = (bf16[176,2048]{1,0:T(8,128)(2,1)}, bf16[176,2048]{1,0:T(8,128)(2,1)}, u32[]{:S(2)}, u32[]{:S(2)}) collective-permute-start(bf16[176,2048]{1,0:T(8,128)(2,1)} %reduce-scatter.4.cloned.1.call-done), channel_id=1, source_target_pairs={{0,16},{8,24},{16,0},{24,8},{1,17},{9,25},{17,1},{25,9},{2,18},{10... | collective-permute-start | bytes 2162696 | tf_op jit(solution)/shard_map/ppermute | solution.py:29
  383.0 28.7 %collective-permute-start.41 = (bf16[512,512]{1,0:T(8,128)(2,1)}, bf16[512,512]{1,0:T(8,128)(2,1)S(1)}, u32[]{:S(2)}, u32[]{:S(2)}) collective-permute-start(bf16[512,512]{1,0:T(8,128)(2,1)} %get-tuple-element.177), channel_id=1, source_target_pairs={{0,8},{8,0},{16,24},{24,16},{1,9},{9,1},{17,25},{25,17},{2,10},{10... | collective-permute-start | bytes 1572872 | tf_op jit(solution)/shard_map/ppermute | solution.py:29
  384.4 27.2 %collective-permute-start.42 = (bf16[512,512]{1,0:T(8,128)(2,1)}, bf16[512,512]{1,0:T(8,128)(2,1)}, u32[]{:S(2)}, u32[]{:S(2)}) collective-permute-start(bf16[512,512]{1,0:T(8,128)(2,1)} %get-tuple-element.178), channel_id=1, source_target_pairs={{0,16},{8,24},{16,0},{24,8},{1,17},{9,25},{17,1},{25,9},{2,18},{10... | collective-permute-start | bytes 1572872 | tf_op jit(solution)/shard_map/ppermute | solution.py:29
  386.3 25.3 %collective-permute-start.43 = (bf16[512,512]{1,0:T(8,128)(2,1)}, bf16[512,512]{1,0:T(8,128)(2,1)}, u32[]{:S(2)}, u32[]{:S(2)}) collective-permute-start(bf16[512,512]{1,0:T(8,128)(2,1)} %get-tuple-element.179), channel_id=1, source_target_pairs={{0,24},{8,16},{16,8},{24,0},{1,25},{9,17},{17,9},{25,1},{2,26},{10... | collective-permute-start | bytes 1572872 | tf_op jit(solution)/shard_map/ppermute | solution.py:29
  434.3 30.9 %collective-permute-start.50 = (bf16[256,2816]{1,0:T(8,128)(2,1)}, bf16[256,2816]{1,0:T(8,128)(2,1)}, u32[]{:S(2)}, u32[]{:S(2)}) collective-permute-start(bf16[256,2816]{1,0:T(8,128)(2,1)} %reduce-scatter.6.cloned.1.call-done.refs_0_), channel_id=1, source_target_pairs={{0,8},{8,0},{16,24},{24,16},{1,9},{9,1},{17,25},{25,17},{2,10},{10... | collective-permute-start | bytes 4325384 | tf_op jit(solution)/shard_map/ppermute | solution.py:29
  435.9 31.4 %collective-permute-start.51 = (bf16[256,2816]{1,0:T(8,128)(2,1)}, bf16[256,2816]{1,0:T(8,128)(2,1)}, u32[]{:S(2)}, u32[]{:S(2)}) collective-permute-start(bf16[256,2816]{1,0:T(8,128)(2,1)} %reduce-scatter.6.cloned.1.call-done.refs_0_), channel_id=1, source_target_pairs={{0,16},{8,24},{16,0},{24,8},{1,17},{9,25},{17,1},{25,9},{2,18},{10... | collective-permute-start | bytes 4325384 | tf_op jit(solution)/shard_map/ppermute | solution.py:29
  467.3 26.3 %collective-permute-start.52 = (bf16[256,2048]{1,0:T(8,128)(2,1)}, bf16[256,2048]{1,0:T(8,128)(2,1)S(1)}, u32[]{:S(2)}, u32[]{:S(2)}) collective-permute-start(bf16[256,2048]{1,0:T(8,128)(2,1)} %get-tuple-element.205), channel_id=1, source_target_pairs={{0,8},{8,0},{16,24},{24,16},{1,9},{9,1},{17,25},{25,17},{2,10},{10... | collective-permute-start | bytes 3145736 | tf_op jit(solution)/shard_map/ppermute | solution.py:29
  467.6 26.3 %collective-permute-start.53 = (bf16[256,2048]{1,0:T(8,128)(2,1)}, bf16[256,2048]{1,0:T(8,128)(2,1)S(1)}, u32[]{:S(2)}, u32[]{:S(2)}) collective-permute-start(bf16[256,2048]{1,0:T(8,128)(2,1)} %get-tuple-element.206), channel_id=1, source_target_pairs={{0,16},{8,24},{16,0},{24,8},{1,17},{9,25},{17,1},{25,9},{2,18},{10... | collective-permute-start | bytes 3145736 | tf_op jit(solution)/shard_map/ppermute | solution.py:29
  479.8 30.2 %collective-permute-start.57 = (bf16[128,2816]{1,0:T(8,128)(2,1)S(1)}, bf16[128,2816]{1,0:T(8,128)(2,1)}, u32[]{:S(2)}, u32[]{:S(2)}) collective-permute-start(bf16[128,2816]{1,0:T(8,128)(2,1)S(1)} %slice.164), channel_id=1, source_target_pairs={{0,16},{8,24},{16,0},{24,8},{1,17},{9,25},{17,1},{25,9},{2,18},{10... | collective-permute-start | bytes 2162696 | tf_op jit(solution)/shard_map/ppermute | solution.py:29
  482.1 27.9 %collective-permute-start.58 = (bf16[128,2816]{1,0:T(8,128)(2,1)}, bf16[128,2816]{1,0:T(8,128)(2,1)}, u32[]{:S(2)}, u32[]{:S(2)}) collective-permute-start(bf16[128,2816]{1,0:T(8,128)(2,1)} %slice.165), channel_id=1, source_target_pairs={{0,8},{8,0},{16,24},{24,16},{1,9},{9,1},{17,25},{25,17},{2,10},{10... | collective-permute-start | bytes 2162696 | tf_op jit(solution)/shard_map/ppermute | solution.py:29
  493.9 27.3 %collective-permute-start.54 = (bf16[256,1152]{1,0:T(8,128)(2,1)}, bf16[256,1152]{1,0:T(8,128)(2,1)}, u32[]{:S(2)}, u32[]{:S(2)}) collective-permute-start(bf16[256,1152]{1,0:T(8,128)(2,1)} %reduce-scatter.8.cloned.1.call-done.refs_0_), channel_id=1, source_target_pairs={{0,8},{8,0},{16,24},{24,16},{1,9},{9,1},{17,25},{25,17},{2,10},{10... | collective-permute-start | bytes 1769480 | tf_op jit(solution)/shard_map/ppermute | solution.py:29
  495.6 32.0 %collective-permute-start.55 = (bf16[256,1152]{1,0:T(8,128)(2,1)}, bf16[256,1152]{1,0:T(8,128)(2,1)}, u32[]{:S(2)}, u32[]{:S(2)}) collective-permute-start(bf16[256,1152]{1,0:T(8,128)(2,1)} %reduce-scatter.8.cloned.1.call-done.refs_0_), channel_id=1, source_target_pairs={{0,16},{8,24},{16,0},{24,8},{1,17},{9,25},{17,1},{25,9},{2,18},{10... | collective-permute-start | bytes 1769480 | tf_op jit(solution)/shard_map/ppermute | solution.py:29
  502.7 25.9 %collective-permute-start.56 = (bf16[256,1152]{1,0:T(8,128)(2,1)S(1)}, bf16[256,1152]{1,0:T(8,128)(2,1)S(1)}, u32[]{:S(2)}, u32[]{:S(2)}) collective-permute-start(bf16[256,1152]{1,0:T(8,128)(2,1)S(1)} %copy-done.18), channel_id=1, source_target_pairs={{0,24},{8,16},{16,8},{24,0},{1,25},{9,17},{17,9},{25,1},{2,26},{10... | collective-permute-start | bytes 1769480 | tf_op jit(solution)/shard_map/ppermute | solution.py:29
  (88 other events, 1262.7 us)
Sparse Core Ops, SparseCore 0:
  10.6 54.4 all-gather.3
  67.3 106.8 all-gather.7
  175.8 58.7 all-gather.5
  249.9 61.8 reduce-scatter.3
  316.2 116.3 reduce-scatter.5
  435.4 54.4 reduce-scatter.7
